TPU v7x, 128 devices: a whole 4x4x4 slice. The times are simulated.
128 devices in a mesh: tile: 32 (over z_hi, x, y), face: 4 (over z_lo, core).
Axes of the slice: x: 4, y: 4, z: 4 (z_hi: 2, z_lo: 2; z = z_hi * 2 + z_lo), core: 2. Of those that a mesh axis runs over, the one named last changes fastest.
Arguments:
- adjoint_seed: float32 [64, 4, 512, 1024], P(None, None, 'tile', 'face'), may hold values from -6 to 6
- face_flow: float32 [2, 64, 512, 1024], P(None, None, 'tile', 'face'), may hold values from -0.4 to 0.4
- vert_diff: float32 [64, 512, 1024], P(None, 'tile', 'face'), may hold values from 0.1 to 10
- wet_mask: int32 [64, 512, 1024], P(None, 'tile', 'face'), may hold values 0 or 1
- smooth_weights: float32 [2, 512, 1024], P(None, ('tile', 'face')), may hold values from 0.02 to 0.24
Outputs:
- adjoint: float32 [64, 4, 512, 1024], P(None, None, 'tile', 'face')
- controls: float32 [132, 512, 1024], P(None, ('tile', 'face'))
All inputs are finite; a program needn't handle non-finite values. No bound on the sum of `wet_mask` on one device may be relied on, other than what follows from the above.
Results may differ from a plain program's by a relative error of at most 0.00011.
Values sent between devices are 32-bit elements; how exact they have to be, the bound alone decides.
No kernel may reach another device: no remote copies, remote signals or barrier semaphores. Data moves between devices by JAX's collectives and lax.ppermute only.
A program may use at most 128 MiB of HBM per device.

v0:
```python
import functools

import jax
import jax.numpy as jnp
from jax import lax
from jax.experimental import pallas as pl
from jax.experimental.pallas import tpu as pltpu
from jax.sharding import PartitionSpec as P

F32 = jnp.float32
LEV = 64
ROWS = 16
LANES = 128
FLAT = LEV * ROWS
WET, UE, VN, VD = 4, 5, 6, 7
KAPPA = 0.15
MIB = 2**20

CHUNKS = ((0, 16), (16, 40), (40, 64))


def iota(shape, dim):
    return lax.broadcasted_iota(jnp.int32, shape, dim)


def rows_of(level):
    return pl.ds(pl.multiple_of(level * ROWS, ROWS), ROWS)


def east_of(tiles):
    last = iota(tiles[0].shape, 1) == LANES - 1
    turned = [pltpu.roll(t, LANES - 1, 1) for t in tiles]
    return [jnp.where(last, turned[(i + 1) % 3], turned[i]) for i in range(3)]


def west_of(tiles):
    first = iota(tiles[0].shape, 1) == 0
    turned = [pltpu.roll(t, 1, 1) for t in tiles]
    return [jnp.where(first, turned[(i + 2) % 3], turned[i]) for i in range(3)]


def call(kernel, outs, scratch=(), limit=8, alias=None, name=None, ins=None):
    def run(*args):
        specs = [pl.BlockSpec(memory_space=pltpu.SMEM)]
        for i in range(1, len(args)):
            space = pltpu.VMEM if ins is None else ins[i]
            specs.append(pl.BlockSpec(memory_space=space))
        return pl.pallas_call(
            kernel,
            out_shape=[jax.ShapeDtypeStruct(s, F32) for s, _ in outs],
            in_specs=specs,
            out_specs=[pl.BlockSpec(memory_space=m) for _, m in outs],
            scratch_shapes=list(scratch),
            input_output_aliases=alias or {},
            compiler_params=pltpu.CompilerParams(vmem_limit_bytes=limit * MIB),
            name=name,
        )(*args)

    return run


VM = pltpu.VMEM


def first_solve(ids, seed, flow, vd, wet, fld, pxa, pxb, ratio, pw, pe):
    lane = iota((ROWS, LANES), 1)
    zero = jnp.zeros((ROWS, LANES), F32)

    def block(b):
        return (lane >= 8 * b) & (lane < 8 * b + 8)

    def pack(b, tiles, west, east):
        sw, se = (8 * b) % LANES, (8 * b + 8) % LANES
        w = pltpu.roll(tiles[0], sw, 1) if sw else tiles[0]
        e = pltpu.roll(tiles[1], se, 1) if se else tiles[1]
        return jnp.where(block(b), w, west), jnp.where(block(b), e, east)

    carry = (
        [zero] * 2,
        [zero] * 2,
        [[zero] * 2 for _ in range(4)],
    )
    for half in range(2):

        def down(i, carry, half=half):
            low, rat, val = carry
            level = half * 32 + i
            at = rows_of(level)
            after = jnp.minimum(level + 1, LEV - 1)
            inside = jnp.where(level < LEV - 1, 1.0, 0.0).astype(F32)
            west = east = zero
            statics = [[], [], [], []]
            nlow, nrat, nval = [], [], [[], [], [], []]
            for t in range(2):
                cols = pl.ds(t * LANES, LANES)
                w = wet[level, :, cols].astype(F32)
                wn = wet[after, :, cols].astype(F32) * inside
                d = vd[level, :, cols]
                statics[0].append(w)
                statics[1].append(flow[0, level, :, cols])
                statics[2].append(flow[1, level, :, cols])
                statics[3].append(d)
                up = d * w * wn
                inv = 1.0 / (1.0 + low[t] + up - low[t] * rat[t])
                r = up * inv
                ratio[t, at, :] = r
                nlow.append(up)
                nrat.append(r)
                for v in range(4):
                    x = (seed[level, v, :, cols] * w + low[t] * val[v][t]) * inv
                    fld[v, t, at, :] = x
                    nval[v].append(x)
            for f in range(4):
                for t in range(2):
                    fld[4 + f, t, at, :] = statics[f][t]
                west, east = pack(8 * half + 4 + f, statics[f], west, east)
            if half == 0:
                pw[i] = west
                pe[i] = east
            else:
                pw[i] = pw[i] + west
                pe[i] = pe[i] + east
            return nlow, nrat, nval

        carry = lax.fori_loop(0, 32, down, carry)

    odd = lax.rem(ids[0], 2) == 1
    follow = [[zero] * 2 for _ in range(4)]
    for half in (1, 0):

        def up(n, follow, half=half):
            i = 31 - n
            at = rows_of(half * 32 + i)
            west = east = zero
            out = []
            r = [ratio[t, at, :] for t in range(2)]
            for v in range(4):
                y = [fld[v, t, at, :] + r[t] * follow[v][t] for t in range(2)]
                for t in range(2):
                    fld[v, t, at, :] = y[t]
                west, east = pack(8 * half + v, y, west, east)
                out.append(y)
            west = pw[i] + west
            east = pe[i] + east
            if half == 1:
                pw[i] = west
                pe[i] = east
            else:
                pxa[i] = jnp.where(odd, west, east)
                pxb[i] = jnp.where(odd, east, west)
            return out

        follow = lax.fori_loop(0, 32, up, follow)


ROWS_TS = 3 * 2 * LEV + 3 * 8
ROWS_UV = 2 * 2 * LEV + 2 * 8


def edge_pack(tiles8):
    lane = iota((8, LANES), 1)
    packed = jnp.zeros((8, LANES), F32)
    for g, t in enumerate(tiles8):
        turned = pltpu.roll(t, (16 * g + 8) % LANES, 1)
        packed = jnp.where((lane >= 16 * g) & (lane < 16 * g + 16), turned, packed)
    return packed


def edge_unpack(packed, g):
    return pltpu.roll(packed, (-(16 * g + 8)) % LANES, 1)


def put_edges(todd, pick, fields, oa, ob):
    for f in range(fields):
        for t in range(2):
            for g in range(8):
                n, s = pick(f, t, g)
                at = pl.ds((f * 2 + t) * LEV + 8 * g, 8)
                oa[at, :] = jnp.where(todd, s, n)
                ob[at, :] = jnp.where(todd, n, s)
        outer = [pick(f, 2, g) for g in range(8)]
        n = edge_pack([o[0] for o in outer])
        s = edge_pack([o[1] for o in outer])
        at = pl.ds(fields * 2 * LEV + 8 * f, 8)
        oa[at, :] = jnp.where(todd, s, n)
        ob[at, :] = jnp.where(todd, n, s)


def edge_rows(ref, g):
    north = ref[pl.ds(g * 8 * ROWS + ROWS - 1, 8, stride=ROWS), :]
    south = ref[pl.ds(g * 8 * ROWS, 8, stride=ROWS), :]
    return north, south


def outer_columns(ids, xa, xb, fld, w0, w1, w2, w3, fe, ya, yb, za, zb, wloc, pieces):
    face, tile = ids[0], ids[1]
    odd = lax.rem(face, 2) == 1
    todd = lax.rem(tile, 2) == 1
    lane = iota((ROWS, LANES), 1)
    on_east = (lane < 8) & (face < 3)
    on_west = (lane >= 120) & (face > 0)

    def unpack(i, carry):
        a, b = xa[i], xb[i]
        from_west = jnp.where(odd, a, b)
        from_east = jnp.where(odd, b, a)
        for half in range(2):
            at = rows_of(half * 32 + i)
            for f in range(8):
                k = 8 * half + f
                w = pltpu.roll(from_west, (120 - 8 * k) % LANES, 1)
                e = pltpu.roll(from_east, (-8 * k) % LANES, 1)
                fe[f, at, :] = jnp.where(on_east, e, jnp.where(on_west, w, 0.0))
        return carry

    lax.fori_loop(0, 32, unpack, 0)

    def source(f, t):
        return fe.at[f] if t == 2 else fld.at[f, t]

    def pick(f, t, g):
        if f < 2:
            return edge_rows(source(f, t), g)
        wn, ws = edge_rows(source(WET, t), g)
        vn, _ = edge_rows(source(VN, t), g)
        return wn * (KAPPA - 0.5 * vn), ws

    put_edges(todd, pick, 3, ya, yb)
    put_edges(todd, lambda f, t, g: edge_rows(source(2 + f, t), g), 2, za, zb)

    for k, w in enumerate((w0, w1, w2, w3)):
        pieces[k] = w[...]
    lane4 = iota((4, LANES), 1)
    for d in range(4):
        slot = jnp.bitwise_xor(face, d)
        for c in range(2):
            for t in range(3):
                at = pl.ds(4 * d, 4)
                if t < 2:
                    first = pl.multiple_of((2 * face + t) * LANES, LANES)
                    wloc[c, t, at, :] = pieces[slot, c, :, pl.ds(first, LANES)]
                    continue
                first = pl.multiple_of(jnp.minimum(2 * face + 2, 7) * LANES, LANES)
                e = pieces[slot, c, :, pl.ds(first, LANES)]
                first = pl.multiple_of(jnp.maximum(2 * face - 1, 0) * LANES, LANES)
                w = pieces[slot, c, :, pl.ds(first, LANES)]
                w = jnp.where((lane4 >= 120) & (face > 0), w, 0.0)
                wloc[c, t, at, :] = jnp.where((lane4 < 8) & (face < 3), e, w)
    for c in range(2):
        for t in range(3):
            n = wloc[c, t, 8:16, :]
            s = wloc[c, t, 0:8, :]
            at = pl.ds(ROWS_TS + 8 * (3 * c + t), 8)
            ya[at, :] = jnp.where(todd, s, n)
            yb[at, :] = jnp.where(todd, n, s)


def coefficients(ids, fld, fe, cf):
    row = iota((ROWS, LANES), 0)
    zero = jnp.zeros((ROWS, LANES), F32)

    def body(level, carry):
        low, rat = carry
        at = rows_of(level)
        after = rows_of(jnp.minimum(level + 1, LEV - 1))
        inside = jnp.where(level < LEV - 1, 1.0, 0.0).astype(F32)

        def get(f, where):
            return [fld[f, 0, where, :], fld[f, 1, where, :], fe[f, where, :]]

        wet, ue, vn, vd = (get(f, at) for f in (WET, UE, VN, VD))
        nxt = get(WET, after)
        wet_e = east_of(wet)
        qw_w = west_of([w * (KAPPA - 0.5 * u) for w, u in zip(wet, ue)])
        nlow, nrat = [], []
        for t in range(3):
            w = wet[t]
            ce = w * (KAPPA + 0.5 * ue[t]) * wet_e[t]
            cw = w * qw_w[t]
            wn = jnp.where(row == ROWS - 1, 1.0, pltpu.roll(w, ROWS - 1, 0))
            qs = jnp.where(row == 0, 1.0, pltpu.roll(w * (KAPPA - 0.5 * vn[t]), 1, 0))
            up = vd[t] * w * nxt[t] * inside
            inv = 1.0 / (1.0 + low[t] + up - low[t] * rat[t])
            r = up * inv
            cf[0, t, at, :] = ce
            cf[1, t, at, :] = cw
            cf[2, t, at, :] = w * (KAPPA + 0.5 * vn[t]) * wn
            cf[3, t, at, :] = w * qs
            cf[4, t, at, :] = w - ce - cw
            cf[5, t, at, :] = low[t]
            cf[6, t, at, :] = inv
            cf[7, t, at, :] = r
            nlow.append(up)
            nrat.append(r)
        return nlow, nrat

    lax.fori_loop(0, LEV, body, ([zero] * 3, [zero] * 3))


def take_edges(ids, ya, yb, hn, hs, fields, groups=(0, 8)):
    todd = lax.rem(ids[1], 2) == 1
    for f in range(fields):
        outer = pl.ds(fields * 2 * LEV + 8 * f, 8)
        oa, ob = ya[outer, :], yb[outer, :]
        on, os = jnp.where(todd, ob, oa), jnp.where(todd, oa, ob)
        for g in range(*groups):
            at = pl.ds(8 * g, 8)
            for t in range(2):
                src = pl.ds((f * 2 + t) * LEV + 8 * g, 8)
                a, b = ya[src, :], yb[src, :]
                hn[f, t, at, :] = jnp.where(todd, b, a)
                hs[f, t, at, :] = jnp.where(todd, a, b)
            hn[f, 2, at, :] = edge_unpack(on, g)
            hs[f, 2, at, :] = edge_unpack(os, g)


def stencil(y, coef, north_row, south_row, row):
    e, w = east_of(y), west_of(y)
    out = []
    for t in range(3):
        n = jnp.where(row == ROWS - 1, north_row[t], pltpu.roll(y[t], ROWS - 1, 0))
        s = jnp.where(row == 0, south_row[t], pltpu.roll(y[t], 1, 0))
        ce, cw, cn, cs, cc = coef[t]
        out.append(cc * y[t] + ce * e[t] + cw * w[t] + cn * n + cs * s)
    return out


def step(first, v0, ids, fld, fe, cfi, ya, yb, *refs):
    if first:
        cf, sol, oa, ob, fo, hn, hs = refs
    else:
        sol, oa, ob, fo, hn, hs = refs
        cf = cfi
    row = iota((ROWS, LANES), 0)
    zero = jnp.zeros((ROWS, LANES), F32)
    take_edges(ids, ya, yb, hn, hs, 3 if first else 2)

    def get(v, at):
        return [fld[v0 + v, 0, at, :], fld[v0 + v, 1, at, :], fe[v0 + v, at, :]]

    north_in = jnp.where(ids[1] < 31, 1.0, 0.0).astype(F32)
    south_in = jnp.where(ids[1] > 0, 1.0, 0.0).astype(F32)

    def down(level, prev):
        at = rows_of(level)
        one = pl.ds(level, 1)
        coef = []
        for t in range(3):
            ce, cw, cn, cs, cc = (cfi[k, t, at, :] for k in range(5))
            if first:
                cn = jnp.where(row == ROWS - 1, cn * (hn[2, t, one, :] * north_in), cn)
                cs = jnp.where(row == 0, cs * (hs[2, t, one, :] * south_in), cs)
                cc = cc - cn - cs
                cf[0, t, at, :] = ce
                cf[1, t, at, :] = cw
                cf[2, t, at, :] = cn
                cf[3, t, at, :] = cs
                cf[4, t, at, :] = cc
            coef.append((ce, cw, cn, cs, cc))
        out = []
        for v in range(2):
            y = get(v, at)
            n = [hn[v, t, one, :] for t in range(3)]
            s = [hs[v, t, one, :] for t in range(3)]
            adj = stencil(y, coef, n, s, row)
            new = []
            for t in range(3):
                x = (adj[t] + cfi[5, t, at, :] * prev[v][t]) * cfi[6, t, at, :]
                sol[v, t, at, :] = x
                new.append(x)
            out.append(new)
        return out

    lax.fori_loop(0, LEV, down, [[zero] * 3 for _ in range(2)])

    def up(n, follow):
        at = rows_of(LEV - 1 - n)
        out = [[], []]
        for t in range(3):
            r = cfi[7, t, at, :]
            for v in range(2):
                y = sol[v, t, at, :] + r * follow[v][t]
                sol[v, t, at, :] = y
                out[v].append(y)
        return out

    top = lax.fori_loop(0, LEV, up, [[zero] * 3 for _ in range(2)])
    for v in range(2):
        y = get(v, pl.ds(0, ROWS))
        for t in range(3):
            fo[v, t] = y[t] + top[v][t]
    todd = lax.rem(ids[1], 2) == 1
    put_edges(todd, lambda f, t, g: edge_rows(sol.at[f, t], g), 2, oa, ob)


def last_stencil(v0, l0, nl, extra, grads, *refs):
    ids, sol, cf, ya, yb = refs[:5]
    refs = refs[5:]
    fos = refs[:extra]
    refs = refs[extra:]
    if l0 or v0:
        refs = refs[1:]
    if grads:
        adj_out, g, ga, gb, hn, hs, en, es, buf, sem = refs
    else:
        adj_out, hn, hs, buf, sem = refs
    row = iota((ROWS, LANES), 0)
    low_half = iota((8, LANES), 0) < 4
    todd = lax.rem(ids[1], 2) == 1
    take_edges(ids, ya, yb, hn, hs, 2, (l0 // 8, (l0 + nl) // 8))

    def edges(u, ts, ss):
        for t in range(3):
            a, b = ts[t], ss[t]
            n = jnp.where(low_half, pltpu.roll(a[8:16], 4, 0), b[8:16])
            s = jnp.where(low_half, a[0:8], pltpu.roll(b[0:8], 4, 0))
            if t < 2:
                ga[2 * u + t] = jnp.where(todd, s, n)
                gb[2 * u + t] = jnp.where(todd, n, s)
            else:
                en[u] = n
                es[u] = s

    def body(u, carry):
        level = l0 + u
        at = rows_of(level)
        one = pl.ds(level, 1)
        coef = [tuple(cf[k, t, at, :] for k in range(5)) for t in range(3)]
        both = []
        for v in range(2):
            y = [sol[v, t, at, :] for t in range(3)]
            n = [hn[v, t, one, :] for t in range(3)]
            s = [hs[v, t, one, :] for t in range(3)]
            x = stencil(y, coef, n, s, row)
            buf[u, v, :, 0:LANES] = x[0]
            buf[u, v, :, LANES : 2 * LANES] = x[1]
            if grads:
                for t in range(3):
                    g[u, v, t] = x[t]
            both.append(x)
        if grads:
            edges(u, *both)
        return carry

    lax.fori_loop(0, nl, body, 0)
    copy = pltpu.make_async_copy(buf, adj_out.at[pl.ds(l0, nl), pl.ds(v0, 2)], sem)
    copy.start()
    if grads:
        for i, fo in enumerate(fos):
            pair = [[fo[v, t] for t in range(3)] for v in range(2)]
            for v in range(2):
                for t in range(3):
                    g[nl + i, v, t] = pair[v][t]
            edges(nl + i, *pair)
        units = nl + extra
        per = -(-units // 8)
        lane = iota((8, LANES), 1)
        for i in range(per):
            pn = ps = jnp.zeros((8, LANES), F32)
            for j in range(8):
                u = j * per + i
                if u < units:
                    mine = (lane >= 16 * j) & (lane < 16 * j + 16)
                    pn = jnp.where(mine, pltpu.roll(en[u], (16 * j + 8) % LANES, 1), pn)
                    ps = jnp.where(mine, pltpu.roll(es[u], (16 * j + 8) % LANES, 1), ps)
            ga[2 * units + i] = jnp.where(todd, ps, pn)
            gb[2 * units + i] = jnp.where(todd, pn, ps)
    copy.wait()


def smooth(units, ids, g, ga, gb, wloc, ya, yb, z0, z1, z2, z3, w5, hn, hs):
    zs = (z0, z1, z2, z3)
    face, tile = ids[0], ids[1]
    todd = lax.rem(tile, 2) == 1
    has_n, has_s = tile < 31, tile > 0
    sub = iota((8, LANES), 0)
    lane = iota((8, LANES), 1)
    low_half = sub < 4

    def stack3(lo, m0, m1, hi):
        r0, r1 = pltpu.roll(m0, 4, 0), pltpu.roll(m1, 4, 0)
        return [
            jnp.where(low_half, lo, r0),
            jnp.where(low_half, r0, r1),
            jnp.where(low_half, r1, hi),
        ]

    def north_of(k3):
        turned = [pltpu.roll(x, 7, 0) for x in k3]
        return [
            jnp.where(sub == 7, turned[1], turned[0]),
            jnp.where(sub == 7, turned[2], turned[1]),
            turned[2],
        ]

    def south_of(k3, below=None):
        turned = [pltpu.roll(x, 1, 0) for x in k3]
        return [
            turned[0] if below is None else jnp.where(sub == 0, below, turned[0]),
            jnp.where(sub == 0, turned[0], turned[1]),
            jnp.where(sub == 0, turned[1], turned[2]),
        ]

    we, wn, below = [], [], []
    for c, dest in ((0, we), (1, wn)):
        for t in range(3):
            at = pl.ds(ROWS_TS + 8 * (3 * c + t), 8)
            a, b = ya[at, :], yb[at, :]
            hi = jnp.where(has_n, jnp.where(todd, b, a), 0.0)
            lo = jnp.where(has_s, jnp.where(todd, a, b), 0.0)
            if c == 1:
                below.append(pltpu.roll(lo, 5, 0))
            dest.append(
                stack3(pltpu.roll(lo, 4, 0), wloc[c, t, 0:8, :], wloc[c, t, 8:16, :], pltpu.roll(hi, 4, 0))
            )
    for k in range(3):
        cw3 = west_of([we[t][k] for t in range(3)])
        for t in range(3):
            ok = jnp.ones((8, LANES), F32)
            if k == 0:
                ok = jnp.where(low_half & (tile == 0), 0.0, ok)
            if k == 2:
                ok = jnp.where((~low_half) & (tile == 31), 0.0, ok)
            if t == 2:
                inside = ((lane < 64) & (face < 3)) | ((lane >= 64) & (face > 0))
                ok = jnp.where(inside, ok, 0.0)
            ce = we[t][k] * ok
            cw = cw3[t] * ok
            cn = wn[t][k] * ok
            cs = south_of(wn[t], below[t])[k] * ok
            w5[0, t, k] = ce
            w5[1, t, k] = cw
            w5[2, t, k] = cn
            w5[3, t, k] = cs
            w5[4, t, k] = 1.0 - ce - cw - cn - cs

    per = -(-units // 8)
    for u in range(units):
        j, i = divmod(u, per)
        a, b = ga[2 * units + i], gb[2 * units + i]
        n = edge_unpack(jnp.where(todd, b, a), j)
        s = edge_unpack(jnp.where(todd, a, b), j)
        hn[u] = jnp.where(has_n, n, 0.0)
        hs[u] = jnp.where(has_s, s, 0.0)

    bit0 = lax.rem(face, 2) == 1
    bit1 = face >= 2

    def body(u, carry):
        hi, lo = [], []
        for t in range(2):
            a, b = ga[2 * u + t], gb[2 * u + t]
            hi.append(jnp.where(has_n, jnp.where(todd, b, a), 0.0))
            lo.append(jnp.where(has_s, jnp.where(todd, a, b), 0.0))
        hi.append(hn[u])
        lo.append(hs[u])
        for v in range(2):
            x = []
            for t in range(3):
                m = g[u, v, t]
                top = pltpu.roll(hi[t], 4, 0) if v == 0 else hi[t]
                bottom = lo[t] if v == 0 else pltpu.roll(lo[t], 4, 0)
                x.append(stack3(bottom, m[0:8], m[8:16], top))
            for _ in range(4):
                ns = [north_of(x[t]) for t in range(3)]
                ss = [south_of(x[t]) for t in range(3)]
                new = [[], [], []]
                for k in range(3):
                    at_k = [x[t][k] for t in range(3)]
                    e, w = east_of(at_k), west_of(at_k)
                    for t in range(3):
                        new[t].append(
                            w5[4, t, k] * x[t][k]
                            + w5[0, t, k] * e[t]
                            + w5[1, t, k] * w[t]
                            + w5[2, t, k] * ns[t][k]
                            + w5[3, t, k] * ss[t][k]
                        )
                x = new
            for t in range(2):
                p = [pltpu.roll(x[t][0], 4, 0), x[t][1], pltpu.roll(x[t][1], 4, 0), x[t][2]]
                p = [jnp.where(bit0, p[d ^ 1], p[d]) for d in range(4)]
                p = [jnp.where(bit1, p[d ^ 2], p[d]) for d in range(4)]
                for k in range(4):
                    zs[k][2 * u + v, :, t * LANES : (t + 1) * LANES] = p[k][0:4]
        return carry

    lax.fori_loop(0, units, body, 0)


def gather_rows(sizes, ids, *refs):
    face = ids[0]
    n = len(sizes)
    out, sem = refs[4 * n], refs[4 * n + 1]
    copies = []
    first = 0
    for c, size in enumerate(sizes):
        for k in range(4):
            cols = pl.multiple_of(jnp.bitwise_xor(face, k) * 256, 256)
            copies.append(
                pltpu.make_async_copy(
                    refs[4 * c + k],
                    out.at[pl.ds(first, size), :, pl.ds(cols, 256)],
                    sem.at[c, k],
                )
            )
        first += size
    for copy in copies:
        copy.start()
    for copy in copies:
        copy.wait()


def on_device(adjoint_seed, face_flow, vert_diff, wet_mask, smooth_weights):
    ids = jnp.stack([lax.axis_index("face"), lax.axis_index("tile")]).astype(jnp.int32)
    tiles = lax.axis_size("tile")
    pair_a = [(i, i ^ 1) for i in range(tiles)]
    pair_b = [(0, 0), (tiles - 1, tiles - 1)]
    for i in range(1, tiles - 1, 2):
        pair_b += [(i, i + 1), (i + 1, i)]
    side_a = [(0, 1), (1, 0), (2, 3), (3, 2)]
    side_b = [(0, 0), (1, 2), (2, 1), (3, 3)]

    def across(a, b):
        return lax.ppermute(a, "tile", pair_a), lax.ppermute(b, "tile", pair_b)

    def to_face(x, k):
        return lax.ppermute(x, "face", [(i, i ^ k) for i in range(4)])

    weights = [smooth_weights] + [to_face(smooth_weights, k) for k in (1, 2, 3)]
    edge = (ROWS, LANES)
    fld, pxa, pxb = call(
        first_solve,
        [((8, 2, FLAT, LANES), VM), ((32,) + edge, VM), ((32,) + edge, VM)],
        [VM((2, FLAT, LANES), F32), VM((32,) + edge, F32), VM((32,) + edge, F32)],
        limit=4,
        name="first_solve",
    )(ids, adjoint_seed, face_flow, vert_diff, wet_mask)
    xa = lax.ppermute(pxa, "face", side_a)
    xb = lax.ppermute(pxb, "face", side_b)
    rows_ts = ROWS_TS + 48
    fe, ya, yb, za, zb, wloc = call(
        outer_columns,
        [
            ((8, FLAT, LANES), VM),
            ((rows_ts, LANES), VM),
            ((rows_ts, LANES), VM),
            ((ROWS_UV, LANES), VM),
            ((ROWS_UV, LANES), VM),
            ((2, 3) + edge, VM),
        ],
        [VM((4, 2, 4, 1024), F32)],
        limit=4,
        name="outer_columns",
    )(ids, xa, xb, fld, *weights)
    ya, yb = across(ya, yb)
    za, zb = across(za, zb)
    (cf,) = call(coefficients, [((8, 3, FLAT, LANES), VM)], limit=4, name="coefficients")(ids, fld, fe)
    halo = VM((3, 3, LEV, LANES), F32)
    after = [
        ((2, 3, FLAT, LANES), VM),
        ((ROWS_UV, LANES), VM),
        ((ROWS_UV, LANES), VM),
        ((2, 3) + edge, VM),
    ]
    cf, sol_t, ta, tb, fo_t = call(
        functools.partial(step, True, 0),
        [((8, 3, FLAT, LANES), VM)] + after,
        [halo, halo],
        limit=4,
        alias={3: 0},
        name="step_ts",
    )(ids, fld, fe, cf, ya, yb)
    ta, tb = across(ta, tb)
    sol_u, ua, ub, fo_u = call(
        functools.partial(step, False, 2), after, [halo, halo], limit=4, name="step_uv"
    )(ids, fld, fe, cf, za, zb)
    ua, ub = across(ua, ub)

    adj_shape = adjoint_seed.shape
    adj = None
    sent = []
    sizes = []
    for l0, l1 in CHUNKS:
        nl = l1 - l0
        fos = [fo_t, fo_u] if l1 == LEV else []
        units = nl + len(fos)
        per = -(-units // 8)
        args = [ids, sol_t, cf, ta, tb] + fos
        spaces = [None] + [VM] * (len(args) - 1)
        alias = {}
        if adj is not None:
            alias = {len(args): 0}
            args.append(adj)
            spaces.append(pl.ANY)
        adj, g, ga, gb = call(
            functools.partial(last_stencil, 0, l0, nl, len(fos), True),
            [
                (adj_shape, pl.ANY),
                ((units, 2, 3) + edge, VM),
                ((2 * units + per, 8, LANES), VM),
                ((2 * units + per, 8, LANES), VM),
            ],
            [
                halo,
                halo,
                VM((units, 8, LANES), F32),
                VM((units, 8, LANES), F32),
                VM((nl, 2, ROWS, 256), F32),
                pltpu.SemaphoreType.DMA,
            ],
            limit=6,
            alias=alias,
            ins=spaces,
            name="last_ts_%d" % l0,
        )(*args)
        ga, gb = across(ga, gb)
        zs = call(
            functools.partial(smooth, units),
            [((2 * units, 4, 256), VM)] * 4,
            [
                VM((5, 3, 3, 8, LANES), F32),
                VM((units, 8, LANES), F32),
                VM((units, 8, LANES), F32),
            ],
            limit=4,
            name="smooth_%d" % l0,
        )(ids, g, ga, gb, wloc, ya, yb)
        sent.append([zs[0]] + [to_face(zs[k], k) for k in (1, 2, 3)])
        sizes.append(2 * units)
    (adj,) = call(
        functools.partial(last_stencil, 2, 0, LEV, 0, False),
        [(adj_shape, pl.ANY)],
        [halo, halo, VM((LEV, 2, ROWS, 256), F32), pltpu.SemaphoreType.DMA],
        limit=6,
        alias={5: 0},
        ins=[None] + [VM] * 4 + [pl.ANY],
        name="last_uv",
    )(ids, sol_u, cf, ua, ub, adj)
    flat = [x for group in sent for x in group]
    (controls,) = call(
        functools.partial(gather_rows, tuple(sizes)),
        [((sum(sizes), 4, 1024), pl.ANY)],
        [pltpu.SemaphoreType.DMA((len(sizes), 4))],
        ins=[None] + [pl.ANY] * len(flat),
        limit=4,
        name="gather_rows",
    )(ids, *flat)
    return adj, controls


def solution(mesh):
    placed = (
        P(None, None, "tile", "face"),
        P(None, None, "tile", "face"),
        P(None, "tile", "face"),
        P(None, "tile", "face"),
        P(None, ("tile", "face"), None),
    )
    return jax.shard_map(
        on_device,
        mesh=mesh,
        in_specs=placed,
        out_specs=(P(None, None, "tile", "face"), P(None, ("tile", "face"), None)),
        check_vma=False,
    )
```

profile of v0, /device:TPU:97, one launch (start us, length us, event | category | flops | bytes accessed | tf_op | source)
XLA Modules:
  0.0 164.9 jit_solution(14348207181012198267)
XLA Ops:
  6.9 11.7 %first_solve.1 = (f32[8,2,1024,128]{3,2,1,0:T(8,128)S(1)}, f32[32,16,128]{2,1,0:T(8,128)S(1)}, f32[32,16,128]{2,1,0:T(8,128)S(1)}) custom-call(s32[2]{0:T(128)S(1)} %pad_add_fusion.ids.refs_0_, f32[64,4,16,256]{3,2,1,0:T(8,128)S(1)} %copy-done, f32[2,64,16,256]{3,2,1,0:T(8,128)S(1)} %copy-done.1, f32[64,16,256]{2,1,0:T(8,128)S(1)} %copy-done.2, ...), custom_call_target="tpu_custom_call" | custom-call | tf_op jit(solution)/shard_map/first_solve/pallas_call | solution.py:48
  20.1 2.7 %collective-permute-start.3 = (f32[2,4,1024]{2,1,0:T(4,128)S(1)}, f32[2,4,1024]{2,1,0:T(4,128)S(1)}, u32[]{:S(2)}, u32[]{:S(2)}) collective-permute-start(f32[2,4,1024]{2,1,0:T(4,128)S(1)} %copy-done.4), channel_id=1, source_target_pairs={{0,2},{1,3},{2,0},{3,1},{4,6},{5,7},{6,4},{7,5},{8,10},{9,11},{10,... | collective-permute-start | bytes 98312 | tf_op jit(solution)/shard_map/ppermute | solution.py:628
  23.5 3.9 %collective-permute-done.3.w2 = f32[2,4,1024]{2,1,0:T(4,128)S(1)} collective-permute-done((f32[2,4,1024]{2,1,0:T(4,128)S(1)}, f32[2,4,1024]{2,1,0:T(4,128)S(1)}, u32[]{:S(2)}, u32[]{:S(2)}) %collective-permute-start.3) | collective-permute-done | bytes 32800 | tf_op jit(solution)/shard_map/ppermute | solution.py:628
  27.5 5.2 %outer_columns.1 = (f32[8,1024,128]{2,1,0:T(8,128)S(1)}, f32[456,128]{1,0:T(8,128)S(1)}, f32[456,128]{1,0:T(8,128)S(1)}, f32[272,128]{1,0:T(8,128)S(1)}, f32[272...) custom-call(s32[2]{0:T(128)S(1)} %pad_add_fusion.ids.refs_0_, f32[32,16,128]{2,1,0:T(8,128)S(1)} %collective-permute-done.xa, ...), custom_call_target="tpu_custom_call" | custom-call | tf_op jit(solution)/shard_map/outer_columns/pallas_call | solution.py:48
  34.0 6.0 %collective-permute-start.6 = (f32[456,128]{1,0:T(8,128)S(1)}, f32[456,128]{1,0:T(8,128)S(1)}, u32[]{:S(2)}, u32[]{:S(2)}) collective-permute-start(f32[456,128]{1,0:T(8,128)S(1)} %get-tuple-element.49), channel_id=1, source_target_pairs={{0,0},{124,124},{4,8},{8,4},{12,16},{16,12},{20,24},{24,20},{28,32... | collective-permute-start | bytes 700424 | tf_op jit(solution)/shard_map/ppermute | solution.py:625
  40.0 6.7 %coefficients.1.cfi = f32[8,3,1024,128]{3,2,1,0:T(8,128)S(1)} custom-call(s32[2]{0:T(128)S(1)} %pad_add_fusion.ids.refs_0_, f32[8,2,1024,128]{3,2,1,0:T(8,128)S(1)} %get-tuple-element.44.fld, f32[8,1024,128]{2,1,0:T(8,128)S(1)} %get-tuple-element.47.fe), custom_call_target="tpu_custom_call" | custom-call | tf_op jit(solution)/shard_map/coefficients/pallas_call | solution.py:48
  47.5 8.0 %step_ts.1 = (f32[8,3,1024,128]{3,2,1,0:T(8,128)S(1)}, f32[2,3,1024,128]{3,2,1,0:T(8,128)S(1)}, f32[272,128]{1,0:T(8,128)S(1)}, f32[272,128]{1,0:T(8,128)S(1)}, f32[2,3,16,128]{3,2,1,0:T(8,128)S(1)}) custom-call(s32[2]{0:T(128)S(1)} %pad_add_fusion.ids.refs_0_, f32[8,2,1024,128]{3,2,1,0:T(8,128)S(1)} %get-tuple-element.44.fld, ...), custom_call_target="tpu_custom_call", output_to_operand_aliasing={{0}: (3, {})} | custom-call | tf_op jit(solution)/shard_map/step_ts/pallas_call | solution.py:48
  55.6 6.0 %collective-permute-start.12 = (f32[272,128]{1,0:T(8,128)S(1)}, f32[272,128]{1,0:T(8,128)S(1)}, u32[]{:S(2)}, u32[]{:S(2)}) collective-permute-start(f32[272,128]{1,0:T(8,128)S(1)} %get-tuple-element.58), channel_id=1, source_target_pairs={{0,0},{124,124},{4,8},{8,4},{12,16},{16,12},{20,24},{24,20},{28,32... | collective-permute-start | bytes 417800 | tf_op jit(solution)/shard_map/ppermute | solution.py:625
  61.7 5.0 %collective-permute-start.8 = (f32[272,128]{1,0:T(8,128)S(1)}, f32[272,128]{1,0:T(8,128)S(1)}, u32[]{:S(2)}, u32[]{:S(2)}) collective-permute-start(f32[272,128]{1,0:T(8,128)S(1)} %get-tuple-element.52), channel_id=1, source_target_pairs={{0,0},{124,124},{4,8},{8,4},{12,16},{16,12},{20,24},{24,20},{28,32... | collective-permute-start | bytes 417800 | tf_op jit(solution)/shard_map/ppermute | solution.py:625
  67.1 3.0 %last_ts_0.1 = (f32[64,4,16,256]{3,2,1,0:T(8,128)}, f32[16,2,3,16,128]{4,3,2,1,0:T(8,128)S(1)}, f32[34,8,128]{2,1,0:T(8,128)S(1)}, f32[34,8,128]{2,1,0:T(8,128)S(1)}) custom-call(s32[2]{0:T(128)S(1)} %pad_add_fusion.ids.refs_0_, f32[2,3,1024,128]{3,2,1,0:T(8,128)S(1)} %get-tuple-element.56.refs_1_, f32[8,3,1024,128]{3,2,1,0:T(8,128)S(1)} %get-tuple-element.50.cfi.refs_2_, ...), custom_call_target="tpu_custom_call" | custom-call | tf_op jit(solution)/shard_map/last_ts_0/pallas_call | solution.py:48
  70.2 4.0 %last_ts_16.1 = (f32[64,4,16,256]{3,2,1,0:T(8,128)}, f32[24,2,3,16,128]{4,3,2,1,0:T(8,128)S(1)}, f32[51,8,128]{2,1,0:T(8,128)S(1)}, f32[51,8,128]{2,1,0:T(8,128)S(1)}) custom-call(s32[2]{0:T(128)S(1)} %pad_add_fusion.ids.refs_0_, f32[2,3,1024,128]{3,2,1,0:T(8,128)S(1)} %get-tuple-element.56.refs_1_, ...), custom_call_target="tpu_custom_call", output_to_operand_aliasing={{0}: (5, {})} | custom-call | tf_op jit(solution)/shard_map/last_ts_16/pallas_call | solution.py:48
  74.2 6.0 %collective-permute-start.19 = (f32[51,8,128]{2,1,0:T(8,128)S(1)}, f32[51,8,128]{2,1,0:T(8,128)S(1)}, u32[]{:S(2)}, u32[]{:S(2)}) collective-permute-start(f32[51,8,128]{2,1,0:T(8,128)S(1)} %get-tuple-element.74), channel_id=1, source_target_pairs={{0,0},{124,124},{4,8},{8,4},{12,16},{16,12},{20,24},{24,20},{28,32... | collective-permute-start | bytes 626696 | tf_op jit(solution)/shard_map/ppermute | solution.py:625
  80.3 7.9 %step_uv.1 = (f32[2,3,1024,128]{3,2,1,0:T(8,128)S(1)}, f32[272,128]{1,0:T(8,128)S(1)}, f32[272,128]{1,0:T(8,128)S(1)}, f32[2,3,16,128]{3,2,1,0:T(8,128)S(1)}) custom-call(s32[2]{0:T(128)S(1)} %pad_add_fusion.ids.refs_0_, f32[8,2,1024,128]{3,2,1,0:T(8,128)S(1)} %get-tuple-element.44.fld, f32[8,1024,128]{2,1,0:T(8,128)S(1)} %get-tuple-element.47.fe, ...), custom_call_target="tpu_custom_call" | custom-call | tf_op jit(solution)/shard_map/step_uv/pallas_call | solution.py:48
  88.2 3.9 %last_ts_40.1 = (f32[64,4,16,256]{3,2,1,0:T(8,128)}, f32[26,2,3,16,128]{4,3,2,1,0:T(8,128)S(1)}, f32[56,8,128]{2,1,0:T(8,128)S(1)}, f32[56,8,128]{2,1,0:T(8,128)S(1)}) custom-call(s32[2]{0:T(128)S(1)} %pad_add_fusion.ids.refs_0_, f32[2,3,1024,128]{3,2,1,0:T(8,128)S(1)} %get-tuple-element.56.refs_1_, ...), custom_call_target="tpu_custom_call", output_to_operand_aliasing={{0}: (7, {})} | custom-call | tf_op jit(solution)/shard_map/last_ts_40/pallas_call | solution.py:48
  92.2 5.0 %collective-permute-start.24 = (f32[56,8,128]{2,1,0:T(8,128)S(1)}, f32[56,8,128]{2,1,0:T(8,128)S(1)}, u32[]{:S(2)}, u32[]{:S(2)}) collective-permute-start(f32[56,8,128]{2,1,0:T(8,128)S(1)} %get-tuple-element.81), channel_id=1, source_target_pairs={{0,0},{124,124},{4,8},{8,4},{12,16},{16,12},{20,24},{24,20},{28,32... | collective-permute-start | bytes 688136 | tf_op jit(solution)/shard_map/ppermute | solution.py:625
  97.3 6.0 %collective-permute-start.14 = (f32[34,8,128]{2,1,0:T(8,128)S(1)}, f32[34,8,128]{2,1,0:T(8,128)S(1)}, u32[]{:S(2)}, u32[]{:S(2)}) collective-permute-start(f32[34,8,128]{2,1,0:T(8,128)S(1)} %get-tuple-element.66), channel_id=1, source_target_pairs={{0,0},{124,124},{4,8},{8,4},{12,16},{16,12},{20,24},{24,20},{28,32... | collective-permute-start | bytes 417800 | tf_op jit(solution)/shard_map/ppermute | solution.py:625
  103.4 10.0 %smooth_16.1 = (f32[48,4,256]{2,1,0:T(4,128)S(1)}, f32[48,4,256]{2,1,0:T(4,128)S(1)}, f32[48,4,256]{2,1,0:T(4,128)S(1)}, f32[48,4,256]{2,1,0:T(4,128)S(1)}) custom-call(s32[2]{0:T(128)S(1)} %pad_add_fusion.ids.refs_0_, f32[24,2,3,16,128]{4,3,2,1,0:T(8,128)S(1)} %get-tuple-element.72.g, f32[51,8,128]{2,1,0:T(8,128)S(1)} %collective-permute-done.18.ga, ...), custom_call_target="tpu_custom_call" | custom-call | tf_op jit(solution)/shard_map/smooth_16/pallas_call | solution.py:48
  113.5 4.3 %collective-permute-start.20 = (f32[48,4,256]{2,1,0:T(4,128)S(1)}, f32[48,4,256]{2,1,0:T(4,128)S(1)}, u32[]{:S(2)}, u32[]{:S(2)}) collective-permute-start(f32[48,4,256]{2,1,0:T(4,128)S(1)} %get-tuple-element.76), channel_id=1, source_target_pairs={{0,1},{1,0},{2,3},{3,2},{4,5},{5,4},{6,7},{7,6},{8,9},{9,8},{10,11... | collective-permute-start | bytes 589832 | tf_op jit(solution)/shard_map/ppermute | solution.py:628
  117.8 5.0 %collective-permute-start.10 = (f32[272,128]{1,0:T(8,128)S(1)}, f32[272,128]{1,0:T(8,128)S(1)}, u32[]{:S(2)}, u32[]{:S(2)}) collective-permute-start(f32[272,128]{1,0:T(8,128)S(1)} %get-tuple-element.55), channel_id=1, source_target_pairs={{0,0},{124,124},{4,8},{8,4},{12,16},{16,12},{20,24},{24,20},{28,32... | collective-permute-start | bytes 417800 | tf_op jit(solution)/shard_map/ppermute | solution.py:625
  122.8 6.9 %smooth_0.1 = (f32[32,4,256]{2,1,0:T(4,128)S(1)}, f32[32,4,256]{2,1,0:T(4,128)S(1)}, f32[32,4,256]{2,1,0:T(4,128)S(1)}, f32[32,4,256]{2,1,0:T(4,128)S(1)}) custom-call(s32[2]{0:T(128)S(1)} %pad_add_fusion.ids.refs_0_, f32[16,2,3,16,128]{4,3,2,1,0:T(8,128)S(1)} %get-tuple-element.64.g, f32[34,8,128]{2,1,0:T(8,128)S(1)} %collective-permute-done.13.ga, ...), custom_call_target="tpu_custom_call" | custom-call | tf_op jit(solution)/shard_map/smooth_0/pallas_call | solution.py:48
  131.9 10.8 %smooth_40.1 = (f32[52,4,256]{2,1,0:T(4,128)S(1)}, f32[52,4,256]{2,1,0:T(4,128)S(1)}, f32[52,4,256]{2,1,0:T(4,128)S(1)}, f32[52,4,256]{2,1,0:T(4,128)S(1)}) custom-call(s32[2]{0:T(128)S(1)} %pad_add_fusion.ids.refs_0_, f32[26,2,3,16,128]{4,3,2,1,0:T(8,128)S(1)} %get-tuple-element.79.g, f32[56,8,128]{2,1,0:T(8,128)S(1)} %collective-permute-done.23.ga, ...), custom_call_target="tpu_custom_call" | custom-call | tf_op jit(solution)/shard_map/smooth_40/pallas_call | solution.py:48
  146.5 8.2 %last_uv.1 = f32[64,4,16,256]{3,2,1,0:T(8,128)} custom-call(s32[2]{0:T(128)S(1)} %pad_add_fusion.ids.refs_0_, f32[2,3,1024,128]{3,2,1,0:T(8,128)S(1)} %get-tuple-element.53.refs_1_, f32[8,3,1024,128]{3,2,1,0:T(8,128)S(1)} %get-tuple-element.50.cfi.refs_2_, f32[272,128]{1,0:T(8,128)S(1)} %collective-permute-done.9.refs_3_, ...), custom_call_target="tpu_custom_call", output_to_operand_aliasing={{}: (5, {})} | custom-call | tf_op jit(solution)/shard_map/last_uv/pallas_call | solution.py:48
  154.7 3.4 %collective-permute-done.21.refs_6_ = f32[48,4,256]{2,1,0:T(4,128)S(1)} collective-permute-done((f32[48,4,256]{2,1,0:T(4,128)S(1)}, f32[48,4,256]{2,1,0:T(4,128)S(1)}, u32[]{:S(2)}, u32[]{:S(2)}) %collective-permute-start.21) | collective-permute-done | bytes 196640 | tf_op jit(solution)/shard_map/ppermute | solution.py:628
  158.1 4.8 %collective-permute-done.22.refs_7_ = f32[48,4,256]{2,1,0:T(4,128)S(1)} collective-permute-done((f32[48,4,256]{2,1,0:T(4,128)S(1)}, f32[48,4,256]{2,1,0:T(4,128)S(1)}, u32[]{:S(2)}, u32[]{:S(2)}) %collective-permute-start.22) | collective-permute-done | bytes 196640 | tf_op jit(solution)/shard_map/ppermute | solution.py:628
  (56 shorter events, 19.5 us)
Async XLA Ops:
  18.6 8.8 %collective-permute-start = (f32[32,16,128]{2,1,0:T(8,128)S(1)}, f32[32,16,128]{2,1,0:T(8,128)S(1)}, u32[]{:S(2)}, u32[]{:S(2)}) collective-permute-start(f32[32,16,128]{2,1,0:T(8,128)S(1)} %get-tuple-element.45), channel_id=1, source_target_pairs={{0,1},{1,0},{2,3},{3,2},{4,5},{5,4},{6,7},{7,6},{8,9},{9,8},{10,11... | collective-permute-start | bytes 786440 | tf_op jit(solution)/shard_map/ppermute | solution.py:639
  32.7 14.0 %collective-permute-start.5 = (f32[456,128]{1,0:T(8,128)S(1)}, f32[456,128]{1,0:T(8,128)S(1)}, u32[]{:S(2)}, u32[]{:S(2)}) collective-permute-start(f32[456,128]{1,0:T(8,128)S(1)} %get-tuple-element.48), channel_id=1, source_target_pairs={{0,4},{4,0},{8,12},{12,8},{16,20},{20,16},{24,28},{28,24},{32,36},... | collective-permute-start | bytes 700424 | tf_op jit(solution)/shard_map/ppermute | solution.py:625
  34.0 13.5 %collective-permute-start.6 = (f32[456,128]{1,0:T(8,128)S(1)}, f32[456,128]{1,0:T(8,128)S(1)}, u32[]{:S(2)}, u32[]{:S(2)}) collective-permute-start(f32[456,128]{1,0:T(8,128)S(1)} %get-tuple-element.49), channel_id=1, source_target_pairs={{0,0},{124,124},{4,8},{8,4},{12,16},{16,12},{20,24},{24,20},{28,32... | collective-permute-start | bytes 700424 | tf_op jit(solution)/shard_map/ppermute | solution.py:625
  55.5 11.2 %collective-permute-start.11 = (f32[272,128]{1,0:T(8,128)S(1)}, f32[272,128]{1,0:T(8,128)S(1)}, u32[]{:S(2)}, u32[]{:S(2)}) collective-permute-start(f32[272,128]{1,0:T(8,128)S(1)} %get-tuple-element.57), channel_id=1, source_target_pairs={{0,4},{4,0},{8,12},{12,8},{16,20},{20,16},{24,28},{28,24},{32,36},... | collective-permute-start | bytes 417800 | tf_op jit(solution)/shard_map/ppermute | solution.py:625
  55.6 11.5 %collective-permute-start.12 = (f32[272,128]{1,0:T(8,128)S(1)}, f32[272,128]{1,0:T(8,128)S(1)}, u32[]{:S(2)}, u32[]{:S(2)}) collective-permute-start(f32[272,128]{1,0:T(8,128)S(1)} %get-tuple-element.58), channel_id=1, source_target_pairs={{0,0},{124,124},{4,8},{8,4},{12,16},{16,12},{20,24},{24,20},{28,32... | collective-permute-start | bytes 417800 | tf_op jit(solution)/shard_map/ppermute | solution.py:625
  61.6 18.6 %collective-permute-start.7 = (f32[272,128]{1,0:T(8,128)S(1)}, f32[272,128]{1,0:T(8,128)S(1)}, u32[]{:S(2)}, u32[]{:S(2)}) collective-permute-start(f32[272,128]{1,0:T(8,128)S(1)} %get-tuple-element.51), channel_id=1, source_target_pairs={{0,4},{4,0},{8,12},{12,8},{16,20},{20,16},{24,28},{28,24},{32,36},... | collective-permute-start | bytes 417800 | tf_op jit(solution)/shard_map/ppermute | solution.py:625
  61.7 18.5 %collective-permute-start.8 = (f32[272,128]{1,0:T(8,128)S(1)}, f32[272,128]{1,0:T(8,128)S(1)}, u32[]{:S(2)}, u32[]{:S(2)}) collective-permute-start(f32[272,128]{1,0:T(8,128)S(1)} %get-tuple-element.52), channel_id=1, source_target_pairs={{0,0},{124,124},{4,8},{8,4},{12,16},{16,12},{20,24},{24,20},{28,32... | collective-permute-start | bytes 417800 | tf_op jit(solution)/shard_map/ppermute | solution.py:625
  74.1 23.2 %collective-permute-start.18 = (f32[51,8,128]{2,1,0:T(8,128)S(1)}, f32[51,8,128]{2,1,0:T(8,128)S(1)}, u32[]{:S(2)}, u32[]{:S(2)}) collective-permute-start(f32[51,8,128]{2,1,0:T(8,128)S(1)} %get-tuple-element.73), channel_id=1, source_target_pairs={{0,4},{4,0},{8,12},{12,8},{16,20},{20,16},{24,28},{28,24},{32,36},... | collective-permute-start | bytes 626696 | tf_op jit(solution)/shard_map/ppermute | solution.py:625
  74.2 29.1 %collective-permute-start.19 = (f32[51,8,128]{2,1,0:T(8,128)S(1)}, f32[51,8,128]{2,1,0:T(8,128)S(1)}, u32[]{:S(2)}, u32[]{:S(2)}) collective-permute-start(f32[51,8,128]{2,1,0:T(8,128)S(1)} %get-tuple-element.74), channel_id=1, source_target_pairs={{0,0},{124,124},{4,8},{8,4},{12,16},{16,12},{20,24},{24,20},{28,32... | collective-permute-start | bytes 626696 | tf_op jit(solution)/shard_map/ppermute | solution.py:625
  92.1 38.0 %collective-permute-start.23 = (f32[56,8,128]{2,1,0:T(8,128)S(1)}, f32[56,8,128]{2,1,0:T(8,128)S(1)}, u32[]{:S(2)}, u32[]{:S(2)}) collective-permute-start(f32[56,8,128]{2,1,0:T(8,128)S(1)} %get-tuple-element.80), channel_id=1, source_target_pairs={{0,4},{4,0},{8,12},{12,8},{16,20},{20,16},{24,28},{28,24},{32,36},... | collective-permute-start | bytes 688136 | tf_op jit(solution)/shard_map/ppermute | solution.py:625
  92.2 39.0 %collective-permute-start.24 = (f32[56,8,128]{2,1,0:T(8,128)S(1)}, f32[56,8,128]{2,1,0:T(8,128)S(1)}, u32[]{:S(2)}, u32[]{:S(2)}) collective-permute-start(f32[56,8,128]{2,1,0:T(8,128)S(1)} %get-tuple-element.81), channel_id=1, source_target_pairs={{0,0},{124,124},{4,8},{8,4},{12,16},{16,12},{20,24},{24,20},{28,32... | collective-permute-start | bytes 688136 | tf_op jit(solution)/shard_map/ppermute | solution.py:625
  97.2 16.3 %collective-permute-start.13 = (f32[34,8,128]{2,1,0:T(8,128)S(1)}, f32[34,8,128]{2,1,0:T(8,128)S(1)}, u32[]{:S(2)}, u32[]{:S(2)}) collective-permute-start(f32[34,8,128]{2,1,0:T(8,128)S(1)} %get-tuple-element.65), channel_id=1, source_target_pairs={{0,4},{4,0},{8,12},{12,8},{16,20},{20,16},{24,28},{28,24},{32,36},... | collective-permute-start | bytes 417800 | tf_op jit(solution)/shard_map/ppermute | solution.py:625
  97.3 20.4 %collective-permute-start.14 = (f32[34,8,128]{2,1,0:T(8,128)S(1)}, f32[34,8,128]{2,1,0:T(8,128)S(1)}, u32[]{:S(2)}, u32[]{:S(2)}) collective-permute-start(f32[34,8,128]{2,1,0:T(8,128)S(1)} %get-tuple-element.66), channel_id=1, source_target_pairs={{0,0},{124,124},{4,8},{8,4},{12,16},{16,12},{20,24},{24,20},{28,32... | collective-permute-start | bytes 417800 | tf_op jit(solution)/shard_map/ppermute | solution.py:625
  103.4 26.3 %collective-permute-start.9 = (f32[272,128]{1,0:T(8,128)S(1)}, f32[272,128]{1,0:T(8,128)S(1)}, u32[]{:S(2)}, u32[]{:S(2)}) collective-permute-start(f32[272,128]{1,0:T(8,128)S(1)} %get-tuple-element.54), channel_id=1, source_target_pairs={{0,4},{4,0},{8,12},{12,8},{16,20},{20,16},{24,28},{28,24},{32,36},... | collective-permute-start | bytes 417800 | tf_op jit(solution)/shard_map/ppermute | solution.py:625
  113.5 32.6 %collective-permute-start.20 = (f32[48,4,256]{2,1,0:T(4,128)S(1)}, f32[48,4,256]{2,1,0:T(4,128)S(1)}, u32[]{:S(2)}, u32[]{:S(2)}) collective-permute-start(f32[48,4,256]{2,1,0:T(4,128)S(1)} %get-tuple-element.76), channel_id=1, source_target_pairs={{0,1},{1,0},{2,3},{3,2},{4,5},{5,4},{6,7},{7,6},{8,9},{9,8},{10,11... | collective-permute-start | bytes 589832 | tf_op jit(solution)/shard_map/ppermute | solution.py:628
  117.8 25.0 %collective-permute-start.10 = (f32[272,128]{1,0:T(8,128)S(1)}, f32[272,128]{1,0:T(8,128)S(1)}, u32[]{:S(2)}, u32[]{:S(2)}) collective-permute-start(f32[272,128]{1,0:T(8,128)S(1)} %get-tuple-element.55), channel_id=1, source_target_pairs={{0,0},{124,124},{4,8},{8,4},{12,16},{16,12},{20,24},{24,20},{28,32... | collective-permute-start | bytes 417800 | tf_op jit(solution)/shard_map/ppermute | solution.py:625
  129.7 13.2 %collective-permute-start.15 = (f32[32,4,256]{2,1,0:T(4,128)S(1)}, f32[32,4,256]{2,1,0:T(4,128)S(1)}, u32[]{:S(2)}, u32[]{:S(2)}) collective-permute-start(f32[32,4,256]{2,1,0:T(4,128)S(1)} %get-tuple-element.69), channel_id=1, source_target_pairs={{0,1},{1,0},{2,3},{3,2},{4,5},{5,4},{6,7},{7,6},{8,9},{9,8},{10,11... | collective-permute-start | bytes 393224 | tf_op jit(solution)/shard_map/ppermute | solution.py:628
  130.1 14.0 %collective-permute-start.16 = (f32[32,4,256]{2,1,0:T(4,128)S(1)}, f32[32,4,256]{2,1,0:T(4,128)S(1)}, u32[]{:S(2)}, u32[]{:S(2)}) collective-permute-start(f32[32,4,256]{2,1,0:T(4,128)S(1)} %get-tuple-element.70), channel_id=1, source_target_pairs={{0,2},{1,3},{2,0},{3,1},{4,6},{5,7},{6,4},{7,5},{8,10},{9,11},{10,... | collective-permute-start | bytes 393224 | tf_op jit(solution)/shard_map/ppermute | solution.py:628
  131.2 13.8 %collective-permute-start.17 = (f32[32,4,256]{2,1,0:T(4,128)S(1)}, f32[32,4,256]{2,1,0:T(4,128)S(1)}, u32[]{:S(2)}, u32[]{:S(2)}) collective-permute-start(f32[32,4,256]{2,1,0:T(4,128)S(1)} %get-tuple-element.71), channel_id=1, source_target_pairs={{0,3},{1,2},{2,1},{3,0},{4,7},{5,6},{6,5},{7,4},{8,11},{9,10},{10,... | collective-permute-start | bytes 393224 | tf_op jit(solution)/shard_map/ppermute | solution.py:628
  142.8 20.2 %collective-permute-start.25 = (f32[52,4,256]{2,1,0:T(4,128)S(1)}, f32[52,4,256]{2,1,0:T(4,128)S(1)}, u32[]{:S(2)}, u32[]{:S(2)}) collective-permute-start(f32[52,4,256]{2,1,0:T(4,128)S(1)} %get-tuple-element.83), channel_id=1, source_target_pairs={{0,1},{1,0},{2,3},{3,2},{4,5},{5,4},{6,7},{7,6},{8,9},{9,8},{10,11... | collective-permute-start | bytes 638984 | tf_op jit(solution)/shard_map/ppermute | solution.py:628
  142.9 20.0 %collective-permute-start.26 = (f32[52,4,256]{2,1,0:T(4,128)S(1)}, f32[52,4,256]{2,1,0:T(4,128)S(1)}, u32[]{:S(2)}, u32[]{:S(2)}) collective-permute-start(f32[52,4,256]{2,1,0:T(4,128)S(1)} %get-tuple-element.84), channel_id=1, source_target_pairs={{0,2},{1,3},{2,0},{3,1},{4,6},{5,7},{6,4},{7,5},{8,10},{9,11},{10,... | collective-permute-start | bytes 638984 | tf_op jit(solution)/shard_map/ppermute | solution.py:628
  144.1 18.9 %collective-permute-start.27 = (f32[52,4,256]{2,1,0:T(4,128)S(1)}, f32[52,4,256]{2,1,0:T(4,128)S(1)}, u32[]{:S(2)}, u32[]{:S(2)}) collective-permute-start(f32[52,4,256]{2,1,0:T(4,128)S(1)} %get-tuple-element.85), channel_id=1, source_target_pairs={{0,3},{1,2},{2,1},{3,0},{4,7},{5,6},{6,5},{7,4},{8,11},{9,10},{10,... | collective-permute-start | bytes 638984 | tf_op jit(solution)/shard_map/ppermute | solution.py:628
  145.0 13.2 %collective-permute-start.21 = (f32[48,4,256]{2,1,0:T(4,128)S(1)}, f32[48,4,256]{2,1,0:T(4,128)S(1)}, u32[]{:S(2)}, u32[]{:S(2)}) collective-permute-start(f32[48,4,256]{2,1,0:T(4,128)S(1)} %get-tuple-element.77), channel_id=1, source_target_pairs={{0,2},{1,3},{2,0},{3,1},{4,6},{5,7},{6,4},{7,5},{8,10},{9,11},{10,... | collective-permute-start | bytes 589832 | tf_op jit(solution)/shard_map/ppermute | solution.py:628
  146.1 16.8 %collective-permute-start.22 = (f32[48,4,256]{2,1,0:T(4,128)S(1)}, f32[48,4,256]{2,1,0:T(4,128)S(1)}, u32[]{:S(2)}, u32[]{:S(2)}) collective-permute-start(f32[48,4,256]{2,1,0:T(4,128)S(1)} %get-tuple-element.78), channel_id=1, source_target_pairs={{0,3},{1,2},{2,1},{3,0},{4,7},{5,6},{6,5},{7,4},{8,11},{9,10},{10,... | collective-permute-start | bytes 589832 | tf_op jit(solution)/shard_map/ppermute | solution.py:628
  (9 other events, 44.2 us)
where the time goes:
time: 166 us; the launch traced here: 165 us
  Pallas kernels  88.4 us (53%)
  starting transfers between devices  55.9 us (34%)
  waiting for transfers between devices  13.4 us (8%)
  local copies, waits for them, and re-layouts  6.23 us (4%)
    pallas_call x13, Pallas kernels, run(): pl.pallas_call(kernel, out_shape=[jax.ShapeDtypeStruct(s, F32) for s, _ i...  88.4 us
    ppermute x14, starting transfers between devices, across(): return (lax.ppermute(a, 'tile', pair_a), lax.ppermute(b, 'tile', pair_b))  40.8 us
    ppermute x12, starting transfers between devices, to_face(): return lax.ppermute(x, 'face', [(i, i ^ k) for i in range(4)])  13.7 us
    ppermute x12, waiting for transfers between devices, to_face(): return lax.ppermute(x, 'face', [(i, i ^ k) for i in range(4)])  12.1 us
    unnamed x10, local copies, waits for them, and re-layouts  6.23 us
  transfers between devices with their start and end apart: 28, of which 5 were waited for; matrix products, arithmetic and copies ran while one was open for 0% of the time, Pallas kernels for 37%

commit v1 on v0

v1 whole, which is shorter than its diff:
```python
import functools

import jax
import jax.numpy as jnp
from jax import lax
from jax.experimental import pallas as pl
from jax.experimental.pallas import tpu as pltpu
from jax.sharding import PartitionSpec as P

F32 = jnp.float32
LEV = 64
ROWS = 16
LANES = 128
FLAT = LEV * ROWS
WET, UE, VN, VD = 4, 5, 6, 7
KAPPA = 0.15
MIB = 2**20
UNROLL_C = 4
UNROLL_S = 4
UNROLL_L = 4
UNROLL_M = 2

CHUNKS = ((0, 24), (24, 64))
PIECES = ((0, 0, 24), (1, 0, 22), (1, 22, 42))


def iota(shape, dim):
    return lax.broadcasted_iota(jnp.int32, shape, dim)


def rows_of(level):
    return pl.ds(pl.multiple_of(level * ROWS, ROWS), ROWS)


def east_of(tiles):
    last = iota(tiles[0].shape, 1) == LANES - 1
    turned = [pltpu.roll(t, LANES - 1, 1) for t in tiles]
    return [jnp.where(last, turned[(i + 1) % 3], turned[i]) for i in range(3)]


def west_of(tiles):
    first = iota(tiles[0].shape, 1) == 0
    turned = [pltpu.roll(t, 1, 1) for t in tiles]
    return [jnp.where(first, turned[(i + 2) % 3], turned[i]) for i in range(3)]


def call(kernel, outs, scratch=(), limit=8, alias=None, name=None, ins=None):
    def run(*args):
        args = list(args)
        specs = [pl.BlockSpec(memory_space=pltpu.SMEM)]
        for i in range(1, len(args)):
            if ins is not None and ins[i] is pltpu.HBM:
                args[i] = pltpu.with_memory_space_constraint(args[i], pltpu.HBM)
        for i in range(1, len(args)):
            space = pltpu.VMEM if ins is None else ins[i]
            specs.append(pl.BlockSpec(memory_space=space))
        return pl.pallas_call(
            kernel,
            out_shape=[jax.ShapeDtypeStruct(s, F32) for s, _ in outs],
            in_specs=specs,
            out_specs=[pl.BlockSpec(memory_space=m) for _, m in outs],
            scratch_shapes=list(scratch),
            input_output_aliases=alias or {},
            compiler_params=pltpu.CompilerParams(vmem_limit_bytes=limit * MIB),
            name=name,
        )(*args)

    return run


VM = pltpu.VMEM


HALF = LEV // 2


def pair_of(i):
    return rows_of(i), rows_of(LEV - 1 - i)


def thirds(tri, wet, vd, tiles, beside=None):
    zero = jnp.zeros((ROWS, LANES), F32)

    def body(i, carry):
        low, rat, low2, rat2 = ([], [], [], [])
        top, bottom = pair_of(i)
        for t in tiles:
            w = wet(t, i)
            up = vd(t, i) * w * wet(t, i + 1)
            p, q = carry[0][t - tiles[0]], carry[1][t - tiles[0]]
            inv = 1.0 / (1.0 + p + up - p * q)
            r = up * inv
            tri[0, t - tiles[0], top, :] = p
            tri[1, t - tiles[0], top, :] = inv
            tri[2, t - tiles[0], top, :] = r
            low.append(up)
            rat.append(r)
            j = LEV - 1 - i
            up = vd(t, j - 1) * wet(t, j - 1) * wet(t, j)
            p, q = carry[2][t - tiles[0]], carry[3][t - tiles[0]]
            inv = 1.0 / (1.0 + p + up - p * q)
            r = up * inv
            tri[0, t - tiles[0], bottom, :] = p
            tri[1, t - tiles[0], bottom, :] = inv
            tri[2, t - tiles[0], bottom, :] = r
            low2.append(up)
            rat2.append(r)
        if beside is not None:
            beside(i)
        return low, rat, low2, rat2

    n = len(tiles)
    lax.fori_loop(0, HALF, body, tuple([zero] * n for _ in range(4)))


def eliminate(rhs, put, get, tri, items, beside=None):
    zero = jnp.zeros((ROWS, LANES), F32)
    n = len(items)

    def inwards(i, carry):
        out = ([], [])
        for side, at in enumerate(pair_of(i)):
            for c, (key, t) in enumerate(items):
                x = (rhs(key, t, at) + tri(0, t, at) * carry[side][c]) * tri(1, t, at)
                put(key, t, at, x)
                out[side].append(x)
        return out

    ends = lax.fori_loop(0, HALF, inwards, ([zero] * n, [zero] * n))
    at, bt = pair_of(HALF - 1)
    start = ([], [])
    for c, (key, t) in enumerate(items):
        r, r2 = tri(2, t, at), tri(2, t, bt)
        y = (ends[0][c] + r * ends[1][c]) * (1.0 / (1.0 - r * r2))
        y2 = ends[1][c] + r2 * y
        put(key, t, at, y)
        put(key, t, bt, y2)
        start[0].append(y)
        start[1].append(y2)
    if beside is not None:
        beside(HALF - 1, start)

    def outwards(k, carry):
        out = ([], [])
        for side, at in enumerate(pair_of(HALF - 2 - k)):
            for c, (key, t) in enumerate(items):
                x = get(key, t, at) + tri(2, t, at) * carry[side][c]
                put(key, t, at, x)
                out[side].append(x)
        if beside is not None:
            beside(HALF - 2 - k, out)
        return out

    return lax.fori_loop(0, HALF - 1, outwards, start)


def first_solve(ids, seed, flow, vd, wet, fld, tri, pxa, pxb, wbuf, pw, pe, sems):
    def tile_copy(src, dst, k):
        copy = pltpu.make_async_copy(src, dst, sems.at[k])
        copy.start()
        return copy

    def place(f, t):
        return fld.at[f, t].reshape(LEV, ROWS, LANES)

    early, late = [], []
    for t in range(2):
        cols = pl.ds(t * LANES, LANES)
        early.append(tile_copy(wet.at[:, :, cols], wbuf.at[t], 8 * t))
        early.append(tile_copy(vd.at[:, :, cols], place(VD, t), 8 * t + 1))
        for v in range(2):
            early.append(tile_copy(flow.at[v, :, :, cols], place(UE + v, t), 8 * t + 2 + v))
    for t in range(2):
        cols = pl.ds(t * LANES, LANES)
        for v in range(4):
            late.append(tile_copy(seed.at[:, v, :, cols], place(v, t), 8 * t + 4 + v))
    for copy in early:
        copy.wait()

    def wet_to_float(i, carry):
        for k in range(8):
            for t in range(2):
                fld[WET, t, rows_of(8 * i + k), :] = wbuf[t, 8 * i + k].astype(F32)
        return carry

    lax.fori_loop(0, LEV // 8, wet_to_float, 0)
    lane = iota((ROWS, LANES), 1)
    zero = jnp.zeros((ROWS, LANES), F32)
    odd = lax.rem(ids[0], 2) == 1

    def pack(values):
        west = east = zero
        for b, x0, x1 in values:
            mine = (lane >= 8 * b) & (lane < 8 * b + 8)
            west = jnp.where(mine, pltpu.roll(x0, 8 * b, 1) if b else x0, west)
            s = (8 * b + 8) % LANES
            east = jnp.where(mine, pltpu.roll(x1, s, 1) if s else x1, east)
        return west, east

    def statics(i):
        values = []
        for half, at in enumerate(pair_of(i)):
            for f in range(4, 8):
                values.append((8 * half + f, fld[f, 0, at, :], fld[f, 1, at, :]))
        west, east = pack(values)
        pw[rows_of(i), :] = west
        pe[rows_of(i), :] = east

    thirds(
        tri,
        lambda t, level: fld[WET, t, rows_of(level), :],
        lambda t, level: fld[VD, t, rows_of(level), :],
        (0, 1),
        statics,
    )
    for copy in late:
        copy.wait()

    def put(v, t, at, x):
        fld[v, t, at, :] = x

    for pair in ((0, 1), (2, 3)):

        def solved(i, out, pair=pair):
            values = []
            for half in range(2):
                for c, v in enumerate(pair):
                    values.append((8 * half + v, out[half][2 * c], out[half][2 * c + 1]))
            west, east = pack(values)
            at = rows_of(i)
            west = pw[at, :] + west
            east = pe[at, :] + east
            if pair[0] == 0:
                pw[at, :] = west
                pe[at, :] = east
            else:
                pxa[at, :] = jnp.where(odd, west, east)
                pxb[at, :] = jnp.where(odd, east, west)

        eliminate(
            lambda v, t, at: fld[v, t, at, :] * fld[WET, t, at, :],
            put,
            lambda v, t, at: fld[v, t, at, :],
            lambda k, t, at: tri[k, t, at, :],
            [(v, t) for v in pair for t in range(2)],
            solved,
        )


OUTER = 5 * 2 * LEV
ROWS_1 = OUTER + LEV
ROWS_2 = 2 * 2 * LEV + 2 * 8
BLOCKS_2 = ROWS_2 // 8


def edge_pack(tiles8):
    lane = iota((8, LANES), 1)
    packed = jnp.zeros((8, LANES), F32)
    for g, t in enumerate(tiles8):
        turned = pltpu.roll(t, (16 * g + 8) % LANES, 1)
        packed = jnp.where((lane >= 16 * g) & (lane < 16 * g + 16), turned, packed)
    return packed


def edge_unpack(packed, g):
    return pltpu.roll(packed, (-(16 * g + 8)) % LANES, 1)


def put_edges(todd, pick, fields, oa, ob):
    for f in range(fields):
        for t in range(2):
            for g in range(8):
                n, s = pick(f, t, g)
                at = pl.ds((f * 2 + t) * LEV + 8 * g, 8)
                oa[at, :] = jnp.where(todd, s, n)
                ob[at, :] = jnp.where(todd, n, s)
        outer = [pick(f, 2, g) for g in range(8)]
        n = edge_pack([o[0] for o in outer])
        s = edge_pack([o[1] for o in outer])
        at = pl.ds(fields * 2 * LEV + 8 * f, 8)
        oa[at, :] = jnp.where(todd, s, n)
        ob[at, :] = jnp.where(todd, n, s)


def edge_rows(ref, g):
    north = ref[pl.ds(g * 8 * ROWS + ROWS - 1, 8, stride=ROWS), :]
    south = ref[pl.ds(g * 8 * ROWS, 8, stride=ROWS), :]
    return north, south


def main_edges(ids, fld, ya, yb):
    todd = lax.rem(ids[1], 2) == 1
    for k, f in enumerate((0, 1, WET, 2, 3)):
        for t in range(2):
            for g in range(8):
                n, s = edge_rows(fld.at[f, t], g)
                if f == WET:
                    n = n * (KAPPA - 0.5 * edge_rows(fld.at[VN, t], g)[0])
                at = pl.ds((2 * k + t) * LEV + 8 * g, 8)
                ya[at, :] = jnp.where(todd, s, n)
                yb[at, :] = jnp.where(todd, n, s)


def outer_edges(ids, xa, xb, ya_in, yb_in, ya, yb):
    face, tile = ids[0], ids[1]
    odd = lax.rem(face, 2) == 1
    todd = lax.rem(tile, 2) == 1
    for g in range(4):
        na, sa = edge_rows(xa, g)
        nb, sb = edge_rows(xb, g)
        west = (jnp.where(odd, na, nb), jnp.where(odd, sa, sb))
        east = (jnp.where(odd, nb, na), jnp.where(odd, sb, sa))
        for first, inside, (n, s) in ((0, face > 0, west), (HALF, face < 3, east)):
            n = jnp.where(inside, n, 0.0)
            s = jnp.where(inside, s, 0.0)
            at = pl.ds(OUTER + first + 8 * g, 8)
            ya[at, :] = jnp.where(todd, s, n)
            yb[at, :] = jnp.where(todd, n, s)


def local_weights(ids, w0, w1, w2, w3, wloc, pieces):
    face = ids[0]
    for k, w in enumerate((w0, w1, w2, w3)):
        pieces[k] = w[...]
    lane4 = iota((4, LANES), 1)
    for d in range(4):
        slot = jnp.bitwise_xor(face, d)
        for c in range(2):
            for t in range(3):
                at = pl.ds(4 * d, 4)
                if t < 2:
                    first = pl.multiple_of((2 * face + t) * LANES, LANES)
                    wloc[c, t, at, :] = pieces[slot, c, :, pl.ds(first, LANES)]
                    continue
                first = pl.multiple_of(jnp.minimum(2 * face + 2, 7) * LANES, LANES)
                e = pieces[slot, c, :, pl.ds(first, LANES)]
                first = pl.multiple_of(jnp.maximum(2 * face - 1, 0) * LANES, LANES)
                w = pieces[slot, c, :, pl.ds(first, LANES)]
                w = jnp.where((lane4 >= 120) & (face > 0), w, 0.0)
                wloc[c, t, at, :] = jnp.where((lane4 < 8) & (face < 3), e, w)


def coefficients(ids, fld, xa, xb, fe, cf, tri):
    row = iota((ROWS, LANES), 0)
    face = ids[0]
    odd = lax.rem(face, 2) == 1
    lane = iota((ROWS, LANES), 1)
    on_east = (lane < 8) & (face < 3)
    on_west = (lane >= 120) & (face > 0)

    def unpack(n, carry):
        for i in (2 * n, 2 * n + 1):
            a, b = xa[rows_of(i), :], xb[rows_of(i), :]
            from_west = jnp.where(odd, a, b)
            from_east = jnp.where(odd, b, a)
            for half, at in enumerate(pair_of(i)):
                for f in range(8):
                    k = 8 * half + f
                    w = pltpu.roll(from_west, (120 - 8 * k) % LANES, 1)
                    e = pltpu.roll(from_east, (-8 * k) % LANES, 1)
                    fe[f, at, :] = jnp.where(on_east, e, jnp.where(on_west, w, 0.0))
        return carry

    lax.fori_loop(0, HALF // 2, unpack, 0)
    thirds(
        tri,
        lambda t, level: fe[WET, rows_of(level), :],
        lambda t, level: fe[VD, rows_of(level), :],
        (2,),
    )

    def body(i, carry):
        for k in range(UNROLL_C):
            at = rows_of(UNROLL_C * i + k)

            def get(f):
                return [fld[f, 0, at, :], fld[f, 1, at, :], fe[f, at, :]]

            wet, ue, vn = (get(f) for f in (WET, UE, VN))
            wet_e = east_of(wet)
            qw_w = west_of([w * (KAPPA - 0.5 * u) for w, u in zip(wet, ue)])
            for t in range(3):
                w = wet[t]
                ce = w * (KAPPA + 0.5 * ue[t]) * wet_e[t]
                cw = w * qw_w[t]
                wn = jnp.where(row == ROWS - 1, 1.0, pltpu.roll(w, ROWS - 1, 0))
                qs = jnp.where(row == 0, 1.0, pltpu.roll(w * (KAPPA - 0.5 * vn[t]), 1, 0))
                cf[0, t, at, :] = ce
                cf[1, t, at, :] = cw
                cf[2, t, at, :] = w * (KAPPA + 0.5 * vn[t]) * wn
                cf[3, t, at, :] = w * qs
                cf[4, t, at, :] = w - ce - cw
        return carry

    lax.fori_loop(0, LEV // UNROLL_C, body, 0)


def slot_of(level):
    return jnp.where(level < HALF, level, LEV + HALF - 1 - level)


def take_first_edges(ids, ya, yb, hn, hs, first):
    todd = lax.rem(ids[1], 2) == 1
    lane = iota((8, LANES), 1)

    def both(at):
        a, b = ya[at, :], yb[at, :]
        return jnp.where(todd, b, a), jnp.where(todd, a, b)

    for f, k in enumerate((0, 1, 2) if first else (3, 4)):
        for t in range(2):
            for g in range(8):
                at = pl.ds(8 * g, 8)
                n, s = both(pl.ds((2 * k + t) * LEV + 8 * g, 8))
                hn[f, t, at, :] = n
                hs[f, t, at, :] = s
    for g in range(4):
        wests = both(pl.ds(OUTER + 8 * g, 8))
        easts = both(pl.ds(OUTER + HALF + 8 * g, 8))
        for half in range(2):

            def outer(side, f):
                b = 8 * half + f
                w = pltpu.roll(wests[side], (120 - 8 * b) % LANES, 1)
                e = pltpu.roll(easts[side], (-8 * b) % LANES, 1)
                return jnp.where(lane < 64, e, w)

            at = pl.ds(HALF * half + 8 * g, 8)
            for f, k in enumerate((0, 1) if first else (2, 3)):
                hn[f, 2, at, :] = outer(0, k)
                hs[f, 2, at, :] = outer(1, k)
            if first:
                hn[2, 2, at, :] = outer(0, WET)
                hs[2, 2, at, :] = outer(1, WET) * (KAPPA - 0.5 * outer(1, VN))


def take_edges(ids, load, hn, hs, groups=(0, 8)):
    todd = lax.rem(ids[1], 2) == 1
    for f in range(2):
        oa, ob = load(32 + f)
        on, os = jnp.where(todd, ob, oa), jnp.where(todd, oa, ob)
        for g in range(*groups):
            at = pl.ds(8 * g, 8)
            for t in range(2):
                a, b = load((f * 2 + t) * 8 + g)
                hn[f, t, at, :] = jnp.where(todd, b, a)
                hs[f, t, at, :] = jnp.where(todd, a, b)
            hn[f, 2, at, :] = edge_unpack(on, g)
            hs[f, 2, at, :] = edge_unpack(os, g)


def stencil(y, coef, north_row, south_row, row, tiles=3):
    e, w = east_of(y), west_of(y)
    out = []
    for t in range(tiles):
        n = jnp.where(row == ROWS - 1, north_row[t], pltpu.roll(y[t], ROWS - 1, 0))
        s = jnp.where(row == 0, south_row[t], pltpu.roll(y[t], 1, 0))
        ce, cw, cn, cs, cc = coef[t]
        out.append(cc * y[t] + ce * e[t] + cw * w[t] + cn * n + cs * s)
    return out


def step(first, v0, ids, fld, fe, cfi, trm, tre, ya, yb, *refs):
    if first:
        wloc, cf, sol, oa, ob, fo, hn, hs = refs
    else:
        sol, oa, ob, fo, hn, hs = refs
    row = iota((ROWS, LANES), 0)
    take_first_edges(ids, ya, yb, hn, hs, first)

    def get(v, at):
        return [fld[v0 + v, 0, at, :], fld[v0 + v, 1, at, :], fe[v0 + v, at, :]]

    north_in = jnp.where(ids[1] < 31, 1.0, 0.0).astype(F32)
    south_in = jnp.where(ids[1] > 0, 1.0, 0.0).astype(F32)

    def apply(i, carry):
        for k in range(UNROLL_S):
            level = UNROLL_S * i + k
            at = rows_of(level)
            ones = [pl.ds(level, 1), pl.ds(level, 1), pl.ds(slot_of(level), 1)]
            coef = []
            for t in range(3):
                ce, cw, cn, cs, cc = (cfi[c, t, at, :] for c in range(5))
                if first:
                    cn = jnp.where(row == ROWS - 1, cn * (hn[2, t, ones[t], :] * north_in), cn)
                    cs = jnp.where(row == 0, cs * (hs[2, t, ones[t], :] * south_in), cs)
                    cc = cc - cn - cs
                    cf[2, t, at, :] = cn
                    cf[3, t, at, :] = cs
                    cf[4, t, at, :] = cc
                coef.append((ce, cw, cn, cs, cc))
            for v in range(2):
                n = [hn[v, t, ones[t], :] for t in range(3)]
                s = [hs[v, t, ones[t], :] for t in range(3)]
                adj = stencil(get(v, at), coef, n, s, row)
                for t in range(3):
                    sol[v, t, at, :] = adj[t]
        return carry

    lax.fori_loop(0, LEV // UNROLL_S, apply, 0)

    def put(v, t, at, x):
        sol[v, t, at, :] = x

    def load(v, t, at):
        return sol[v, t, at, :]

    top = eliminate(
        load,
        put,
        load,
        lambda k, t, at: tre[k, 0, at, :] if t == 2 else trm[k, t, at, :],
        [(v, t) for v in range(2) for t in range(3)],
    )[0]
    for v in range(2):
        y = get(v, pl.ds(0, ROWS))
        for t in range(3):
            fo[v, t] = y[t] + top[3 * v + t]
    todd = lax.rem(ids[1], 2) == 1
    put_edges(todd, lambda f, t, g: edge_rows(sol.at[f, t], g), 2, oa, ob)
    if first:
        for c in range(2):
            for t in range(3):
                n = wloc[c, t, 8:16, :]
                s = wloc[c, t, 0:8, :]
                at = pl.ds(ROWS_2 + 8 * (3 * c + t), 8)
                oa[at, :] = jnp.where(todd, s, n)
                ob[at, :] = jnp.where(todd, n, s)


def last_stencil(v0, l0, nl, extra, carried, grads, *refs):
    ids, sol, cf, ya, yb = refs[:5]
    refs = refs[5:]
    fos = refs[:extra]
    refs = refs[extra:]
    if grads and carried:
        ua, ub = refs[:2]
        refs = refs[2:]
    if not grads:
        refs = refs[1:]
    if l0 or v0:
        refs = refs[1:]
    if grads:
        adj_out, g, ga, gb, hn, hs, en, es, buf, sem = refs
    else:
        adj_out, hn, hs, buf, sem = refs
    row = iota((ROWS, LANES), 0)
    low_half = iota((8, LANES), 0) < 4
    todd = lax.rem(ids[1], 2) == 1

    def load(block):
        if not grads:
            return ya[carried + block], yb[carried + block]
        at = pl.ds(8 * block, 8)
        return ya[at, :], yb[at, :]

    take_edges(ids, load, hn, hs, (l0 // 8, (l0 + nl) // 8))

    def edges(u, ts, ss):
        for t in range(3):
            a, b = ts[t], ss[t]
            n = jnp.where(low_half, pltpu.roll(a[8:16], 4, 0), b[8:16])
            s = jnp.where(low_half, a[0:8], pltpu.roll(b[0:8], 4, 0))
            if t < 2:
                ga[2 * u + t] = jnp.where(todd, s, n)
                gb[2 * u + t] = jnp.where(todd, n, s)
            else:
                en[u] = n
                es[u] = s

    def body(i, carry):
        for k in range(UNROLL_L):
            u = UNROLL_L * i + k
            level = l0 + u
            at = rows_of(level)
            one = pl.ds(level, 1)
            coef = [tuple(cf[c, t, at, :] for c in range(5)) for t in range(3)]
            both = []
            for v in range(2):
                y = [sol[v, t, at, :] for t in range(3)]
                n = [hn[v, t, one, :] for t in range(3)]
                s = [hs[v, t, one, :] for t in range(3)]
                x = stencil(y, coef, n, s, row, 3 if grads else 2)
                buf[u, v, :, 0:LANES] = x[0]
                buf[u, v, :, LANES : 2 * LANES] = x[1]
                if grads:
                    for t in range(3):
                        g[u, v, t] = x[t]
                both.append(x)
            if grads:
                edges(u, *both)
        return carry

    lax.fori_loop(0, nl // UNROLL_L, body, 0)
    copy = pltpu.make_async_copy(buf, adj_out.at[pl.ds(l0, nl), pl.ds(v0, 2)], sem)
    copy.start()
    if grads:
        for i, fo in enumerate(fos):
            pair = [[fo[v, t] for t in range(3)] for v in range(2)]
            for v in range(2):
                for t in range(3):
                    g[nl + i, v, t] = pair[v][t]
            edges(nl + i, *pair)
        units = nl + extra
        per = -(-units // 8)
        lane = iota((8, LANES), 1)
        for i in range(per):
            pn = ps = jnp.zeros((8, LANES), F32)
            for j in range(8):
                u = j * per + i
                if u < units:
                    mine = (lane >= 16 * j) & (lane < 16 * j + 16)
                    pn = jnp.where(mine, pltpu.roll(en[u], (16 * j + 8) % LANES, 1), pn)
                    ps = jnp.where(mine, pltpu.roll(es[u], (16 * j + 8) % LANES, 1), ps)
            ga[2 * units + i] = jnp.where(todd, ps, pn)
            gb[2 * units + i] = jnp.where(todd, pn, ps)
        if carried:
            for i in range(BLOCKS_2):
                ga[2 * units + per + i] = ua[pl.ds(8 * i, 8), :]
                gb[2 * units + per + i] = ub[pl.ds(8 * i, 8), :]
    copy.wait()


def smooth(units, u0, u1, ids, g, ga, gb, wloc, ya, yb, after, z0, z1, z2, z3, w5, hn, hs):
    del after
    zs = (z0, z1, z2, z3)
    face, tile = ids[0], ids[1]
    todd = lax.rem(tile, 2) == 1
    has_n, has_s = tile < 31, tile > 0
    sub = iota((8, LANES), 0)
    lane = iota((8, LANES), 1)
    low_half = sub < 4

    def stack3(lo, m0, m1, hi):
        r0, r1 = pltpu.roll(m0, 4, 0), pltpu.roll(m1, 4, 0)
        return [
            jnp.where(low_half, lo, r0),
            jnp.where(low_half, r0, r1),
            jnp.where(low_half, r1, hi),
        ]

    def north_of(k3):
        turned = [pltpu.roll(x, 7, 0) for x in k3]
        return [
            jnp.where(sub == 7, turned[1], turned[0]),
            jnp.where(sub == 7, turned[2], turned[1]),
            turned[2],
        ]

    def south_of(k3, below=None):
        turned = [pltpu.roll(x, 1, 0) for x in k3]
        return [
            turned[0] if below is None else jnp.where(sub == 0, below, turned[0]),
            jnp.where(sub == 0, turned[0], turned[1]),
            jnp.where(sub == 0, turned[1], turned[2]),
        ]

    we, wn, below = [], [], []
    for c, dest in ((0, we), (1, wn)):
        for t in range(3):
            at = pl.ds(ROWS_2 + 8 * (3 * c + t), 8)
            a, b = ya[at, :], yb[at, :]
            hi = jnp.where(has_n, jnp.where(todd, b, a), 0.0)
            lo = jnp.where(has_s, jnp.where(todd, a, b), 0.0)
            if c == 1:
                below.append(pltpu.roll(lo, 5, 0))
            dest.append(
                stack3(pltpu.roll(lo, 4, 0), wloc[c, t, 0:8, :], wloc[c, t, 8:16, :], pltpu.roll(hi, 4, 0))
            )
    for k in range(3):
        cw3 = west_of([we[t][k] for t in range(3)])
        for t in range(3):
            ok = jnp.ones((8, LANES), F32)
            if k == 0:
                ok = jnp.where(low_half & (tile == 0), 0.0, ok)
            if k == 2:
                ok = jnp.where((~low_half) & (tile == 31), 0.0, ok)
            if t == 2:
                inside = ((lane < 64) & (face < 3)) | ((lane >= 64) & (face > 0))
                ok = jnp.where(inside, ok, 0.0)
            ce = we[t][k] * ok
            cw = cw3[t] * ok
            cn = wn[t][k] * ok
            cs = south_of(wn[t], below[t])[k] * ok
            w5[0, t, k] = ce
            w5[1, t, k] = cw
            w5[2, t, k] = cn
            w5[3, t, k] = cs
            w5[4, t, k] = 1.0 - ce - cw - cn - cs

    per = -(-units // 8)
    for u in range(u0, u1):
        j, i = divmod(u, per)
        a, b = ga[2 * units + i], gb[2 * units + i]
        n = edge_unpack(jnp.where(todd, b, a), j)
        s = edge_unpack(jnp.where(todd, a, b), j)
        u -= u0
        hn[u] = jnp.where(has_n, n, 0.0)
        hs[u] = jnp.where(has_s, s, 0.0)

    bit0 = lax.rem(face, 2) == 1
    bit1 = face >= 2

    def body(i, carry):
        fields = []
        for u in [UNROLL_M * i + k for k in range(UNROLL_M)]:
            hi, lo = [], []
            for t in range(2):
                a, b = ga[2 * (u0 + u) + t], gb[2 * (u0 + u) + t]
                hi.append(jnp.where(has_n, jnp.where(todd, b, a), 0.0))
                lo.append(jnp.where(has_s, jnp.where(todd, a, b), 0.0))
            hi.append(hn[u])
            lo.append(hs[u])
            for v in range(2):
                x = []
                for t in range(3):
                    m = g[u0 + u, v, t]
                    top = pltpu.roll(hi[t], 4, 0) if v == 0 else hi[t]
                    bottom = lo[t] if v == 0 else pltpu.roll(lo[t], 4, 0)
                    x.append(stack3(bottom, m[0:8], m[8:16], top))
                fields.append(x)
        for _ in range(4):
            coefs = [[[w5[c, t, k] for c in range(5)] for k in range(3)] for t in range(3)]
            swept = []
            for x in fields:
                ns = [north_of(x[t]) for t in range(3)]
                ss = [south_of(x[t]) for t in range(3)]
                new = [[], [], []]
                for k in range(3):
                    at_k = [x[t][k] for t in range(3)]
                    e, w = east_of(at_k), west_of(at_k)
                    for t in range(3):
                        ce, cw, cn, cs, cc = coefs[t][k]
                        new[t].append(
                            cc * x[t][k] + ce * e[t] + cw * w[t] + cn * ns[t][k] + cs * ss[t][k]
                        )
                swept.append(new)
            fields = swept
        for c, x in enumerate(fields):
            u = UNROLL_M * i + c // 2
            for t in range(2):
                p = [pltpu.roll(x[t][0], 4, 0), x[t][1], pltpu.roll(x[t][1], 4, 0), x[t][2]]
                p = [jnp.where(bit0, p[d ^ 1], p[d]) for d in range(4)]
                p = [jnp.where(bit1, p[d ^ 2], p[d]) for d in range(4)]
                for k in range(4):
                    zs[k][2 * u + c % 2, :, t * LANES : (t + 1) * LANES] = p[k][0:4]
        return carry

    lax.fori_loop(0, (u1 - u0) // UNROLL_M, body, 0)


def gather_rows(first, size, ids, z0, z1, z2, z3, *refs):
    out, sem = refs[-2:]
    copies = []
    for k, z in enumerate((z0, z1, z2, z3)):
        cols = pl.multiple_of(jnp.bitwise_xor(ids[0], k) * 256, 256)
        dst = out.at[pl.ds(first, size), :, pl.ds(cols, 256)]
        copies.append(pltpu.make_async_copy(z, dst, sem.at[k]))
    for copy in copies:
        copy.start()
    for copy in copies:
        copy.wait()


def on_device(adjoint_seed, face_flow, vert_diff, wet_mask, smooth_weights):
    ids = jnp.stack([lax.axis_index("face"), lax.axis_index("tile")]).astype(jnp.int32)
    tiles = lax.axis_size("tile")
    pair_a = [(i, i ^ 1) for i in range(tiles)]
    pair_b = [(0, 0), (tiles - 1, tiles - 1)]
    for i in range(1, tiles - 1, 2):
        pair_b += [(i, i + 1), (i + 1, i)]
    side_a = [(0, 1), (1, 0), (2, 3), (3, 2)]
    side_b = [(0, 0), (1, 2), (2, 1), (3, 3)]
    hbm, any_space = pltpu.HBM, pl.ANY

    def across(a, b):
        return lax.ppermute(a, "tile", pair_a), lax.ppermute(b, "tile", pair_b)

    def to_face(x, k):
        return lax.ppermute(x, "face", [(i, i ^ k) for i in range(4)])

    edge = (ROWS, LANES)
    packed = (HALF * ROWS, LANES)
    fld, tri, pxa, pxb = call(
        first_solve,
        [((8, 2, FLAT, LANES), VM), ((3, 2, FLAT, LANES), VM), (packed, VM), (packed, VM)],
        [
            VM((2, LEV) + edge, jnp.int32),
            VM(packed, F32),
            VM(packed, F32),
            pltpu.SemaphoreType.DMA((16,)),
        ],
        limit=5,
        ins=[None] + [hbm] * 4,
        name="first_solve",
    )(ids, adjoint_seed, face_flow, vert_diff, wet_mask)
    xa = lax.ppermute(pxa, "face", side_a)
    xb = lax.ppermute(pxb, "face", side_b)
    rows_1 = ((ROWS_1, LANES), VM)
    ya, yb = call(main_edges, [rows_1, rows_1], limit=4, name="main_edges")(ids, fld)
    ya, yb = call(
        outer_edges, [rows_1, rows_1], limit=4, alias={3: 0, 4: 1}, name="outer_edges"
    )(ids, xa, xb, ya, yb)
    later, _ = lax.optimization_barrier((smooth_weights, ya))
    ya, yb = across(ya, yb)
    fe, cf, tre = call(
        coefficients,
        [((8, FLAT, LANES), VM), ((5, 3, FLAT, LANES), VM), ((3, 1, FLAT, LANES), VM)],
        limit=4,
        name="coefficients",
    )(ids, fld, xa, xb)
    weights = [later] + [to_face(later, k) for k in (1, 2, 3)]
    (wloc,) = call(
        local_weights,
        [((2, 3) + edge, VM)],
        [VM((4, 2, 4, 1024), F32)],
        limit=4,
        name="local_weights",
    )(ids, *weights)
    halo = VM((3, 3, LEV, LANES), F32)
    sol_shape = ((2, 3, FLAT, LANES), VM)
    fo_shape = ((2, 3) + edge, VM)
    rows_w = ((ROWS_2 + 48, LANES), VM)
    rows_2 = ((ROWS_2, LANES), VM)
    cf, sol_t, ta, tb, fo_t = call(
        functools.partial(step, True, 0),
        [((5, 3, FLAT, LANES), VM), sol_shape, rows_w, rows_w, fo_shape],
        [halo, halo],
        limit=4,
        alias={3: 0},
        name="step_ts",
    )(ids, fld, fe, cf, tri, tre, ya, yb, wloc)
    ta, tb = across(ta, tb)
    sol_u, ua, ub, fo_u = call(
        functools.partial(step, False, 2),
        [sol_shape, rows_2, rows_2, fo_shape],
        [halo, halo],
        limit=4,
        name="step_uv",
    )(ids, fld, fe, cf, tri, tre, ya, yb)

    adj_shape = adjoint_seed.shape
    adj = None
    chunks = []
    for l0, l1 in CHUNKS:
        nl = l1 - l0
        fos = [fo_t, fo_u] if l1 == LEV else []
        units = nl + len(fos)
        per = -(-units // 8)
        args = [ids, sol_t, cf, ta, tb] + fos
        blocks = 2 * units + per
        carried = 0
        if l0 == 0:
            args += [ua, ub]
            carried = blocks
            blocks += BLOCKS_2
        spaces = [None] + [VM] * (len(args) - 1)
        alias = {}
        if adj is not None:
            alias = {len(args): 0}
            args.append(adj)
            spaces.append(any_space)
        adj, g, ga, gb = call(
            functools.partial(last_stencil, 0, l0, nl, len(fos), carried, True),
            [
                (adj_shape, any_space),
                ((units, 2, 3) + edge, VM),
                ((blocks, 8, LANES), VM),
                ((blocks, 8, LANES), VM),
            ],
            [
                halo,
                halo,
                VM((units, 8, LANES), F32),
                VM((units, 8, LANES), F32),
                VM((nl, 2, ROWS, 256), F32),
                pltpu.SemaphoreType.DMA,
            ],
            limit=6,
            alias=alias,
            ins=spaces,
            name="last_ts_%d" % l0,
        )(*args)
        ga, gb = across(ga, gb)
        chunks.append((units, g, ga, gb))
        if l0 == 0:
            uv_rows = (carried, ga, gb)

    controls = None
    after = chunks[-1][1]
    sent = []
    first = 0

    def gather(controls, first, size, parts):
        args = [ids] + parts
        alias = {}
        if controls is not None:
            alias = {len(args): 0}
            args.append(controls)
        (controls,) = call(
            functools.partial(gather_rows, first, size),
            [((2 * (LEV + 2), 4, 1024), any_space)],
            [pltpu.SemaphoreType.DMA((4,))],
            ins=[None] + [any_space] * (len(args) - 1),
            limit=4,
            alias=alias,
            name="gather_%d" % first,
        )(*args)
        return controls

    for c, u0, u1 in PIECES:
        units, g, ga, gb = chunks[c]
        n = u1 - u0
        zs = call(
            functools.partial(smooth, units, u0, u1),
            [((2 * n, 4, 256), VM)] * 4,
            [
                VM((5, 3, 3, 8, LANES), F32),
                VM((n, 8, LANES), F32),
                VM((n, 8, LANES), F32),
            ],
            ins=[None] + [VM] * 6 + [any_space],
            limit=4,
            name="smooth_%d_%d" % (c, u0),
        )(ids, g, ga, gb, wloc, ta, tb, after)
        after = zs[0]
        sent.append((first, 2 * n, [zs[0]] + [to_face(zs[k], k) for k in (1, 2, 3)]))
        first += 2 * n
    carried, ga, gb = uv_rows
    (adj,) = call(
        functools.partial(last_stencil, 2, 0, LEV, 0, carried, False),
        [(adj_shape, any_space)],
        [halo, halo, VM((LEV, 2, ROWS, 256), F32), pltpu.SemaphoreType.DMA],
        limit=6,
        alias={6: 0},
        ins=[None] + [VM] * 4 + [any_space] * 2,
        name="last_uv",
    )(ids, sol_u, cf, ga, gb, after, adj)
    for start, size, parts in sent:
        controls = gather(controls, start, size, parts)
    return adj, controls


def solution(mesh):
    placed = (
        P(None, None, "tile", "face"),
        P(None, None, "tile", "face"),
        P(None, "tile", "face"),
        P(None, "tile", "face"),
        P(None, ("tile", "face"), None),
    )
    return jax.shard_map(
        on_device,
        mesh=mesh,
        in_specs=placed,
        out_specs=(P(None, None, "tile", "face"), P(None, ("tile", "face"), None)),
        check_vma=False,
    )
```

time: 166 us -> 114 us (0.69)
  Pallas kernels: 88.4 us -> 63.8 us
  starting transfers between devices: 55.9 us -> 42.9 us
  waiting for transfers between devices: 13.4 us -> 4.64 us
  local copies, waits for them, and re-layouts: 6.23 us -> 0.01 us
    pallas_call x13 -> x16, Pallas kernels: 88.4 us -> 63.8 us  [run(): pl.pallas_call(kernel, out_shape=[jax.ShapeDtypeStruct(s, F32) for s, _ i...]
    ppermute x14 -> x8, starting transfers between devices: 40.8 us -> 24 us  [across(): return (lax.ppermute(a, 'tile', pair_a), lax.ppermute(b, 'tile', pair_b))]
    ppermute x12, waiting for transfers between devices: 12.1 us -> 0.91 us  [to_face(): return lax.ppermute(x, 'face', [(i, i ^ k) for i in range(4)])]
    unnamed x10 -> x2, local copies, waits for them, and re-layouts: 6.23 us -> 0.01 us
    ppermute x12, starting transfers between devices: 13.7 us -> 17.5 us  [to_face(): return lax.ppermute(x, 'face', [(i, i ^ k) for i in range(4)])]
    ppermute x14 -> x8, waiting for transfers between devices: 1.25 us -> 3.73 us  [across(): return (lax.ppermute(a, 'tile', pair_a), lax.ppermute(b, 'tile', pair_b))]
  transfers between devices with their start and end apart: 28 -> 22, of which waited for: 5 -> 3; matrix products, arithmetic and copies ran while one was open for 0% -> 0% of each run, Pallas kernels for 37% -> 36%
where the time goes in v1:
time: 114 us; the launch traced here: 112 us
  Pallas kernels  63.8 us (56%)
  starting transfers between devices  42.9 us (38%)
  waiting for transfers between devices  4.64 us (4%)
    pallas_call x16, Pallas kernels, run(): pl.pallas_call(kernel, out_shape=[jax.ShapeDtypeStruct(s, F32) for s, _ i...  63.8 us
    ppermute x8, starting transfers between devices, across(): return (lax.ppermute(a, 'tile', pair_a), lax.ppermute(b, 'tile', pair_b))  24 us
    ppermute x12, starting transfers between devices, to_face(): return lax.ppermute(x, 'face', [(i, i ^ k) for i in range(4)])  17.5 us
    ppermute x8, waiting for transfers between devices, across(): return (lax.ppermute(a, 'tile', pair_a), lax.ppermute(b, 'tile', pair_b))  3.73 us
  transfers between devices with their start and end apart: 22, of which 3 were waited for; matrix products, arithmetic and copies ran while one was open for 0% of the time, Pallas kernels for 36%

profile of v1, /device:TPU:97, one launch (start us, length us, event | category | flops | bytes accessed | tf_op | source)
XLA Modules:
  0.0 112.4 jit_solution(5857326281173705682)
XLA Ops:
  0.7 13.2 %first_solve.1 = (f32[8,2,1024,128]{3,2,1,0:T(8,128)S(1)}, f32[3,2,1024,128]{3,2,1,0:T(8,128)S(1)}, f32[512,128]{1,0:T(8,128)S(1)}, f32[512,128]{1,0:T(8,128)S(1)}) custom-call(s32[2]{0:T(128)S(1)} %pad_add_fusion.ids.refs_0_, f32[64,4,16,256]{3,2,1,0:T(8,128)} %seed.1, f32[2,64,16,256]{3,2,1,0:T(8,128)} %flow.1, f32[64,16,256]{2,1,0:T(8,128)} %vd.1, ...), custom_call_target="tpu_custom_call" | custom-call | tf_op jit(solution)/shard_map/first_solve/pallas_call | solution.py:57
  16.7 6.8 %collective-permute-start.3 = (f32[704,128]{1,0:T(8,128)S(1)}, f32[704,128]{1,0:T(8,128)S(1)}, u32[]{:S(2)}, u32[]{:S(2)}) collective-permute-start(f32[704,128]{1,0:T(8,128)S(1)} %get-tuple-element.53), channel_id=1, source_target_pairs={{0,0},{124,124},{4,8},{8,4},{12,16},{16,12},{20,24},{24,20},{28,32... | collective-permute-start | bytes 1081352 | tf_op jit(solution)/shard_map/ppermute | solution.py:778
  23.8 7.8 %collective-permute-start.5 = (f32[2,4,1024]{2,1,0:T(4,128)S(1)}, f32[2,4,1024]{2,1,0:T(4,128)S(1)}, u32[]{:S(2)}, u32[]{:S(2)}) collective-permute-start(f32[2,4,1024]{2,1,0:T(4,128)S(1)} %copy-done), channel_id=1, source_target_pairs={{0,2},{1,3},{2,0},{3,1},{4,6},{5,7},{6,4},{7,5},{8,10},{9,11},{10,... | collective-permute-start | bytes 98312 | tf_op jit(solution)/shard_map/ppermute | solution.py:781
  31.6 6.3 %coefficients.1 = (f32[8,1024,128]{2,1,0:T(8,128)S(1)}, f32[5,3,1024,128]{3,2,1,0:T(8,128)S(1)}, f32[3,1,1024,128]{3,2,1,0:T(8,128)S(1)}) custom-call(s32[2]{0:T(128)S(1)} %pad_add_fusion.ids.refs_0_, f32[8,2,1024,128]{3,2,1,0:T(8,128)S(1)} %get-tuple-element.43.fld, f32[512,128]{1,0:T(8,128)S(1)} %collective-permute-done.xa, ...), custom_call_target="tpu_custom_call" | custom-call | tf_op jit(solution)/shard_map/coefficients/pallas_call | solution.py:57
  38.6 5.5 %step_ts.1 = (f32[5,3,1024,128]{3,2,1,0:T(8,128)S(1)}, f32[2,3,1024,128]{3,2,1,0:T(8,128)S(1)}, f32[320,128]{1,0:T(8,128)S(1)}, f32[320,128]{1,0:T(8,128)S(1)}, f32[2,3,16,128]{3,2,1,0:T(8,128)S(1)}) custom-call(s32[2]{0:T(128)S(1)} %pad_add_fusion.ids.refs_0_, f32[8,2,1024,128]{3,2,1,0:T(8,128)S(1)} %get-tuple-element.43.fld, ...), custom_call_target="tpu_custom_call", output_to_operand_aliasing={{0}: (3, {})} | custom-call | tf_op jit(solution)/shard_map/step_ts/pallas_call | solution.py:57
  44.1 1.7 %collective-permute-start.7 = (f32[320,128]{1,0:T(8,128)S(1)}, f32[320,128]{1,0:T(8,128)S(1)}, u32[]{:S(2)}, u32[]{:S(2)}) collective-permute-start(f32[320,128]{1,0:T(8,128)S(1)} %get-tuple-element.58), channel_id=1, source_target_pairs={{0,4},{4,0},{8,12},{12,8},{16,20},{20,16},{24,28},{28,24},{32,36},... | collective-permute-start | bytes 491528 | tf_op jit(solution)/shard_map/ppermute | solution.py:778
  45.8 4.2 %collective-permute-start.8 = (f32[320,128]{1,0:T(8,128)S(1)}, f32[320,128]{1,0:T(8,128)S(1)}, u32[]{:S(2)}, u32[]{:S(2)}) collective-permute-start(f32[320,128]{1,0:T(8,128)S(1)} %get-tuple-element.59), channel_id=1, source_target_pairs={{0,0},{124,124},{4,8},{8,4},{12,16},{16,12},{20,24},{24,20},{28,32... | collective-permute-start | bytes 491528 | tf_op jit(solution)/shard_map/ppermute | solution.py:778
  50.0 5.3 %step_uv.1 = (f32[2,3,1024,128]{3,2,1,0:T(8,128)S(1)}, f32[272,128]{1,0:T(8,128)S(1)}, f32[272,128]{1,0:T(8,128)S(1)}, f32[2,3,16,128]{3,2,1,0:T(8,128)S(1)}) custom-call(s32[2]{0:T(128)S(1)} %pad_add_fusion.ids.refs_0_, f32[8,2,1024,128]{3,2,1,0:T(8,128)S(1)} %get-tuple-element.43.fld, f32[8,1024,128]{2,1,0:T(8,128)S(1)} %get-tuple-element.46.fe, ...), custom_call_target="tpu_custom_call" | custom-call | tf_op jit(solution)/shard_map/step_uv/pallas_call | solution.py:57
  55.3 3.1 %collective-permute-done.8.refs_4_.yb = f32[320,128]{1,0:T(8,128)S(1)} collective-permute-done((f32[320,128]{1,0:T(8,128)S(1)}, f32[320,128]{1,0:T(8,128)S(1)}, u32[]{:S(2)}, u32[]{:S(2)}) %collective-permute-start.8) | collective-permute-done | bytes 163872 | tf_op jit(solution)/shard_map/ppermute | solution.py:778
  58.3 2.8 %last_ts_0.1 = (f32[64,4,16,256]{3,2,1,0:T(8,128)}, f32[24,2,3,16,128]{4,3,2,1,0:T(8,128)S(1)}, f32[85,8,128]{2,1,0:T(8,128)S(1)}, f32[85,8,128]{2,1,0:T(8,128)S(1)}) custom-call(s32[2]{0:T(128)S(1)} %pad_add_fusion.ids.refs_0_, f32[2,3,1024,128]{3,2,1,0:T(8,128)S(1)} %get-tuple-element.57.refs_1_, f32[5,3,1024,128]{3,2,1,0:T(8,128)S(1)} %get-tuple-element.55.cfi.refs_2_, ...), custom_call_target="tpu_custom_call" | custom-call | tf_op jit(solution)/shard_map/last_ts_0/pallas_call | solution.py:57
  61.3 4.2 %collective-permute-start.10 = (f32[85,8,128]{2,1,0:T(8,128)S(1)}, f32[85,8,128]{2,1,0:T(8,128)S(1)}, u32[]{:S(2)}, u32[]{:S(2)}) collective-permute-start(f32[85,8,128]{2,1,0:T(8,128)S(1)} %get-tuple-element.63), channel_id=1, source_target_pairs={{0,0},{124,124},{4,8},{8,4},{12,16},{16,12},{20,24},{24,20},{28,32... | collective-permute-start | bytes 1044488 | tf_op jit(solution)/shard_map/ppermute | solution.py:778
  65.5 3.8 %last_ts_24.1 = (f32[64,4,16,256]{3,2,1,0:T(8,128)}, f32[42,2,3,16,128]{4,3,2,1,0:T(8,128)S(1)}, f32[90,8,128]{2,1,0:T(8,128)S(1)}, f32[90,8,128]{2,1,0:T(8,128)S(1)}) custom-call(s32[2]{0:T(128)S(1)} %pad_add_fusion.ids.refs_0_, f32[2,3,1024,128]{3,2,1,0:T(8,128)S(1)} %get-tuple-element.57.refs_1_, ...), custom_call_target="tpu_custom_call", output_to_operand_aliasing={{0}: (7, {})} | custom-call | tf_op jit(solution)/shard_map/last_ts_24/pallas_call | solution.py:57
  69.4 6.8 %collective-permute-start.12 = (f32[90,8,128]{2,1,0:T(8,128)S(1)}, f32[90,8,128]{2,1,0:T(8,128)S(1)}, u32[]{:S(2)}, u32[]{:S(2)}) collective-permute-start(f32[90,8,128]{2,1,0:T(8,128)S(1)} %get-tuple-element.69), channel_id=1, source_target_pairs={{0,0},{124,124},{4,8},{8,4},{12,16},{16,12},{20,24},{24,20},{28,32... | collective-permute-start | bytes 1105928 | tf_op jit(solution)/shard_map/ppermute | solution.py:778
  76.9 5.7 %smooth_0_0.1 = (f32[48,4,256]{2,1,0:T(4,128)S(1)}, f32[48,4,256]{2,1,0:T(4,128)S(1)}, f32[48,4,256]{2,1,0:T(4,128)S(1)}, f32[48,4,256]{2,1,0:T(4,128)S(1)}) custom-call(s32[2]{0:T(128)S(1)} %pad_add_fusion.ids.refs_0_, f32[24,2,3,16,128]{4,3,2,1,0:T(8,128)S(1)} %get-tuple-element.70.g, f32[85,8,128]{2,1,0:T(8,128)S(1)} %collective-permute-done.9.ga.refs_3_, ...), custom_call_target="tpu_custom_call" | custom-call | tf_op jit(solution)/shard_map/smooth_0_0/pallas_call | solution.py:57
  82.5 2.8 %collective-permute-start.19 = (f32[48,4,256]{2,1,0:T(4,128)S(1)}, f32[48,4,256]{2,1,0:T(4,128)S(1)}, u32[]{:S(2)}, u32[]{:S(2)}) collective-permute-start(f32[48,4,256]{2,1,0:T(4,128)S(1)} %get-tuple-element.81), channel_id=1, source_target_pairs={{0,1},{1,0},{2,3},{3,2},{4,5},{5,4},{6,7},{7,6},{8,9},{9,8},{10,11... | collective-permute-start | bytes 589832 | tf_op jit(solution)/shard_map/ppermute | solution.py:781
  85.3 1.0 collective-permute-start.20
  87.1 5.2 %smooth_1_0.1 = (f32[44,4,256]{2,1,0:T(4,128)S(1)}, f32[44,4,256]{2,1,0:T(4,128)S(1)}, f32[44,4,256]{2,1,0:T(4,128)S(1)}, f32[44,4,256]{2,1,0:T(4,128)S(1)}) custom-call(s32[2]{0:T(128)S(1)} %pad_add_fusion.ids.refs_0_, f32[42,2,3,16,128]{4,3,2,1,0:T(8,128)S(1)} %get-tuple-element.67.after.g, f32[90,8,128]{2,1,0:T(8,128)S(1)} %collective-permute-done.11.ga, ...), custom_call_target="tpu_custom_call" | custom-call | tf_op jit(solution)/shard_map/smooth_1_0/pallas_call | solution.py:57
  92.3 1.1 %collective-permute-start.16 = (f32[44,4,256]{2,1,0:T(4,128)S(1)}, f32[44,4,256]{2,1,0:T(4,128)S(1)}, u32[]{:S(2)}, u32[]{:S(2)}) collective-permute-start(f32[44,4,256]{2,1,0:T(4,128)S(1)} %get-tuple-element.78), channel_id=1, source_target_pairs={{0,1},{1,0},{2,3},{3,2},{4,5},{5,4},{6,7},{7,6},{8,9},{9,8},{10,11... | collective-permute-start | bytes 540680 | tf_op jit(solution)/shard_map/ppermute | solution.py:781
  95.2 4.8 %smooth_1_22.1 = (f32[40,4,256]{2,1,0:T(4,128)S(1)}, f32[40,4,256]{2,1,0:T(4,128)S(1)}, f32[40,4,256]{2,1,0:T(4,128)S(1)}, f32[40,4,256]{2,1,0:T(4,128)S(1)}) custom-call(s32[2]{0:T(128)S(1)} %pad_add_fusion.ids.refs_0_, f32[42,2,3,16,128]{4,3,2,1,0:T(8,128)S(1)} %get-tuple-element.67.after.g, f32[90,8,128]{2,1,0:T(8,128)S(1)} %collective-permute-done.11.ga, ...), custom_call_target="tpu_custom_call" | custom-call | tf_op jit(solution)/shard_map/smooth_1_22/pallas_call | solution.py:57
  101.1 1.1 collective-permute-start.15
  102.2 4.9 %last_uv.1 = f32[64,4,16,256]{3,2,1,0:T(8,128)} custom-call(s32[2]{0:T(128)S(1)} %pad_add_fusion.ids.refs_0_, f32[2,3,1024,128]{3,2,1,0:T(8,128)S(1)} %get-tuple-element.56.refs_1_, f32[5,3,1024,128]{3,2,1,0:T(8,128)S(1)} %get-tuple-element.55.cfi.refs_2_, f32[85,8,128]{2,1,0:T(8,128)S(1)} %collective-permute-done.9.ga.refs_3_, ...), custom_call_target="tpu_custom_call", output_to_operand_aliasing={{}: (6, {})} | custom-call | tf_op jit(solution)/shard_map/last_uv/pallas_call | solution.py:57
  107.1 1.5 %gather_0.1.refs_0_ = f32[132,4,1024]{2,1,0:T(4,128)} custom-call(s32[2]{0:T(128)S(1)} %pad_add_fusion.ids.refs_0_, f32[48,4,256]{2,1,0:T(4,128)S(1)} %get-tuple-element.71.after.z0, f32[48,4,256]{2,1,0:T(4,128)S(1)} %collective-permute-done.19.z1, f32[48,4,256]{2,1,0:T(4,128)S(1)} %collective-permute-done.20.z2, f32[48,4,256]{2,1,0:T(4,128)S(1)} %collective-permute-done.21.z3), custom_call_target="tpu_custom_call" | custom-call | tf_op jit(solution)/shard_map/gather_0/pallas_call | solution.py:57
  108.6 1.4 %gather_48.1.refs_0_ = f32[132,4,1024]{2,1,0:T(4,128)} custom-call(s32[2]{0:T(128)S(1)} %pad_add_fusion.ids.refs_0_, f32[44,4,256]{2,1,0:T(4,128)S(1)} %get-tuple-element.72.after.z0, f32[44,4,256]{2,1,0:T(4,128)S(1)} %collective-permute-done.16.z1, f32[44,4,256]{2,1,0:T(4,128)S(1)} %collective-permute-done.17.z2, ...), custom_call_target="tpu_custom_call", output_to_operand_aliasing={{}: (5, {})} | custom-call | tf_op jit(solution)/shard_map/gather_48/pallas_call | solution.py:57
  111.0 1.4 %gather_92.1 = f32[132,4,1024]{2,1,0:T(4,128)} custom-call(s32[2]{0:T(128)S(1)} %pad_add_fusion.ids.refs_0_, f32[40,4,256]{2,1,0:T(4,128)S(1)} %get-tuple-element.73.refs_5_.z0, f32[40,4,256]{2,1,0:T(4,128)S(1)} %collective-permute-done.13.z1, f32[40,4,256]{2,1,0:T(4,128)S(1)} %collective-permute-done.14.z2, ...), custom_call_target="tpu_custom_call", output_to_operand_aliasing={{}: (5, {})} | custom-call | tf_op jit(solution)/shard_map/gather_92/pallas_call | solution.py:57
  (39 shorter events, 8.9 us)
Async XLA Ops:
  13.9 2.2 %collective-permute-start = (f32[512,128]{1,0:T(8,128)S(1)}, f32[512,128]{1,0:T(8,128)S(1)}, u32[]{:S(2)}, u32[]{:S(2)}) collective-permute-start(f32[512,128]{1,0:T(8,128)S(1)} %get-tuple-element.44), channel_id=1, source_target_pairs={{0,1},{1,0},{2,3},{3,2},{4,5},{5,4},{6,7},{7,6},{8,9},{9,8},{10,11... | collective-permute-start | bytes 786440 | tf_op jit(solution)/shard_map/ppermute | solution.py:798
  14.7 1.5 %collective-permute-start.1 = (f32[512,128]{1,0:T(8,128)S(1)}, f32[512,128]{1,0:T(8,128)S(1)}, u32[]{:S(2)}, u32[]{:S(2)}) collective-permute-start(f32[512,128]{1,0:T(8,128)S(1)} %get-tuple-element.45), channel_id=1, source_target_pairs={{0,0},{1,2},{2,1},{3,3},{4,4},{5,6},{6,5},{7,7},{8,8},{9,10},{10,9... | collective-permute-start | bytes 786440 | tf_op jit(solution)/shard_map/ppermute | solution.py:799
  15.4 8.3 %copy-start = (f32[2,4,1024]{2,1,0:T(4,128)S(1)}, f32[2,4,1024]{2,1,0:T(4,128)}, u32[]{:S(2)}) copy-start(f32[2,4,1024]{2,1,0:T(4,128)} %w0) | copy-start | bytes 98308
  16.7 21.8 %collective-permute-start.3 = (f32[704,128]{1,0:T(8,128)S(1)}, f32[704,128]{1,0:T(8,128)S(1)}, u32[]{:S(2)}, u32[]{:S(2)}) collective-permute-start(f32[704,128]{1,0:T(8,128)S(1)} %get-tuple-element.53), channel_id=1, source_target_pairs={{0,0},{124,124},{4,8},{8,4},{12,16},{16,12},{20,24},{24,20},{28,32... | collective-permute-start | bytes 1081352 | tf_op jit(solution)/shard_map/ppermute | solution.py:778
  23.6 15.0 %collective-permute-start.2 = (f32[704,128]{1,0:T(8,128)S(1)}, f32[704,128]{1,0:T(8,128)S(1)}, u32[]{:S(2)}, u32[]{:S(2)}) collective-permute-start(f32[704,128]{1,0:T(8,128)S(1)} %get-tuple-element.52), channel_id=1, source_target_pairs={{0,4},{4,0},{8,12},{12,8},{16,20},{20,16},{24,28},{28,24},{32,36},... | collective-permute-start | bytes 1081352 | tf_op jit(solution)/shard_map/ppermute | solution.py:778
  23.7 14.3 %collective-permute-start.6 = (f32[2,4,1024]{2,1,0:T(4,128)S(1)}, f32[2,4,1024]{2,1,0:T(4,128)S(1)}, u32[]{:S(2)}, u32[]{:S(2)}) collective-permute-start(f32[2,4,1024]{2,1,0:T(4,128)S(1)} %copy-done), channel_id=1, source_target_pairs={{0,3},{1,2},{2,1},{3,0},{4,7},{5,6},{6,5},{7,4},{8,11},{9,10},{10,... | collective-permute-start | bytes 98312 | tf_op jit(solution)/shard_map/ppermute | solution.py:781
  23.8 14.2 %collective-permute-start.5 = (f32[2,4,1024]{2,1,0:T(4,128)S(1)}, f32[2,4,1024]{2,1,0:T(4,128)S(1)}, u32[]{:S(2)}, u32[]{:S(2)}) collective-permute-start(f32[2,4,1024]{2,1,0:T(4,128)S(1)} %copy-done), channel_id=1, source_target_pairs={{0,2},{1,3},{2,0},{3,1},{4,6},{5,7},{6,4},{7,5},{8,10},{9,11},{10,... | collective-permute-start | bytes 98312 | tf_op jit(solution)/shard_map/ppermute | solution.py:781
  31.6 6.3 %collective-permute-start.4 = (f32[2,4,1024]{2,1,0:T(4,128)S(1)}, f32[2,4,1024]{2,1,0:T(4,128)S(1)}, u32[]{:S(2)}, u32[]{:S(2)}) collective-permute-start(f32[2,4,1024]{2,1,0:T(4,128)S(1)} %copy-done), channel_id=1, source_target_pairs={{0,1},{1,0},{2,3},{3,2},{4,5},{5,4},{6,7},{7,6},{8,9},{9,8},{10,11... | collective-permute-start | bytes 98312 | tf_op jit(solution)/shard_map/ppermute | solution.py:781
  44.1 11.2 %collective-permute-start.7 = (f32[320,128]{1,0:T(8,128)S(1)}, f32[320,128]{1,0:T(8,128)S(1)}, u32[]{:S(2)}, u32[]{:S(2)}) collective-permute-start(f32[320,128]{1,0:T(8,128)S(1)} %get-tuple-element.58), channel_id=1, source_target_pairs={{0,4},{4,0},{8,12},{12,8},{16,20},{20,16},{24,28},{28,24},{32,36},... | collective-permute-start | bytes 491528 | tf_op jit(solution)/shard_map/ppermute | solution.py:778
  45.8 12.5 %collective-permute-start.8 = (f32[320,128]{1,0:T(8,128)S(1)}, f32[320,128]{1,0:T(8,128)S(1)}, u32[]{:S(2)}, u32[]{:S(2)}) collective-permute-start(f32[320,128]{1,0:T(8,128)S(1)} %get-tuple-element.59), channel_id=1, source_target_pairs={{0,0},{124,124},{4,8},{8,4},{12,16},{16,12},{20,24},{24,20},{28,32... | collective-permute-start | bytes 491528 | tf_op jit(solution)/shard_map/ppermute | solution.py:778
  61.2 15.0 %collective-permute-start.9 = (f32[85,8,128]{2,1,0:T(8,128)S(1)}, f32[85,8,128]{2,1,0:T(8,128)S(1)}, u32[]{:S(2)}, u32[]{:S(2)}) collective-permute-start(f32[85,8,128]{2,1,0:T(8,128)S(1)} %get-tuple-element.62), channel_id=1, source_target_pairs={{0,4},{4,0},{8,12},{12,8},{16,20},{20,16},{24,28},{28,24},{32,36},... | collective-permute-start | bytes 1044488 | tf_op jit(solution)/shard_map/ppermute | solution.py:778
  61.3 15.6 %collective-permute-start.10 = (f32[85,8,128]{2,1,0:T(8,128)S(1)}, f32[85,8,128]{2,1,0:T(8,128)S(1)}, u32[]{:S(2)}, u32[]{:S(2)}) collective-permute-start(f32[85,8,128]{2,1,0:T(8,128)S(1)} %get-tuple-element.63), channel_id=1, source_target_pairs={{0,0},{124,124},{4,8},{8,4},{12,16},{16,12},{20,24},{24,20},{28,32... | collective-permute-start | bytes 1044488 | tf_op jit(solution)/shard_map/ppermute | solution.py:778
  69.3 17.8 %collective-permute-start.11 = (f32[90,8,128]{2,1,0:T(8,128)S(1)}, f32[90,8,128]{2,1,0:T(8,128)S(1)}, u32[]{:S(2)}, u32[]{:S(2)}) collective-permute-start(f32[90,8,128]{2,1,0:T(8,128)S(1)} %get-tuple-element.68), channel_id=1, source_target_pairs={{0,4},{4,0},{8,12},{12,8},{16,20},{20,16},{24,28},{28,24},{32,36},... | collective-permute-start | bytes 1105928 | tf_op jit(solution)/shard_map/ppermute | solution.py:778
  69.4 17.7 %collective-permute-start.12 = (f32[90,8,128]{2,1,0:T(8,128)S(1)}, f32[90,8,128]{2,1,0:T(8,128)S(1)}, u32[]{:S(2)}, u32[]{:S(2)}) collective-permute-start(f32[90,8,128]{2,1,0:T(8,128)S(1)} %get-tuple-element.69), channel_id=1, source_target_pairs={{0,0},{124,124},{4,8},{8,4},{12,16},{16,12},{20,24},{24,20},{28,32... | collective-permute-start | bytes 1105928 | tf_op jit(solution)/shard_map/ppermute | solution.py:778
  82.5 11.8 %collective-permute-start.19 = (f32[48,4,256]{2,1,0:T(4,128)S(1)}, f32[48,4,256]{2,1,0:T(4,128)S(1)}, u32[]{:S(2)}, u32[]{:S(2)}) collective-permute-start(f32[48,4,256]{2,1,0:T(4,128)S(1)} %get-tuple-element.81), channel_id=1, source_target_pairs={{0,1},{1,0},{2,3},{3,2},{4,5},{5,4},{6,7},{7,6},{8,9},{9,8},{10,11... | collective-permute-start | bytes 589832 | tf_op jit(solution)/shard_map/ppermute | solution.py:781
  85.3 14.7 %collective-permute-start.20 = (f32[48,4,256]{2,1,0:T(4,128)S(1)}, f32[48,4,256]{2,1,0:T(4,128)S(1)}, u32[]{:S(2)}, u32[]{:S(2)}) collective-permute-start(f32[48,4,256]{2,1,0:T(4,128)S(1)} %get-tuple-element.82), channel_id=1, source_target_pairs={{0,2},{1,3},{2,0},{3,1},{4,6},{5,7},{6,4},{7,5},{8,10},{9,11},{10,... | collective-permute-start | bytes 589832 | tf_op jit(solution)/shard_map/ppermute | solution.py:781
  86.3 13.9 %collective-permute-start.21 = (f32[48,4,256]{2,1,0:T(4,128)S(1)}, f32[48,4,256]{2,1,0:T(4,128)S(1)}, u32[]{:S(2)}, u32[]{:S(2)}) collective-permute-start(f32[48,4,256]{2,1,0:T(4,128)S(1)} %get-tuple-element.83), channel_id=1, source_target_pairs={{0,3},{1,2},{2,1},{3,0},{4,7},{5,6},{6,5},{7,4},{8,11},{9,10},{10,... | collective-permute-start | bytes 589832 | tf_op jit(solution)/shard_map/ppermute | solution.py:781
  92.3 8.8 %collective-permute-start.16 = (f32[44,4,256]{2,1,0:T(4,128)S(1)}, f32[44,4,256]{2,1,0:T(4,128)S(1)}, u32[]{:S(2)}, u32[]{:S(2)}) collective-permute-start(f32[44,4,256]{2,1,0:T(4,128)S(1)} %get-tuple-element.78), channel_id=1, source_target_pairs={{0,1},{1,0},{2,3},{3,2},{4,5},{5,4},{6,7},{7,6},{8,9},{9,8},{10,11... | collective-permute-start | bytes 540680 | tf_op jit(solution)/shard_map/ppermute | solution.py:781
  93.4 15.2 %collective-permute-start.17 = (f32[44,4,256]{2,1,0:T(4,128)S(1)}, f32[44,4,256]{2,1,0:T(4,128)S(1)}, u32[]{:S(2)}, u32[]{:S(2)}) collective-permute-start(f32[44,4,256]{2,1,0:T(4,128)S(1)} %get-tuple-element.79), channel_id=1, source_target_pairs={{0,2},{1,3},{2,0},{3,1},{4,6},{5,7},{6,4},{7,5},{8,10},{9,11},{10,... | collective-permute-start | bytes 540680 | tf_op jit(solution)/shard_map/ppermute | solution.py:781
  94.4 14.3 %collective-permute-start.18 = (f32[44,4,256]{2,1,0:T(4,128)S(1)}, f32[44,4,256]{2,1,0:T(4,128)S(1)}, u32[]{:S(2)}, u32[]{:S(2)}) collective-permute-start(f32[44,4,256]{2,1,0:T(4,128)S(1)} %get-tuple-element.80), channel_id=1, source_target_pairs={{0,3},{1,2},{2,1},{3,0},{4,7},{5,6},{6,5},{7,4},{8,11},{9,10},{10,... | collective-permute-start | bytes 540680 | tf_op jit(solution)/shard_map/ppermute | solution.py:781
  100.0 10.1 %collective-permute-start.13 = (f32[40,4,256]{2,1,0:T(4,128)S(1)}, f32[40,4,256]{2,1,0:T(4,128)S(1)}, u32[]{:S(2)}, u32[]{:S(2)}) collective-permute-start(f32[40,4,256]{2,1,0:T(4,128)S(1)} %get-tuple-element.75), channel_id=1, source_target_pairs={{0,1},{1,0},{2,3},{3,2},{4,5},{5,4},{6,7},{7,6},{8,9},{9,8},{10,11... | collective-permute-start | bytes 491528 | tf_op jit(solution)/shard_map/ppermute | solution.py:781
  100.2 9.8 %collective-permute-start.14 = (f32[40,4,256]{2,1,0:T(4,128)S(1)}, f32[40,4,256]{2,1,0:T(4,128)S(1)}, u32[]{:S(2)}, u32[]{:S(2)}) collective-permute-start(f32[40,4,256]{2,1,0:T(4,128)S(1)} %get-tuple-element.76), channel_id=1, source_target_pairs={{0,2},{1,3},{2,0},{3,1},{4,6},{5,7},{6,4},{7,5},{8,10},{9,11},{10,... | collective-permute-start | bytes 491528 | tf_op jit(solution)/shard_map/ppermute | solution.py:781
  101.1 9.8 %collective-permute-start.15 = (f32[40,4,256]{2,1,0:T(4,128)S(1)}, f32[40,4,256]{2,1,0:T(4,128)S(1)}, u32[]{:S(2)}, u32[]{:S(2)}) collective-permute-start(f32[40,4,256]{2,1,0:T(4,128)S(1)} %get-tuple-element.77), channel_id=1, source_target_pairs={{0,3},{1,2},{2,1},{3,0},{4,7},{5,6},{6,5},{7,4},{8,11},{9,10},{10,... | collective-permute-start | bytes 491528 | tf_op jit(solution)/shard_map/ppermute | solution.py:781

commit v2 on v1

--- a/solution.py
+++ b/solution.py
@@ -15,7 +15,6 @@
 WET, UE, VN, VD = 4, 5, 6, 7
 KAPPA = 0.15
 MIB = 2**20
-UNROLL_C = 4
 UNROLL_S = 4
 UNROLL_L = 4
 UNROLL_M = 2
@@ -154,7 +153,7 @@
     return lax.fori_loop(0, HALF - 1, outwards, start)
 
 
-def first_solve(ids, seed, flow, vd, wet, fld, tri, pxa, pxb, wbuf, pw, pe, sems):
+def first_solve(ids, seed, flow, vd, wet, fld, tri, pxa, pxb, wbuf, pw, sems):
     def tile_copy(src, dst, k):
         copy = pltpu.make_async_copy(src, dst, sems.at[k])
         copy.start()
@@ -185,26 +184,22 @@
 
     lax.fori_loop(0, LEV // 8, wet_to_float, 0)
     lane = iota((ROWS, LANES), 1)
-    zero = jnp.zeros((ROWS, LANES), F32)
+    first8 = lane < 8
     odd = lax.rem(ids[0], 2) == 1
 
-    def pack(values):
-        west = east = zero
-        for b, x0, x1 in values:
-            mine = (lane >= 8 * b) & (lane < 8 * b + 8)
-            west = jnp.where(mine, pltpu.roll(x0, 8 * b, 1) if b else x0, west)
-            s = (8 * b + 8) % LANES
-            east = jnp.where(mine, pltpu.roll(x1, s, 1) if s else x1, east)
-        return west, east
+    def pack(at, fields):
+        out = jnp.zeros((ROWS, LANES), F32)
+        for f in fields:
+            edge = jnp.where(first8, fld[f, 0, at, :], fld[f, 1, at, :])
+            mine = (lane >= 16 * f) & (lane < 16 * f + 16)
+            by = (16 * f + 8) % LANES
+            out = jnp.where(mine, pltpu.roll(edge, by, 1) if by else edge, out)
+        return out
 
     def statics(i):
-        values = []
-        for half, at in enumerate(pair_of(i)):
-            for f in range(4, 8):
-                values.append((8 * half + f, fld[f, 0, at, :], fld[f, 1, at, :]))
-        west, east = pack(values)
-        pw[rows_of(i), :] = west
-        pe[rows_of(i), :] = east
+        top, bottom = pair_of(i)
+        pw[top, :] = pack(top, range(4, 8))
+        pw[bottom, :] = pack(bottom, range(4, 8))
 
     thirds(
         tri,
@@ -220,31 +215,40 @@
         fld[v, t, at, :] = x
 
     for pair in ((0, 1), (2, 3)):
-
-        def solved(i, out, pair=pair):
-            values = []
-            for half in range(2):
-                for c, v in enumerate(pair):
-                    values.append((8 * half + v, out[half][2 * c], out[half][2 * c + 1]))
-            west, east = pack(values)
-            at = rows_of(i)
-            west = pw[at, :] + west
-            east = pe[at, :] + east
-            if pair[0] == 0:
-                pw[at, :] = west
-                pe[at, :] = east
-            else:
-                pxa[at, :] = jnp.where(odd, west, east)
-                pxb[at, :] = jnp.where(odd, east, west)
-
         eliminate(
             lambda v, t, at: fld[v, t, at, :] * fld[WET, t, at, :],
             put,
             lambda v, t, at: fld[v, t, at, :],
             lambda k, t, at: tri[k, t, at, :],
             [(v, t) for v in pair for t in range(2)],
-            solved,
         )
+
+    low = lax.rem(lane, 16) < 8
+
+    def states(n, carry):
+        for i in [4 * n + k for k in range(4)]:
+            top, bottom = pair_of(i)
+            a = pw[top, :] + pack(top, range(4))
+            b = pw[bottom, :] + pack(bottom, range(4))
+            east = jnp.where(low, a, pltpu.roll(b, 8, 1))
+            west = jnp.where(low, pltpu.roll(a, LANES - 8, 1), b)
+            at = rows_of(i)
+            pxa[at, :] = jnp.where(odd, west, east)
+            pxb[at, :] = jnp.where(odd, east, west)
+        return carry
+
+    lax.fori_loop(0, HALF // 4, states, 0)
+
+
+def spread(west, east, half, low):
+    if half == 0:
+        return jnp.where(low, west, pltpu.roll(east, 8, 1))
+    return jnp.where(low, pltpu.roll(west, LANES - 8, 1), east)
+
+
+def outer_of(both, f):
+    by = (120 - 16 * f) % LANES
+    return pltpu.roll(both, by, 1) if by else both
 
 
 OUTER = 5 * 2 * LEV
@@ -266,20 +270,26 @@
     return pltpu.roll(packed, (-(16 * g + 8)) % LANES, 1)
 
 
+def odd_tile(ids):
+    return lax.rem(ids[1], 2) == 1
+
+
+def turn(todd, x, y):
+    return jnp.where(todd, y, x), jnp.where(todd, x, y)
+
+
 def put_edges(todd, pick, fields, oa, ob):
     for f in range(fields):
         for t in range(2):
             for g in range(8):
                 n, s = pick(f, t, g)
                 at = pl.ds((f * 2 + t) * LEV + 8 * g, 8)
-                oa[at, :] = jnp.where(todd, s, n)
-                ob[at, :] = jnp.where(todd, n, s)
+                oa[at, :], ob[at, :] = turn(todd, n, s)
         outer = [pick(f, 2, g) for g in range(8)]
         n = edge_pack([o[0] for o in outer])
         s = edge_pack([o[1] for o in outer])
         at = pl.ds(fields * 2 * LEV + 8 * f, 8)
-        oa[at, :] = jnp.where(todd, s, n)
-        ob[at, :] = jnp.where(todd, n, s)
+        oa[at, :], ob[at, :] = turn(todd, n, s)
 
 
 def edge_rows(ref, g):
@@ -289,7 +299,7 @@
 
 
 def main_edges(ids, fld, ya, yb):
-    todd = lax.rem(ids[1], 2) == 1
+    todd = odd_tile(ids)
     for k, f in enumerate((0, 1, WET, 2, 3)):
         for t in range(2):
             for g in range(8):
@@ -297,14 +307,13 @@
                 if f == WET:
                     n = n * (KAPPA - 0.5 * edge_rows(fld.at[VN, t], g)[0])
                 at = pl.ds((2 * k + t) * LEV + 8 * g, 8)
-                ya[at, :] = jnp.where(todd, s, n)
-                yb[at, :] = jnp.where(todd, n, s)
+                ya[at, :], yb[at, :] = turn(todd, n, s)
 
 
 def outer_edges(ids, xa, xb, ya_in, yb_in, ya, yb):
     face, tile = ids[0], ids[1]
     odd = lax.rem(face, 2) == 1
-    todd = lax.rem(tile, 2) == 1
+    todd = odd_tile(ids)
     for g in range(4):
         na, sa = edge_rows(xa, g)
         nb, sb = edge_rows(xb, g)
@@ -314,8 +323,7 @@
             n = jnp.where(inside, n, 0.0)
             s = jnp.where(inside, s, 0.0)
             at = pl.ds(OUTER + first + 8 * g, 8)
-            ya[at, :] = jnp.where(todd, s, n)
-            yb[at, :] = jnp.where(todd, n, s)
+            ya[at, :], yb[at, :] = turn(todd, n, s)
 
 
 def local_weights(ids, w0, w1, w2, w3, wloc, pieces):
@@ -348,30 +356,23 @@
     on_east = (lane < 8) & (face < 3)
     on_west = (lane >= 120) & (face > 0)
 
+    outside = on_east | on_west
+    low = lax.rem(lane, 16) < 8
+
     def unpack(n, carry):
-        for i in (2 * n, 2 * n + 1):
+        for i in [4 * n + k for k in range(4)]:
             a, b = xa[rows_of(i), :], xb[rows_of(i), :]
             from_west = jnp.where(odd, a, b)
             from_east = jnp.where(odd, b, a)
             for half, at in enumerate(pair_of(i)):
+                both = spread(from_west, from_east, half, low)
                 for f in range(8):
-                    k = 8 * half + f
-                    w = pltpu.roll(from_west, (120 - 8 * k) % LANES, 1)
-                    e = pltpu.roll(from_east, (-8 * k) % LANES, 1)
-                    fe[f, at, :] = jnp.where(on_east, e, jnp.where(on_west, w, 0.0))
+                    fe[f, at, :] = jnp.where(outside, outer_of(both, f), 0.0)
         return carry
 
-    lax.fori_loop(0, HALF // 2, unpack, 0)
-    thirds(
-        tri,
-        lambda t, level: fe[WET, rows_of(level), :],
-        lambda t, level: fe[VD, rows_of(level), :],
-        (2,),
-    )
-
-    def body(i, carry):
-        for k in range(UNROLL_C):
-            at = rows_of(UNROLL_C * i + k)
+    lax.fori_loop(0, HALF // 4, unpack, 0)
+    def body(i):
+        for at in pair_of(i):
 
             def get(f):
                 return [fld[f, 0, at, :], fld[f, 1, at, :], fe[f, at, :]]
@@ -390,9 +391,14 @@
                 cf[2, t, at, :] = w * (KAPPA + 0.5 * vn[t]) * wn
                 cf[3, t, at, :] = w * qs
                 cf[4, t, at, :] = w - ce - cw
-        return carry
-
-    lax.fori_loop(0, LEV // UNROLL_C, body, 0)
+
+    thirds(
+        tri,
+        lambda t, level: fe[WET, rows_of(level), :],
+        lambda t, level: fe[VD, rows_of(level), :],
+        (2,),
+        body,
+    )
 
 
 def slot_of(level):
@@ -400,12 +406,12 @@
 
 
 def take_first_edges(ids, ya, yb, hn, hs, first):
-    todd = lax.rem(ids[1], 2) == 1
+    todd = odd_tile(ids)
     lane = iota((8, LANES), 1)
 
     def both(at):
         a, b = ya[at, :], yb[at, :]
-        return jnp.where(todd, b, a), jnp.where(todd, a, b)
+        return turn(todd, a, b)
 
     for f, k in enumerate((0, 1, 2) if first else (3, 4)):
         for t in range(2):
@@ -414,16 +420,15 @@
                 n, s = both(pl.ds((2 * k + t) * LEV + 8 * g, 8))
                 hn[f, t, at, :] = n
                 hs[f, t, at, :] = s
+    low = lax.rem(lane, 16) < 8
     for g in range(4):
         wests = both(pl.ds(OUTER + 8 * g, 8))
         easts = both(pl.ds(OUTER + HALF + 8 * g, 8))
         for half in range(2):
+            spreads = [spread(w, e, half, low) for w, e in zip(wests, easts)]
 
             def outer(side, f):
-                b = 8 * half + f
-                w = pltpu.roll(wests[side], (120 - 8 * b) % LANES, 1)
-                e = pltpu.roll(easts[side], (-8 * b) % LANES, 1)
-                return jnp.where(lane < 64, e, w)
+                return outer_of(spreads[side], f)
 
             at = pl.ds(HALF * half + 8 * g, 8)
             for f, k in enumerate((0, 1) if first else (2, 3)):
@@ -435,26 +440,39 @@
 
 
 def take_edges(ids, load, hn, hs, groups=(0, 8)):
-    todd = lax.rem(ids[1], 2) == 1
+    todd = odd_tile(ids)
     for f in range(2):
         oa, ob = load(32 + f)
-        on, os = jnp.where(todd, ob, oa), jnp.where(todd, oa, ob)
+        on, os = turn(todd, oa, ob)
         for g in range(*groups):
             at = pl.ds(8 * g, 8)
             for t in range(2):
                 a, b = load((f * 2 + t) * 8 + g)
-                hn[f, t, at, :] = jnp.where(todd, b, a)
-                hs[f, t, at, :] = jnp.where(todd, a, b)
+                hn[f, t, at, :], hs[f, t, at, :] = turn(todd, a, b)
             hn[f, 2, at, :] = edge_unpack(on, g)
             hs[f, 2, at, :] = edge_unpack(os, g)
 
 
-def stencil(y, coef, north_row, south_row, row, tiles=3):
+def stencil(y, ref, level, coef, north_row, south_row, tiles=3):
     e, w = east_of(y), west_of(y)
+    sub = iota((8, LANES), 0)
+    base = pl.multiple_of(level * ROWS, ROWS)
     out = []
     for t in range(tiles):
-        n = jnp.where(row == ROWS - 1, north_row[t], pltpu.roll(y[t], ROWS - 1, 0))
-        s = jnp.where(row == 0, south_row[t], pltpu.roll(y[t], 1, 0))
+        n = jnp.concatenate(
+            [
+                ref(t)[pl.ds(base + 1, 8), :],
+                jnp.where(sub == 7, north_row[t], pltpu.roll(y[t][8:16], 7, 0)),
+            ],
+            0,
+        )
+        s = jnp.concatenate(
+            [
+                jnp.where(sub == 0, south_row[t], pltpu.roll(y[t][0:8], 1, 0)),
+                ref(t)[pl.ds(base + 7, 8), :],
+            ],
+            0,
+        )
         ce, cw, cn, cs, cc = coef[t]
         out.append(cc * y[t] + ce * e[t] + cw * w[t] + cn * n + cs * s)
     return out
@@ -465,6 +483,7 @@
         wloc, cf, sol, oa, ob, fo, hn, hs = refs
     else:
         sol, oa, ob, fo, hn, hs = refs
+    todd = odd_tile(ids)
     row = iota((ROWS, LANES), 0)
     take_first_edges(ids, ya, yb, hn, hs, first)
 
@@ -493,7 +512,10 @@
             for v in range(2):
                 n = [hn[v, t, ones[t], :] for t in range(3)]
                 s = [hs[v, t, ones[t], :] for t in range(3)]
-                adj = stencil(get(v, at), coef, n, s, row)
+                f = v0 + v
+                adj = stencil(
+                    get(v, at), lambda t: fe.at[f] if t == 2 else fld.at[f, t], level, coef, n, s
+                )
                 for t in range(3):
                     sol[v, t, at, :] = adj[t]
         return carry
@@ -517,7 +539,6 @@
         y = get(v, pl.ds(0, ROWS))
         for t in range(3):
             fo[v, t] = y[t] + top[3 * v + t]
-    todd = lax.rem(ids[1], 2) == 1
     put_edges(todd, lambda f, t, g: edge_rows(sol.at[f, t], g), 2, oa, ob)
     if first:
         for c in range(2):
@@ -525,8 +546,7 @@
                 n = wloc[c, t, 8:16, :]
                 s = wloc[c, t, 0:8, :]
                 at = pl.ds(ROWS_2 + 8 * (3 * c + t), 8)
-                oa[at, :] = jnp.where(todd, s, n)
-                ob[at, :] = jnp.where(todd, n, s)
+                oa[at, :], ob[at, :] = turn(todd, n, s)
 
 
 def last_stencil(v0, l0, nl, extra, carried, grads, *refs):
@@ -546,8 +566,8 @@
     else:
         adj_out, hn, hs, buf, sem = refs
     row = iota((ROWS, LANES), 0)
+    todd = odd_tile(ids)
     low_half = iota((8, LANES), 0) < 4
-    todd = lax.rem(ids[1], 2) == 1
 
     def load(block):
         if not grads:
@@ -563,8 +583,7 @@
             n = jnp.where(low_half, pltpu.roll(a[8:16], 4, 0), b[8:16])
             s = jnp.where(low_half, a[0:8], pltpu.roll(b[0:8], 4, 0))
             if t < 2:
-                ga[2 * u + t] = jnp.where(todd, s, n)
-                gb[2 * u + t] = jnp.where(todd, n, s)
+                ga[2 * u + t], gb[2 * u + t] = turn(todd, n, s)
             else:
                 en[u] = n
                 es[u] = s
@@ -581,7 +600,7 @@
                 y = [sol[v, t, at, :] for t in range(3)]
                 n = [hn[v, t, one, :] for t in range(3)]
                 s = [hs[v, t, one, :] for t in range(3)]
-                x = stencil(y, coef, n, s, row, 3 if grads else 2)
+                x = stencil(y, lambda t: sol.at[v, t], level, coef, n, s, 3 if grads else 2)
                 buf[u, v, :, 0:LANES] = x[0]
                 buf[u, v, :, LANES : 2 * LANES] = x[1]
                 if grads:
@@ -613,8 +632,7 @@
                     mine = (lane >= 16 * j) & (lane < 16 * j + 16)
                     pn = jnp.where(mine, pltpu.roll(en[u], (16 * j + 8) % LANES, 1), pn)
                     ps = jnp.where(mine, pltpu.roll(es[u], (16 * j + 8) % LANES, 1), ps)
-            ga[2 * units + i] = jnp.where(todd, ps, pn)
-            gb[2 * units + i] = jnp.where(todd, pn, ps)
+            ga[2 * units + i], gb[2 * units + i] = turn(todd, pn, ps)
         if carried:
             for i in range(BLOCKS_2):
                 ga[2 * units + per + i] = ua[pl.ds(8 * i, 8), :]
@@ -626,7 +644,7 @@
     del after
     zs = (z0, z1, z2, z3)
     face, tile = ids[0], ids[1]
-    todd = lax.rem(tile, 2) == 1
+    todd = odd_tile(ids)
     has_n, has_s = tile < 31, tile > 0
     sub = iota((8, LANES), 0)
     lane = iota((8, LANES), 1)
@@ -661,8 +679,9 @@
         for t in range(3):
             at = pl.ds(ROWS_2 + 8 * (3 * c + t), 8)
             a, b = ya[at, :], yb[at, :]
-            hi = jnp.where(has_n, jnp.where(todd, b, a), 0.0)
-            lo = jnp.where(has_s, jnp.where(todd, a, b), 0.0)
+            a, b = turn(todd, a, b)
+            hi = jnp.where(has_n, a, 0.0)
+            lo = jnp.where(has_s, b, 0.0)
             if c == 1:
                 below.append(pltpu.roll(lo, 5, 0))
             dest.append(
@@ -693,8 +712,9 @@
     for u in range(u0, u1):
         j, i = divmod(u, per)
         a, b = ga[2 * units + i], gb[2 * units + i]
-        n = edge_unpack(jnp.where(todd, b, a), j)
-        s = edge_unpack(jnp.where(todd, a, b), j)
+        a, b = turn(todd, a, b)
+        n = edge_unpack(a, j)
+        s = edge_unpack(b, j)
         u -= u0
         hn[u] = jnp.where(has_n, n, 0.0)
         hs[u] = jnp.where(has_s, s, 0.0)
@@ -708,8 +728,9 @@
             hi, lo = [], []
             for t in range(2):
                 a, b = ga[2 * (u0 + u) + t], gb[2 * (u0 + u) + t]
-                hi.append(jnp.where(has_n, jnp.where(todd, b, a), 0.0))
-                lo.append(jnp.where(has_s, jnp.where(todd, a, b), 0.0))
+                a, b = turn(todd, a, b)
+                hi.append(jnp.where(has_n, a, 0.0))
+                lo.append(jnp.where(has_s, b, 0.0))
             hi.append(hn[u])
             lo.append(hs[u])
             for v in range(2):
@@ -720,17 +741,18 @@
                     bottom = lo[t] if v == 0 else pltpu.roll(lo[t], 4, 0)
                     x.append(stack3(bottom, m[0:8], m[8:16], top))
                 fields.append(x)
-        for _ in range(4):
+        for sweep in range(4):
+            kept = 3 if sweep < 3 else 2
             coefs = [[[w5[c, t, k] for c in range(5)] for k in range(3)] for t in range(3)]
             swept = []
             for x in fields:
-                ns = [north_of(x[t]) for t in range(3)]
-                ss = [south_of(x[t]) for t in range(3)]
+                ns = [north_of(x[t]) for t in range(kept)]
+                ss = [south_of(x[t]) for t in range(kept)]
                 new = [[], [], []]
                 for k in range(3):
                     at_k = [x[t][k] for t in range(3)]
                     e, w = east_of(at_k), west_of(at_k)
-                    for t in range(3):
+                    for t in range(kept):
                         ce, cw, cn, cs, cc = coefs[t][k]
                         new[t].append(
                             cc * x[t][k] + ce * e[t] + cw * w[t] + cn * ns[t][k] + cs * ss[t][k]
@@ -767,9 +789,7 @@
     ids = jnp.stack([lax.axis_index("face"), lax.axis_index("tile")]).astype(jnp.int32)
     tiles = lax.axis_size("tile")
     pair_a = [(i, i ^ 1) for i in range(tiles)]
-    pair_b = [(0, 0), (tiles - 1, tiles - 1)]
-    for i in range(1, tiles - 1, 2):
-        pair_b += [(i, i + 1), (i + 1, i)]
+    pair_b = [(i, (i + (1 if i % 2 else -1)) % tiles) for i in range(tiles)]
     side_a = [(0, 1), (1, 0), (2, 3), (3, 2)]
     side_b = [(0, 0), (1, 2), (2, 1), (3, 3)]
     hbm, any_space = pltpu.HBM, pl.ANY
@@ -787,14 +807,22 @@
         [((8, 2, FLAT, LANES), VM), ((3, 2, FLAT, LANES), VM), (packed, VM), (packed, VM)],
         [
             VM((2, LEV) + edge, jnp.int32),
-            VM(packed, F32),
-            VM(packed, F32),
+            VM((FLAT, LANES), F32),
             pltpu.SemaphoreType.DMA((16,)),
         ],
         limit=5,
         ins=[None] + [hbm] * 4,
         name="first_solve",
     )(ids, adjoint_seed, face_flow, vert_diff, wet_mask)
+    weights = [smooth_weights] + [to_face(smooth_weights, k) for k in (1, 2, 3)]
+    (wloc,) = call(
+        local_weights,
+        [((2, 3) + edge, VM)],
+        [VM((4, 2, 4, 1024), F32)],
+        limit=4,
+        name="local_weights",
+    )(ids, *weights)
+    pxa, pxb, wloc = lax.optimization_barrier((pxa, pxb, wloc))
     xa = lax.ppermute(pxa, "face", side_a)
     xb = lax.ppermute(pxb, "face", side_b)
     rows_1 = ((ROWS_1, LANES), VM)
@@ -802,7 +830,6 @@
     ya, yb = call(
         outer_edges, [rows_1, rows_1], limit=4, alias={3: 0, 4: 1}, name="outer_edges"
     )(ids, xa, xb, ya, yb)
-    later, _ = lax.optimization_barrier((smooth_weights, ya))
     ya, yb = across(ya, yb)
     fe, cf, tre = call(
         coefficients,
@@ -810,14 +837,6 @@
         limit=4,
         name="coefficients",
     )(ids, fld, xa, xb)
-    weights = [later] + [to_face(later, k) for k in (1, 2, 3)]
-    (wloc,) = call(
-        local_weights,
-        [((2, 3) + edge, VM)],
-        [VM((4, 2, 4, 1024), F32)],
-        limit=4,
-        name="local_weights",
-    )(ids, *weights)
     halo = VM((3, 3, LEV, LANES), F32)
     sol_shape = ((2, 3, FLAT, LANES), VM)
     fo_shape = ((2, 3) + edge, VM)

time: 114 us -> 108 us (0.947)
  the two profiles are of different devices: /device:TPU:97 before, /device:TPU:1 now
where the time goes in v2:
time: 108 us
  Pallas kernels  60.7 us (56%)
  starting transfers between devices  40 us (37%)
  waiting for transfers between devices  6.3 us (6%)
    pallas_call x16, Pallas kernels, run(): pl.pallas_call(kernel, out_shape=[jax.ShapeDtypeStruct(s, F32) for s, _ i...  60.7 us
    ppermute x8, starting transfers between devices, across(): return (lax.ppermute(a, 'tile', pair_a), lax.ppermute(b, 'tile', pair_b))  21.2 us
    ppermute x12, starting transfers between devices, to_face(): return lax.ppermute(x, 'face', [(i, i ^ k) for i in range(4)])  15.1 us
    ppermute x1, waiting for transfers between devices, on_device(): xb = lax.ppermute(pxb, 'face', side_b)  3.74 us
    ppermute x1, starting transfers between devices, on_device(): xb = lax.ppermute(pxb, 'face', side_b)  3.44 us
  transfers between devices with their start and end apart: 22, of which 3 were waited for; matrix products, arithmetic and copies ran while one was open for 0% of the time, Pallas kernels for 46%

profile of v2, /device:TPU:1, one launch (start us, length us, event | category | flops | bytes accessed | tf_op | source)
XLA Modules:
  0.0 108.0 jit_solution(15218072394125368672)
XLA Ops:
  0.6 2.5 %collective-permute-start.1 = (f32[2,4,1024]{2,1,0:T(4,128)}, f32[2,4,1024]{2,1,0:T(4,128)S(1)}, u32[]{:S(2)}, u32[]{:S(2)}) collective-permute-start(f32[2,4,1024]{2,1,0:T(4,128)} %w0.1), channel_id=1, source_target_pairs={{0,2},{1,3},{2,0},{3,1},{4,6},{5,7},{6,4},{7,5},{8,10},{9,11},{10,... | collective-permute-start | bytes 98312 | tf_op jit(solution)/shard_map/ppermute | solution.py:801
  4.2 9.6 %first_solve.1 = (f32[8,2,1024,128]{3,2,1,0:T(8,128)S(1)}, f32[3,2,1024,128]{3,2,1,0:T(8,128)S(1)}, f32[512,128]{1,0:T(8,128)S(1)}, f32[512,128]{1,0:T(8,128)S(1)}) custom-call(s32[2]{0:T(128)S(1)} %pad_add_fusion.ids.refs_0_, f32[64,4,16,256]{3,2,1,0:T(8,128)} %seed.1, f32[2,64,16,256]{3,2,1,0:T(8,128)} %flow.1, f32[64,16,256]{2,1,0:T(8,128)} %vd.1, ...), custom_call_target="tpu_custom_call" | custom-call | tf_op jit(solution)/shard_map/first_solve/pallas_call | solution.py:56
  14.8 3.4 %collective-permute-start.4 = (f32[512,128]{1,0:T(8,128)S(1)}, f32[512,128]{1,0:T(8,128)S(1)}, u32[]{:S(2)}, u32[]{:S(2)}) collective-permute-start(f32[512,128]{1,0:T(8,128)S(1)} %get-tuple-element.49), channel_id=1, source_target_pairs={{0,0},{1,2},{2,1},{3,3},{4,4},{5,6},{6,5},{7,7},{8,8},{9,10},{10,9... | collective-permute-start | bytes 786440 | tf_op jit(solution)/shard_map/ppermute | solution.py:827
  19.0 3.7 %collective-permute-done.4.xb = f32[512,128]{1,0:T(8,128)S(1)} collective-permute-done((f32[512,128]{1,0:T(8,128)S(1)}, f32[512,128]{1,0:T(8,128)S(1)}, u32[]{:S(2)}, u32[]{:S(2)}) %collective-permute-start.4) | collective-permute-done | bytes 262176 | tf_op jit(solution)/shard_map/ppermute | solution.py:827
  24.7 7.4 %collective-permute-start.6 = (f32[704,128]{1,0:T(8,128)S(1)}, f32[704,128]{1,0:T(8,128)S(1)}, u32[]{:S(2)}, u32[]{:S(2)}) collective-permute-start(f32[704,128]{1,0:T(8,128)S(1)} %get-tuple-element.57), channel_id=1, source_target_pairs={{0,124},{4,8},{8,4},{12,16},{16,12},{20,24},{24,20},{28,32},{32,28... | collective-permute-start | bytes 1081352 | tf_op jit(solution)/shard_map/ppermute | solution.py:798
  32.1 7.2 %coefficients.1 = (f32[8,1024,128]{2,1,0:T(8,128)S(1)}, f32[5,3,1024,128]{3,2,1,0:T(8,128)S(1)}, f32[3,1,1024,128]{3,2,1,0:T(8,128)S(1)}) custom-call(s32[2]{0:T(128)S(1)} %pad_add_fusion.ids.refs_0_, f32[8,2,1024,128]{3,2,1,0:T(8,128)S(1)} %get-tuple-element.45.fld, f32[512,128]{1,0:T(8,128)S(1)} %collective-permute-done.3.xa, ...), custom_call_target="tpu_custom_call" | custom-call | tf_op jit(solution)/shard_map/coefficients/pallas_call | solution.py:56
  39.4 5.4 %step_ts.1 = (f32[5,3,1024,128]{3,2,1,0:T(8,128)S(1)}, f32[2,3,1024,128]{3,2,1,0:T(8,128)S(1)}, f32[320,128]{1,0:T(8,128)S(1)}, f32[320,128]{1,0:T(8,128)S(1)}, f32[2,3,16,128]{3,2,1,0:T(8,128)S(1)}) custom-call(s32[2]{0:T(128)S(1)} %pad_add_fusion.ids.refs_0_, f32[8,2,1024,128]{3,2,1,0:T(8,128)S(1)} %get-tuple-element.45.fld, ...), custom_call_target="tpu_custom_call", output_to_operand_aliasing={{0}: (3, {})} | custom-call | tf_op jit(solution)/shard_map/step_ts/pallas_call | solution.py:56
  44.9 4.8 %collective-permute-start.8 = (f32[320,128]{1,0:T(8,128)S(1)}, f32[320,128]{1,0:T(8,128)S(1)}, u32[]{:S(2)}, u32[]{:S(2)}) collective-permute-start(f32[320,128]{1,0:T(8,128)S(1)} %get-tuple-element.63), channel_id=1, source_target_pairs={{0,124},{4,8},{8,4},{12,16},{16,12},{20,24},{24,20},{28,32},{32,28... | collective-permute-start | bytes 491528 | tf_op jit(solution)/shard_map/ppermute | solution.py:798
  49.7 5.2 %step_uv.1 = (f32[2,3,1024,128]{3,2,1,0:T(8,128)S(1)}, f32[272,128]{1,0:T(8,128)S(1)}, f32[272,128]{1,0:T(8,128)S(1)}, f32[2,3,16,128]{3,2,1,0:T(8,128)S(1)}) custom-call(s32[2]{0:T(128)S(1)} %pad_add_fusion.ids.refs_0_, f32[8,2,1024,128]{3,2,1,0:T(8,128)S(1)} %get-tuple-element.45.fld, f32[8,1024,128]{2,1,0:T(8,128)S(1)} %get-tuple-element.50.fe, ...), custom_call_target="tpu_custom_call" | custom-call | tf_op jit(solution)/shard_map/step_uv/pallas_call | solution.py:56
  54.9 2.7 %last_ts_0.1 = (f32[64,4,16,256]{3,2,1,0:T(8,128)}, f32[24,2,3,16,128]{4,3,2,1,0:T(8,128)S(1)}, f32[85,8,128]{2,1,0:T(8,128)S(1)}, f32[85,8,128]{2,1,0:T(8,128)S(1)}) custom-call(s32[2]{0:T(128)S(1)} %pad_add_fusion.ids.refs_0_, f32[2,3,1024,128]{3,2,1,0:T(8,128)S(1)} %get-tuple-element.61.refs_1_, f32[5,3,1024,128]{3,2,1,0:T(8,128)S(1)} %get-tuple-element.59.cfi.refs_2_, ...), custom_call_target="tpu_custom_call" | custom-call | tf_op jit(solution)/shard_map/last_ts_0/pallas_call | solution.py:56
  57.8 4.7 %collective-permute-start.10 = (f32[85,8,128]{2,1,0:T(8,128)S(1)}, f32[85,8,128]{2,1,0:T(8,128)S(1)}, u32[]{:S(2)}, u32[]{:S(2)}) collective-permute-start(f32[85,8,128]{2,1,0:T(8,128)S(1)} %get-tuple-element.67), channel_id=1, source_target_pairs={{0,124},{4,8},{8,4},{12,16},{16,12},{20,24},{24,20},{28,32},{32,28... | collective-permute-start | bytes 1044488 | tf_op jit(solution)/shard_map/ppermute | solution.py:798
  62.5 3.7 %last_ts_24.1 = (f32[64,4,16,256]{3,2,1,0:T(8,128)}, f32[42,2,3,16,128]{4,3,2,1,0:T(8,128)S(1)}, f32[90,8,128]{2,1,0:T(8,128)S(1)}, f32[90,8,128]{2,1,0:T(8,128)S(1)}) custom-call(s32[2]{0:T(128)S(1)} %pad_add_fusion.ids.refs_0_, f32[2,3,1024,128]{3,2,1,0:T(8,128)S(1)} %get-tuple-element.61.refs_1_, ...), custom_call_target="tpu_custom_call", output_to_operand_aliasing={{0}: (7, {})} | custom-call | tf_op jit(solution)/shard_map/last_ts_24/pallas_call | solution.py:56
  66.3 2.6 %collective-permute-start.12 = (f32[90,8,128]{2,1,0:T(8,128)S(1)}, f32[90,8,128]{2,1,0:T(8,128)S(1)}, u32[]{:S(2)}, u32[]{:S(2)}) collective-permute-start(f32[90,8,128]{2,1,0:T(8,128)S(1)} %get-tuple-element.73), channel_id=1, source_target_pairs={{0,124},{4,8},{8,4},{12,16},{16,12},{20,24},{24,20},{28,32},{32,28... | collective-permute-start | bytes 1105928 | tf_op jit(solution)/shard_map/ppermute | solution.py:798
  69.7 5.7 %smooth_0_0.1 = (f32[48,4,256]{2,1,0:T(4,128)S(1)}, f32[48,4,256]{2,1,0:T(4,128)S(1)}, f32[48,4,256]{2,1,0:T(4,128)S(1)}, f32[48,4,256]{2,1,0:T(4,128)S(1)}) custom-call(s32[2]{0:T(128)S(1)} %pad_add_fusion.ids.refs_0_, f32[24,2,3,16,128]{4,3,2,1,0:T(8,128)S(1)} %get-tuple-element.74.g, f32[85,8,128]{2,1,0:T(8,128)S(1)} %collective-permute-done.9.ga.refs_3_, ...), custom_call_target="tpu_custom_call" | custom-call | tf_op jit(solution)/shard_map/smooth_0_0/pallas_call | solution.py:56
  75.5 7.0 %collective-permute-start.20 = (f32[48,4,256]{2,1,0:T(4,128)S(1)}, f32[48,4,256]{2,1,0:T(4,128)S(1)}, u32[]{:S(2)}, u32[]{:S(2)}) collective-permute-start(f32[48,4,256]{2,1,0:T(4,128)S(1)} %get-tuple-element.86), channel_id=1, source_target_pairs={{0,2},{1,3},{2,0},{3,1},{4,6},{5,7},{6,4},{7,5},{8,10},{9,11},{10,... | collective-permute-start | bytes 589832 | tf_op jit(solution)/shard_map/ppermute | solution.py:801
  82.5 5.2 %smooth_1_0.1 = (f32[44,4,256]{2,1,0:T(4,128)S(1)}, f32[44,4,256]{2,1,0:T(4,128)S(1)}, f32[44,4,256]{2,1,0:T(4,128)S(1)}, f32[44,4,256]{2,1,0:T(4,128)S(1)}) custom-call(s32[2]{0:T(128)S(1)} %pad_add_fusion.ids.refs_0_, f32[42,2,3,16,128]{4,3,2,1,0:T(8,128)S(1)} %get-tuple-element.71.after.g, f32[90,8,128]{2,1,0:T(8,128)S(1)} %collective-permute-done.11.ga, ...), custom_call_target="tpu_custom_call" | custom-call | tf_op jit(solution)/shard_map/smooth_1_0/pallas_call | solution.py:56
  88.2 1.4 %collective-permute-start.17 = (f32[44,4,256]{2,1,0:T(4,128)S(1)}, f32[44,4,256]{2,1,0:T(4,128)S(1)}, u32[]{:S(2)}, u32[]{:S(2)}) collective-permute-start(f32[44,4,256]{2,1,0:T(4,128)S(1)} %get-tuple-element.83), channel_id=1, source_target_pairs={{0,2},{1,3},{2,0},{3,1},{4,6},{5,7},{6,4},{7,5},{8,10},{9,11},{10,... | collective-permute-start | bytes 540680 | tf_op jit(solution)/shard_map/ppermute | solution.py:801
  90.0 4.8 %smooth_1_22.1 = (f32[40,4,256]{2,1,0:T(4,128)S(1)}, f32[40,4,256]{2,1,0:T(4,128)S(1)}, f32[40,4,256]{2,1,0:T(4,128)S(1)}, f32[40,4,256]{2,1,0:T(4,128)S(1)}) custom-call(s32[2]{0:T(128)S(1)} %pad_add_fusion.ids.refs_0_, f32[42,2,3,16,128]{4,3,2,1,0:T(8,128)S(1)} %get-tuple-element.71.after.g, f32[90,8,128]{2,1,0:T(8,128)S(1)} %collective-permute-done.11.ga, ...), custom_call_target="tpu_custom_call" | custom-call | tf_op jit(solution)/shard_map/smooth_1_22/pallas_call | solution.py:56
  95.2 1.4 %collective-permute-start.14 = (f32[40,4,256]{2,1,0:T(4,128)S(1)}, f32[40,4,256]{2,1,0:T(4,128)S(1)}, u32[]{:S(2)}, u32[]{:S(2)}) collective-permute-start(f32[40,4,256]{2,1,0:T(4,128)S(1)} %get-tuple-element.80), channel_id=1, source_target_pairs={{0,2},{1,3},{2,0},{3,1},{4,6},{5,7},{6,4},{7,5},{8,10},{9,11},{10,... | collective-permute-start | bytes 491528 | tf_op jit(solution)/shard_map/ppermute | solution.py:801
  97.1 4.9 %last_uv.1 = f32[64,4,16,256]{3,2,1,0:T(8,128)} custom-call(s32[2]{0:T(128)S(1)} %pad_add_fusion.ids.refs_0_, f32[2,3,1024,128]{3,2,1,0:T(8,128)S(1)} %get-tuple-element.60.refs_1_, f32[5,3,1024,128]{3,2,1,0:T(8,128)S(1)} %get-tuple-element.59.cfi.refs_2_, f32[85,8,128]{2,1,0:T(8,128)S(1)} %collective-permute-done.9.ga.refs_3_, ...), custom_call_target="tpu_custom_call", output_to_operand_aliasing={{}: (6, {})} | custom-call | tf_op jit(solution)/shard_map/last_uv/pallas_call | solution.py:56
  102.0 1.5 %gather_0.1.refs_0_ = f32[132,4,1024]{2,1,0:T(4,128)} custom-call(s32[2]{0:T(128)S(1)} %pad_add_fusion.ids.refs_0_, f32[48,4,256]{2,1,0:T(4,128)S(1)} %get-tuple-element.75.after.z0, f32[48,4,256]{2,1,0:T(4,128)S(1)} %collective-permute-done.19.z1, f32[48,4,256]{2,1,0:T(4,128)S(1)} %collective-permute-done.20.z2, f32[48,4,256]{2,1,0:T(4,128)S(1)} %collective-permute-done.21.z3), custom_call_target="tpu_custom_call" | custom-call | tf_op jit(solution)/shard_map/gather_0/pallas_call | solution.py:56
  103.4 1.4 %gather_48.1.refs_0_ = f32[132,4,1024]{2,1,0:T(4,128)} custom-call(s32[2]{0:T(128)S(1)} %pad_add_fusion.ids.refs_0_, f32[44,4,256]{2,1,0:T(4,128)S(1)} %get-tuple-element.76.after.z0, f32[44,4,256]{2,1,0:T(4,128)S(1)} %collective-permute-done.16.z1, f32[44,4,256]{2,1,0:T(4,128)S(1)} %collective-permute-done.17.z2, ...), custom_call_target="tpu_custom_call", output_to_operand_aliasing={{}: (5, {})} | custom-call | tf_op jit(solution)/shard_map/gather_48/pallas_call | solution.py:56
  104.9 1.7 %collective-permute-done.15.z3 = f32[40,4,256]{2,1,0:T(4,128)S(1)} collective-permute-done((f32[40,4,256]{2,1,0:T(4,128)S(1)}, f32[40,4,256]{2,1,0:T(4,128)S(1)}, u32[]{:S(2)}, u32[]{:S(2)}) %collective-permute-start.15) | collective-permute-done | bytes 163872 | tf_op jit(solution)/shard_map/ppermute | solution.py:801
  106.6 1.4 %gather_92.1 = f32[132,4,1024]{2,1,0:T(4,128)} custom-call(s32[2]{0:T(128)S(1)} %pad_add_fusion.ids.refs_0_, f32[40,4,256]{2,1,0:T(4,128)S(1)} %get-tuple-element.77.refs_5_.z0, f32[40,4,256]{2,1,0:T(4,128)S(1)} %collective-permute-done.13.z1, f32[40,4,256]{2,1,0:T(4,128)S(1)} %collective-permute-done.14.z2, ...), custom_call_target="tpu_custom_call", output_to_operand_aliasing={{}: (5, {})} | custom-call | tf_op jit(solution)/shard_map/gather_92/pallas_call | solution.py:56
  (39 shorter events, 7.5 us)
Async XLA Ops:
  0.6 13.2 %collective-permute-start.1 = (f32[2,4,1024]{2,1,0:T(4,128)}, f32[2,4,1024]{2,1,0:T(4,128)S(1)}, u32[]{:S(2)}, u32[]{:S(2)}) collective-permute-start(f32[2,4,1024]{2,1,0:T(4,128)} %w0.1), channel_id=1, source_target_pairs={{0,2},{1,3},{2,0},{3,1},{4,6},{5,7},{6,4},{7,5},{8,10},{9,11},{10,... | collective-permute-start | bytes 98312 | tf_op jit(solution)/shard_map/ppermute | solution.py:801
  3.2 10.7 %collective-permute-start = (f32[2,4,1024]{2,1,0:T(4,128)}, f32[2,4,1024]{2,1,0:T(4,128)S(1)}, u32[]{:S(2)}, u32[]{:S(2)}) collective-permute-start(f32[2,4,1024]{2,1,0:T(4,128)} %w0.1), channel_id=1, source_target_pairs={{0,1},{1,0},{2,3},{3,2},{4,5},{5,4},{6,7},{7,6},{8,9},{9,8},{10,11... | collective-permute-start | bytes 98312 | tf_op jit(solution)/shard_map/ppermute | solution.py:801
  4.1 9.8 %collective-permute-start.2 = (f32[2,4,1024]{2,1,0:T(4,128)}, f32[2,4,1024]{2,1,0:T(4,128)S(1)}, u32[]{:S(2)}, u32[]{:S(2)}) collective-permute-start(f32[2,4,1024]{2,1,0:T(4,128)} %w0.1), channel_id=1, source_target_pairs={{0,3},{1,2},{2,1},{3,0},{4,7},{5,6},{6,5},{7,4},{8,11},{9,10},{10,... | collective-permute-start | bytes 98312 | tf_op jit(solution)/shard_map/ppermute | solution.py:801
  4.2 9.7 %copy-start = (f32[2,4,1024]{2,1,0:T(4,128)S(1)}, f32[2,4,1024]{2,1,0:T(4,128)}, u32[]{:S(2)}) copy-start(f32[2,4,1024]{2,1,0:T(4,128)} %w0.1) | copy-start | bytes 98308
  14.5 4.5 %collective-permute-start.3 = (f32[512,128]{1,0:T(8,128)S(1)}, f32[512,128]{1,0:T(8,128)S(1)}, u32[]{:S(2)}, u32[]{:S(2)}) collective-permute-start(f32[512,128]{1,0:T(8,128)S(1)} %get-tuple-element.48), channel_id=1, source_target_pairs={{0,1},{1,0},{2,3},{3,2},{4,5},{5,4},{6,7},{7,6},{8,9},{9,8},{10,11... | collective-permute-start | bytes 786440 | tf_op jit(solution)/shard_map/ppermute | solution.py:826
  14.8 8.0 %collective-permute-start.4 = (f32[512,128]{1,0:T(8,128)S(1)}, f32[512,128]{1,0:T(8,128)S(1)}, u32[]{:S(2)}, u32[]{:S(2)}) collective-permute-start(f32[512,128]{1,0:T(8,128)S(1)} %get-tuple-element.49), channel_id=1, source_target_pairs={{0,0},{1,2},{2,1},{3,3},{4,4},{5,6},{6,5},{7,7},{8,8},{9,10},{10,9... | collective-permute-start | bytes 786440 | tf_op jit(solution)/shard_map/ppermute | solution.py:827
  23.3 16.0 %collective-permute-start.5 = (f32[704,128]{1,0:T(8,128)S(1)}, f32[704,128]{1,0:T(8,128)S(1)}, u32[]{:S(2)}, u32[]{:S(2)}) collective-permute-start(f32[704,128]{1,0:T(8,128)S(1)} %get-tuple-element.56), channel_id=1, source_target_pairs={{0,4},{4,0},{8,12},{12,8},{16,20},{20,16},{24,28},{28,24},{32,36},... | collective-permute-start | bytes 1081352 | tf_op jit(solution)/shard_map/ppermute | solution.py:798
  24.7 14.6 %collective-permute-start.6 = (f32[704,128]{1,0:T(8,128)S(1)}, f32[704,128]{1,0:T(8,128)S(1)}, u32[]{:S(2)}, u32[]{:S(2)}) collective-permute-start(f32[704,128]{1,0:T(8,128)S(1)} %get-tuple-element.57), channel_id=1, source_target_pairs={{0,124},{4,8},{8,4},{12,16},{16,12},{20,24},{24,20},{28,32},{32,28... | collective-permute-start | bytes 1081352 | tf_op jit(solution)/shard_map/ppermute | solution.py:798
  44.8 10.1 %collective-permute-start.7 = (f32[320,128]{1,0:T(8,128)S(1)}, f32[320,128]{1,0:T(8,128)S(1)}, u32[]{:S(2)}, u32[]{:S(2)}) collective-permute-start(f32[320,128]{1,0:T(8,128)S(1)} %get-tuple-element.62), channel_id=1, source_target_pairs={{0,4},{4,0},{8,12},{12,8},{16,20},{20,16},{24,28},{28,24},{32,36},... | collective-permute-start | bytes 491528 | tf_op jit(solution)/shard_map/ppermute | solution.py:798
  44.9 10.1 %collective-permute-start.8 = (f32[320,128]{1,0:T(8,128)S(1)}, f32[320,128]{1,0:T(8,128)S(1)}, u32[]{:S(2)}, u32[]{:S(2)}) collective-permute-start(f32[320,128]{1,0:T(8,128)S(1)} %get-tuple-element.63), channel_id=1, source_target_pairs={{0,124},{4,8},{8,4},{12,16},{16,12},{20,24},{24,20},{28,32},{32,28... | collective-permute-start | bytes 491528 | tf_op jit(solution)/shard_map/ppermute | solution.py:798
  57.7 11.2 %collective-permute-start.9 = (f32[85,8,128]{2,1,0:T(8,128)S(1)}, f32[85,8,128]{2,1,0:T(8,128)S(1)}, u32[]{:S(2)}, u32[]{:S(2)}) collective-permute-start(f32[85,8,128]{2,1,0:T(8,128)S(1)} %get-tuple-element.66), channel_id=1, source_target_pairs={{0,4},{4,0},{8,12},{12,8},{16,20},{20,16},{24,28},{28,24},{32,36},... | collective-permute-start | bytes 1044488 | tf_op jit(solution)/shard_map/ppermute | solution.py:798
  57.8 11.9 %collective-permute-start.10 = (f32[85,8,128]{2,1,0:T(8,128)S(1)}, f32[85,8,128]{2,1,0:T(8,128)S(1)}, u32[]{:S(2)}, u32[]{:S(2)}) collective-permute-start(f32[85,8,128]{2,1,0:T(8,128)S(1)} %get-tuple-element.67), channel_id=1, source_target_pairs={{0,124},{4,8},{8,4},{12,16},{16,12},{20,24},{24,20},{28,32},{32,28... | collective-permute-start | bytes 1044488 | tf_op jit(solution)/shard_map/ppermute | solution.py:798
  66.2 16.4 %collective-permute-start.11 = (f32[90,8,128]{2,1,0:T(8,128)S(1)}, f32[90,8,128]{2,1,0:T(8,128)S(1)}, u32[]{:S(2)}, u32[]{:S(2)}) collective-permute-start(f32[90,8,128]{2,1,0:T(8,128)S(1)} %get-tuple-element.72), channel_id=1, source_target_pairs={{0,4},{4,0},{8,12},{12,8},{16,20},{20,16},{24,28},{28,24},{32,36},... | collective-permute-start | bytes 1105928 | tf_op jit(solution)/shard_map/ppermute | solution.py:798
  66.3 16.3 %collective-permute-start.12 = (f32[90,8,128]{2,1,0:T(8,128)S(1)}, f32[90,8,128]{2,1,0:T(8,128)S(1)}, u32[]{:S(2)}, u32[]{:S(2)}) collective-permute-start(f32[90,8,128]{2,1,0:T(8,128)S(1)} %get-tuple-element.73), channel_id=1, source_target_pairs={{0,124},{4,8},{8,4},{12,16},{16,12},{20,24},{24,20},{28,32},{32,28... | collective-permute-start | bytes 1105928 | tf_op jit(solution)/shard_map/ppermute | solution.py:798
  75.4 14.3 %collective-permute-start.19 = (f32[48,4,256]{2,1,0:T(4,128)S(1)}, f32[48,4,256]{2,1,0:T(4,128)S(1)}, u32[]{:S(2)}, u32[]{:S(2)}) collective-permute-start(f32[48,4,256]{2,1,0:T(4,128)S(1)} %get-tuple-element.85), channel_id=1, source_target_pairs={{0,1},{1,0},{2,3},{3,2},{4,5},{5,4},{6,7},{7,6},{8,9},{9,8},{10,11... | collective-permute-start | bytes 589832 | tf_op jit(solution)/shard_map/ppermute | solution.py:801
  75.5 19.3 %collective-permute-start.20 = (f32[48,4,256]{2,1,0:T(4,128)S(1)}, f32[48,4,256]{2,1,0:T(4,128)S(1)}, u32[]{:S(2)}, u32[]{:S(2)}) collective-permute-start(f32[48,4,256]{2,1,0:T(4,128)S(1)} %get-tuple-element.86), channel_id=1, source_target_pairs={{0,2},{1,3},{2,0},{3,1},{4,6},{5,7},{6,4},{7,5},{8,10},{9,11},{10,... | collective-permute-start | bytes 589832 | tf_op jit(solution)/shard_map/ppermute | solution.py:801
  82.5 12.8 %collective-permute-start.21 = (f32[48,4,256]{2,1,0:T(4,128)S(1)}, f32[48,4,256]{2,1,0:T(4,128)S(1)}, u32[]{:S(2)}, u32[]{:S(2)}) collective-permute-start(f32[48,4,256]{2,1,0:T(4,128)S(1)} %get-tuple-element.87), channel_id=1, source_target_pairs={{0,3},{1,2},{2,1},{3,0},{4,7},{5,6},{6,5},{7,4},{8,11},{9,10},{10,... | collective-permute-start | bytes 589832 | tf_op jit(solution)/shard_map/ppermute | solution.py:801
  87.8 8.9 %collective-permute-start.16 = (f32[44,4,256]{2,1,0:T(4,128)S(1)}, f32[44,4,256]{2,1,0:T(4,128)S(1)}, u32[]{:S(2)}, u32[]{:S(2)}) collective-permute-start(f32[44,4,256]{2,1,0:T(4,128)S(1)} %get-tuple-element.82), channel_id=1, source_target_pairs={{0,1},{1,0},{2,3},{3,2},{4,5},{5,4},{6,7},{7,6},{8,9},{9,8},{10,11... | collective-permute-start | bytes 540680 | tf_op jit(solution)/shard_map/ppermute | solution.py:801
  88.2 15.2 %collective-permute-start.17 = (f32[44,4,256]{2,1,0:T(4,128)S(1)}, f32[44,4,256]{2,1,0:T(4,128)S(1)}, u32[]{:S(2)}, u32[]{:S(2)}) collective-permute-start(f32[44,4,256]{2,1,0:T(4,128)S(1)} %get-tuple-element.83), channel_id=1, source_target_pairs={{0,2},{1,3},{2,0},{3,1},{4,6},{5,7},{6,4},{7,5},{8,10},{9,11},{10,... | collective-permute-start | bytes 540680 | tf_op jit(solution)/shard_map/ppermute | solution.py:801
  89.7 13.8 %collective-permute-start.18 = (f32[44,4,256]{2,1,0:T(4,128)S(1)}, f32[44,4,256]{2,1,0:T(4,128)S(1)}, u32[]{:S(2)}, u32[]{:S(2)}) collective-permute-start(f32[44,4,256]{2,1,0:T(4,128)S(1)} %get-tuple-element.84), channel_id=1, source_target_pairs={{0,3},{1,2},{2,1},{3,0},{4,7},{5,6},{6,5},{7,4},{8,11},{9,10},{10,... | collective-permute-start | bytes 540680 | tf_op jit(solution)/shard_map/ppermute | solution.py:801
  94.8 10.0 %collective-permute-start.13 = (f32[40,4,256]{2,1,0:T(4,128)S(1)}, f32[40,4,256]{2,1,0:T(4,128)S(1)}, u32[]{:S(2)}, u32[]{:S(2)}) collective-permute-start(f32[40,4,256]{2,1,0:T(4,128)S(1)} %get-tuple-element.79), channel_id=1, source_target_pairs={{0,1},{1,0},{2,3},{3,2},{4,5},{5,4},{6,7},{7,6},{8,9},{9,8},{10,11... | collective-permute-start | bytes 491528 | tf_op jit(solution)/shard_map/ppermute | solution.py:801
  95.2 9.7 %collective-permute-start.14 = (f32[40,4,256]{2,1,0:T(4,128)S(1)}, f32[40,4,256]{2,1,0:T(4,128)S(1)}, u32[]{:S(2)}, u32[]{:S(2)}) collective-permute-start(f32[40,4,256]{2,1,0:T(4,128)S(1)} %get-tuple-element.80), channel_id=1, source_target_pairs={{0,2},{1,3},{2,0},{3,1},{4,6},{5,7},{6,4},{7,5},{8,10},{9,11},{10,... | collective-permute-start | bytes 491528 | tf_op jit(solution)/shard_map/ppermute | solution.py:801
  96.7 9.9 %collective-permute-start.15 = (f32[40,4,256]{2,1,0:T(4,128)S(1)}, f32[40,4,256]{2,1,0:T(4,128)S(1)}, u32[]{:S(2)}, u32[]{:S(2)}) collective-permute-start(f32[40,4,256]{2,1,0:T(4,128)S(1)} %get-tuple-element.81), channel_id=1, source_target_pairs={{0,3},{1,2},{2,1},{3,0},{4,7},{5,6},{6,5},{7,4},{8,11},{9,10},{10,... | collective-permute-start | bytes 491528 | tf_op jit(solution)/shard_map/ppermute | solution.py:801

commit v3 on v2

--- a/solution.py
+++ b/solution.py
@@ -15,12 +15,13 @@
 WET, UE, VN, VD = 4, 5, 6, 7
 KAPPA = 0.15
 MIB = 2**20
-UNROLL_S = 4
-UNROLL_L = 4
+UNROLL_S = 8
+UNROLL_L = 8
 UNROLL_M = 2
 
 CHUNKS = ((0, 24), (24, 64))
 PIECES = ((0, 0, 24), (1, 0, 22), (1, 22, 42))
+CARRIER = 0
 
 
 def iota(shape, dim):
@@ -80,7 +81,7 @@
 def thirds(tri, wet, vd, tiles, beside=None):
     zero = jnp.zeros((ROWS, LANES), F32)
 
-    def body(i, carry):
+    def one(i, carry):
         low, rat, low2, rat2 = ([], [], [], [])
         top, bottom = pair_of(i)
         for t in tiles:
@@ -108,8 +109,11 @@
             beside(i)
         return low, rat, low2, rat2
 
+    def body(m, carry):
+        return one(2 * m + 1, one(2 * m, carry))
+
     n = len(tiles)
-    lax.fori_loop(0, HALF, body, tuple([zero] * n for _ in range(4)))
+    lax.fori_loop(0, HALF // 2, body, tuple([zero] * n for _ in range(4)))
 
 
 def eliminate(rhs, put, get, tri, items, beside=None):
@@ -270,26 +274,26 @@
     return pltpu.roll(packed, (-(16 * g + 8)) % LANES, 1)
 
 
-def odd_tile(ids):
-    return lax.rem(ids[1], 2) == 1
-
-
-def turn(todd, x, y):
-    return jnp.where(todd, y, x), jnp.where(todd, x, y)
-
-
-def put_edges(todd, pick, fields, oa, ob):
+def even_tile(ids):
+    return lax.rem(ids[1], 2) == 0
+
+
+def turn(even, x, y):
+    return jnp.where(even, y, x), jnp.where(even, x, y)
+
+
+def put_edges(even, pick, fields, oa, ob):
     for f in range(fields):
         for t in range(2):
             for g in range(8):
                 n, s = pick(f, t, g)
                 at = pl.ds((f * 2 + t) * LEV + 8 * g, 8)
-                oa[at, :], ob[at, :] = turn(todd, n, s)
+                oa[at, :], ob[at, :] = turn(even, n, s)
         outer = [pick(f, 2, g) for g in range(8)]
         n = edge_pack([o[0] for o in outer])
         s = edge_pack([o[1] for o in outer])
         at = pl.ds(fields * 2 * LEV + 8 * f, 8)
-        oa[at, :], ob[at, :] = turn(todd, n, s)
+        oa[at, :], ob[at, :] = turn(even, n, s)
 
 
 def edge_rows(ref, g):
@@ -299,7 +303,7 @@
 
 
 def main_edges(ids, fld, ya, yb):
-    todd = odd_tile(ids)
+    even = even_tile(ids)
     for k, f in enumerate((0, 1, WET, 2, 3)):
         for t in range(2):
             for g in range(8):
@@ -307,13 +311,13 @@
                 if f == WET:
                     n = n * (KAPPA - 0.5 * edge_rows(fld.at[VN, t], g)[0])
                 at = pl.ds((2 * k + t) * LEV + 8 * g, 8)
-                ya[at, :], yb[at, :] = turn(todd, n, s)
+                ya[at, :], yb[at, :] = turn(even, n, s)
 
 
 def outer_edges(ids, xa, xb, ya_in, yb_in, ya, yb):
     face, tile = ids[0], ids[1]
     odd = lax.rem(face, 2) == 1
-    todd = odd_tile(ids)
+    even = even_tile(ids)
     for g in range(4):
         na, sa = edge_rows(xa, g)
         nb, sb = edge_rows(xb, g)
@@ -323,7 +327,7 @@
             n = jnp.where(inside, n, 0.0)
             s = jnp.where(inside, s, 0.0)
             at = pl.ds(OUTER + first + 8 * g, 8)
-            ya[at, :], yb[at, :] = turn(todd, n, s)
+            ya[at, :], yb[at, :] = turn(even, n, s)
 
 
 def local_weights(ids, w0, w1, w2, w3, wloc, pieces):
@@ -406,12 +410,12 @@
 
 
 def take_first_edges(ids, ya, yb, hn, hs, first):
-    todd = odd_tile(ids)
+    even = even_tile(ids)
     lane = iota((8, LANES), 1)
 
     def both(at):
         a, b = ya[at, :], yb[at, :]
-        return turn(todd, a, b)
+        return turn(even, a, b)
 
     for f, k in enumerate((0, 1, 2) if first else (3, 4)):
         for t in range(2):
@@ -440,15 +444,15 @@
 
 
 def take_edges(ids, load, hn, hs, groups=(0, 8)):
-    todd = odd_tile(ids)
+    even = even_tile(ids)
     for f in range(2):
         oa, ob = load(32 + f)
-        on, os = turn(todd, oa, ob)
+        on, os = turn(even, oa, ob)
         for g in range(*groups):
             at = pl.ds(8 * g, 8)
             for t in range(2):
                 a, b = load((f * 2 + t) * 8 + g)
-                hn[f, t, at, :], hs[f, t, at, :] = turn(todd, a, b)
+                hn[f, t, at, :], hs[f, t, at, :] = turn(even, a, b)
             hn[f, 2, at, :] = edge_unpack(on, g)
             hs[f, 2, at, :] = edge_unpack(os, g)
 
@@ -483,7 +487,7 @@
         wloc, cf, sol, oa, ob, fo, hn, hs = refs
     else:
         sol, oa, ob, fo, hn, hs = refs
-    todd = odd_tile(ids)
+    even = even_tile(ids)
     row = iota((ROWS, LANES), 0)
     take_first_edges(ids, ya, yb, hn, hs, first)
 
@@ -539,14 +543,14 @@
         y = get(v, pl.ds(0, ROWS))
         for t in range(3):
             fo[v, t] = y[t] + top[3 * v + t]
-    put_edges(todd, lambda f, t, g: edge_rows(sol.at[f, t], g), 2, oa, ob)
+    put_edges(even, lambda f, t, g: edge_rows(sol.at[f, t], g), 2, oa, ob)
     if first:
         for c in range(2):
             for t in range(3):
                 n = wloc[c, t, 8:16, :]
                 s = wloc[c, t, 0:8, :]
                 at = pl.ds(ROWS_2 + 8 * (3 * c + t), 8)
-                oa[at, :], ob[at, :] = turn(todd, n, s)
+                oa[at, :], ob[at, :] = turn(even, n, s)
 
 
 def last_stencil(v0, l0, nl, extra, carried, grads, *refs):
@@ -566,7 +570,7 @@
     else:
         adj_out, hn, hs, buf, sem = refs
     row = iota((ROWS, LANES), 0)
-    todd = odd_tile(ids)
+    even = even_tile(ids)
     low_half = iota((8, LANES), 0) < 4
 
     def load(block):
@@ -583,7 +587,7 @@
             n = jnp.where(low_half, pltpu.roll(a[8:16], 4, 0), b[8:16])
             s = jnp.where(low_half, a[0:8], pltpu.roll(b[0:8], 4, 0))
             if t < 2:
-                ga[2 * u + t], gb[2 * u + t] = turn(todd, n, s)
+                ga[2 * u + t], gb[2 * u + t] = turn(even, n, s)
             else:
                 en[u] = n
                 es[u] = s
@@ -632,7 +636,7 @@
                     mine = (lane >= 16 * j) & (lane < 16 * j + 16)
                     pn = jnp.where(mine, pltpu.roll(en[u], (16 * j + 8) % LANES, 1), pn)
                     ps = jnp.where(mine, pltpu.roll(es[u], (16 * j + 8) % LANES, 1), ps)
-            ga[2 * units + i], gb[2 * units + i] = turn(todd, pn, ps)
+            ga[2 * units + i], gb[2 * units + i] = turn(even, pn, ps)
         if carried:
             for i in range(BLOCKS_2):
                 ga[2 * units + per + i] = ua[pl.ds(8 * i, 8), :]
@@ -644,7 +648,7 @@
     del after
     zs = (z0, z1, z2, z3)
     face, tile = ids[0], ids[1]
-    todd = odd_tile(ids)
+    even = even_tile(ids)
     has_n, has_s = tile < 31, tile > 0
     sub = iota((8, LANES), 0)
     lane = iota((8, LANES), 1)
@@ -679,7 +683,7 @@
         for t in range(3):
             at = pl.ds(ROWS_2 + 8 * (3 * c + t), 8)
             a, b = ya[at, :], yb[at, :]
-            a, b = turn(todd, a, b)
+            a, b = turn(even, a, b)
             hi = jnp.where(has_n, a, 0.0)
             lo = jnp.where(has_s, b, 0.0)
             if c == 1:
@@ -712,7 +716,7 @@
     for u in range(u0, u1):
         j, i = divmod(u, per)
         a, b = ga[2 * units + i], gb[2 * units + i]
-        a, b = turn(todd, a, b)
+        a, b = turn(even, a, b)
         n = edge_unpack(a, j)
         s = edge_unpack(b, j)
         u -= u0
@@ -728,7 +732,7 @@
             hi, lo = [], []
             for t in range(2):
                 a, b = ga[2 * (u0 + u) + t], gb[2 * (u0 + u) + t]
-                a, b = turn(todd, a, b)
+                a, b = turn(even, a, b)
                 hi.append(jnp.where(has_n, a, 0.0))
                 lo.append(jnp.where(has_s, b, 0.0))
             hi.append(hn[u])
@@ -795,7 +799,7 @@
     hbm, any_space = pltpu.HBM, pl.ANY
 
     def across(a, b):
-        return lax.ppermute(a, "tile", pair_a), lax.ppermute(b, "tile", pair_b)
+        return lax.ppermute(a, "tile", pair_b), lax.ppermute(b, "tile", pair_a)
 
     def to_face(x, k):
         return lax.ppermute(x, "face", [(i, i ^ k) for i in range(4)])
@@ -870,7 +874,7 @@
         args = [ids, sol_t, cf, ta, tb] + fos
         blocks = 2 * units + per
         carried = 0
-        if l0 == 0:
+        if len(chunks) == CARRIER:
             args += [ua, ub]
             carried = blocks
             blocks += BLOCKS_2
@@ -902,9 +906,7 @@
             name="last_ts_%d" % l0,
         )(*args)
         ga, gb = across(ga, gb)
-        chunks.append((units, g, ga, gb))
-        if l0 == 0:
-            uv_rows = (carried, ga, gb)
+        chunks.append((units, g, ga, gb, carried))
 
     controls = None
     after = chunks[-1][1]
@@ -929,7 +931,7 @@
         return controls
 
     for c, u0, u1 in PIECES:
-        units, g, ga, gb = chunks[c]
+        units, g, ga, gb, _ = chunks[c]
         n = u1 - u0
         zs = call(
             functools.partial(smooth, units, u0, u1),
@@ -946,7 +948,7 @@
         after = zs[0]
         sent.append((first, 2 * n, [zs[0]] + [to_face(zs[k], k) for k in (1, 2, 3)]))
         first += 2 * n
-    carried, ga, gb = uv_rows
+    _, _, ga, gb, carried = chunks[CARRIER]
     (adj,) = call(
         functools.partial(last_stencil, 2, 0, LEV, 0, carried, False),
         [(adj_shape, any_space)],

time: 108 us -> 106 us (0.981)
  Pallas kernels: 60.7 us -> 56 us
  waiting for transfers between devices: 6.3 us -> 9.59 us
  starting transfers between devices: 40 us -> 38.9 us
    pallas_call x16, Pallas kernels: 60.7 us -> 56 us  [run(): pl.pallas_call(kernel, out_shape=[jax.ShapeDtypeStruct(s, F32) for s, _ i...]
    ppermute x8, waiting for transfers between devices: 0.84 us -> 3.81 us  [across(): return (lax.ppermute(a, 'tile', pair_b), lax.ppermute(b, 'tile', pair_a))]
    ppermute x12, starting transfers between devices: 15.1 us -> 13.4 us  [to_face(): return lax.ppermute(x, 'face', [(i, i ^ k) for i in range(4)])]
  transfers between devices with their start and end apart: 22 -> 22, of which waited for: 3 -> 5; matrix products, arithmetic and copies ran while one was open for 0% -> 0% of each run, Pallas kernels for 46% -> 44%
where the time goes in v3:
time: 106 us
  Pallas kernels  56 us (53%)
  starting transfers between devices  38.9 us (37%)
  waiting for transfers between devices  9.59 us (9%)
    pallas_call x16, Pallas kernels, run(): pl.pallas_call(kernel, out_shape=[jax.ShapeDtypeStruct(s, F32) for s, _ i...  56 us
    ppermute x8, starting transfers between devices, across(): return (lax.ppermute(a, 'tile', pair_b), lax.ppermute(b, 'tile', pair_a))  21.8 us
    ppermute x12, starting transfers between devices, to_face(): return lax.ppermute(x, 'face', [(i, i ^ k) for i in range(4)])  13.4 us
    ppermute x8, waiting for transfers between devices, across(): return (lax.ppermute(a, 'tile', pair_b), lax.ppermute(b, 'tile', pair_a))  3.81 us
    ppermute x1, waiting for transfers between devices, on_device(): xb = lax.ppermute(pxb, 'face', side_b)  3.45 us
    ppermute x1, starting transfers between devices, on_device(): xb = lax.ppermute(pxb, 'face', side_b)  3.44 us
    ppermute x12, waiting for transfers between devices, to_face(): return lax.ppermute(x, 'face', [(i, i ^ k) for i in range(4)])  2.34 us
  transfers between devices with their start and end apart: 22, of which 5 were waited for; matrix products, arithmetic and copies ran while one was open for 0% of the time, Pallas kernels for 44%

profile of v3, /device:TPU:1, one launch (start us, length us, event | category | flops | bytes accessed | tf_op | source)
XLA Modules:
  0.0 105.5 jit_solution(2341232617469098396)
XLA Ops:
  0.6 2.5 %collective-permute-start.1 = (f32[2,4,1024]{2,1,0:T(4,128)}, f32[2,4,1024]{2,1,0:T(4,128)S(1)}, u32[]{:S(2)}, u32[]{:S(2)}) collective-permute-start(f32[2,4,1024]{2,1,0:T(4,128)} %w0.1), channel_id=1, source_target_pairs={{0,2},{1,3},{2,0},{3,1},{4,6},{5,7},{6,4},{7,5},{8,10},{9,11},{10,... | collective-permute-start | bytes 98312 | tf_op jit(solution)/shard_map/ppermute | solution.py:805
  4.2 8.6 %first_solve.1 = (f32[8,2,1024,128]{3,2,1,0:T(8,128)S(1)}, f32[3,2,1024,128]{3,2,1,0:T(8,128)S(1)}, f32[512,128]{1,0:T(8,128)S(1)}, f32[512,128]{1,0:T(8,128)S(1)}) custom-call(s32[2]{0:T(128)S(1)} %pad_add_fusion.ids.refs_0_, f32[64,4,16,256]{3,2,1,0:T(8,128)} %seed.1, f32[2,64,16,256]{3,2,1,0:T(8,128)} %flow.1, f32[64,16,256]{2,1,0:T(8,128)} %vd.1, ...), custom_call_target="tpu_custom_call" | custom-call | tf_op jit(solution)/shard_map/first_solve/pallas_call | solution.py:57
  13.7 3.4 %collective-permute-start.4 = (f32[512,128]{1,0:T(8,128)S(1)}, f32[512,128]{1,0:T(8,128)S(1)}, u32[]{:S(2)}, u32[]{:S(2)}) collective-permute-start(f32[512,128]{1,0:T(8,128)S(1)} %get-tuple-element.49), channel_id=1, source_target_pairs={{0,0},{1,2},{2,1},{3,3},{4,4},{5,6},{6,5},{7,7},{8,8},{9,10},{10,9... | collective-permute-start | bytes 786440 | tf_op jit(solution)/shard_map/ppermute | solution.py:831
  17.9 3.4 %collective-permute-done.4.xb = f32[512,128]{1,0:T(8,128)S(1)} collective-permute-done((f32[512,128]{1,0:T(8,128)S(1)}, f32[512,128]{1,0:T(8,128)S(1)}, u32[]{:S(2)}, u32[]{:S(2)}) %collective-permute-start.4) | collective-permute-done | bytes 262176 | tf_op jit(solution)/shard_map/ppermute | solution.py:831
  21.9 8.6 %collective-permute-start.5 = (f32[704,128]{1,0:T(8,128)S(1)}, f32[704,128]{1,0:T(8,128)S(1)}, u32[]{:S(2)}, u32[]{:S(2)}) collective-permute-start(f32[704,128]{1,0:T(8,128)S(1)} %get-tuple-element.56), channel_id=1, source_target_pairs={{0,124},{4,8},{8,4},{12,16},{16,12},{20,24},{24,20},{28,32},{32,28... | collective-permute-start | bytes 1081352 | tf_op jit(solution)/shard_map/ppermute | solution.py:802
  30.6 6.0 %coefficients.1 = (f32[8,1024,128]{2,1,0:T(8,128)S(1)}, f32[5,3,1024,128]{3,2,1,0:T(8,128)S(1)}, f32[3,1,1024,128]{3,2,1,0:T(8,128)S(1)}) custom-call(s32[2]{0:T(128)S(1)} %pad_add_fusion.ids.refs_0_, f32[8,2,1024,128]{3,2,1,0:T(8,128)S(1)} %get-tuple-element.45.fld, f32[512,128]{1,0:T(8,128)S(1)} %collective-permute-done.3.xa, ...), custom_call_target="tpu_custom_call" | custom-call | tf_op jit(solution)/shard_map/coefficients/pallas_call | solution.py:57
  36.8 5.0 %step_ts.1 = (f32[5,3,1024,128]{3,2,1,0:T(8,128)S(1)}, f32[2,3,1024,128]{3,2,1,0:T(8,128)S(1)}, f32[320,128]{1,0:T(8,128)S(1)}, f32[320,128]{1,0:T(8,128)S(1)}, f32[2,3,16,128]{3,2,1,0:T(8,128)S(1)}) custom-call(s32[2]{0:T(128)S(1)} %pad_add_fusion.ids.refs_0_, f32[8,2,1024,128]{3,2,1,0:T(8,128)S(1)} %get-tuple-element.45.fld, ...), custom_call_target="tpu_custom_call", output_to_operand_aliasing={{0}: (3, {})} | custom-call | tf_op jit(solution)/shard_map/step_ts/pallas_call | solution.py:57
  41.8 5.8 %collective-permute-start.7 = (f32[320,128]{1,0:T(8,128)S(1)}, f32[320,128]{1,0:T(8,128)S(1)}, u32[]{:S(2)}, u32[]{:S(2)}) collective-permute-start(f32[320,128]{1,0:T(8,128)S(1)} %get-tuple-element.62), channel_id=1, source_target_pairs={{0,124},{4,8},{8,4},{12,16},{16,12},{20,24},{24,20},{28,32},{32,28... | collective-permute-start | bytes 491528 | tf_op jit(solution)/shard_map/ppermute | solution.py:802
  47.6 4.6 %step_uv.1 = (f32[2,3,1024,128]{3,2,1,0:T(8,128)S(1)}, f32[272,128]{1,0:T(8,128)S(1)}, f32[272,128]{1,0:T(8,128)S(1)}, f32[2,3,16,128]{3,2,1,0:T(8,128)S(1)}) custom-call(s32[2]{0:T(128)S(1)} %pad_add_fusion.ids.refs_0_, f32[8,2,1024,128]{3,2,1,0:T(8,128)S(1)} %get-tuple-element.45.fld, f32[8,1024,128]{2,1,0:T(8,128)S(1)} %get-tuple-element.50.fe, ...), custom_call_target="tpu_custom_call" | custom-call | tf_op jit(solution)/shard_map/step_uv/pallas_call | solution.py:57
  52.2 2.5 %last_ts_0.1 = (f32[64,4,16,256]{3,2,1,0:T(8,128)}, f32[24,2,3,16,128]{4,3,2,1,0:T(8,128)S(1)}, f32[85,8,128]{2,1,0:T(8,128)S(1)}, f32[85,8,128]{2,1,0:T(8,128)S(1)}) custom-call(s32[2]{0:T(128)S(1)} %pad_add_fusion.ids.refs_0_, f32[2,3,1024,128]{3,2,1,0:T(8,128)S(1)} %get-tuple-element.61.refs_1_, f32[5,3,1024,128]{3,2,1,0:T(8,128)S(1)} %get-tuple-element.59.cfi.refs_2_, ...), custom_call_target="tpu_custom_call" | custom-call | tf_op jit(solution)/shard_map/last_ts_0/pallas_call | solution.py:57
  54.7 5.4 %collective-permute-start.9 = (f32[85,8,128]{2,1,0:T(8,128)S(1)}, f32[85,8,128]{2,1,0:T(8,128)S(1)}, u32[]{:S(2)}, u32[]{:S(2)}) collective-permute-start(f32[85,8,128]{2,1,0:T(8,128)S(1)} %get-tuple-element.66), channel_id=1, source_target_pairs={{0,124},{4,8},{8,4},{12,16},{16,12},{20,24},{24,20},{28,32},{32,28... | collective-permute-start | bytes 1044488 | tf_op jit(solution)/shard_map/ppermute | solution.py:802
  60.1 3.3 %last_ts_24.1 = (f32[64,4,16,256]{3,2,1,0:T(8,128)}, f32[42,2,3,16,128]{4,3,2,1,0:T(8,128)S(1)}, f32[90,8,128]{2,1,0:T(8,128)S(1)}, f32[90,8,128]{2,1,0:T(8,128)S(1)}) custom-call(s32[2]{0:T(128)S(1)} %pad_add_fusion.ids.refs_0_, f32[2,3,1024,128]{3,2,1,0:T(8,128)S(1)} %get-tuple-element.61.refs_1_, ...), custom_call_target="tpu_custom_call", output_to_operand_aliasing={{0}: (7, {})} | custom-call | tf_op jit(solution)/shard_map/last_ts_24/pallas_call | solution.py:57
  63.4 2.0 %collective-permute-start.11 = (f32[90,8,128]{2,1,0:T(8,128)S(1)}, f32[90,8,128]{2,1,0:T(8,128)S(1)}, u32[]{:S(2)}, u32[]{:S(2)}) collective-permute-start(f32[90,8,128]{2,1,0:T(8,128)S(1)} %get-tuple-element.72), channel_id=1, source_target_pairs={{0,124},{4,8},{8,4},{12,16},{16,12},{20,24},{24,20},{28,32},{32,28... | collective-permute-start | bytes 1105928 | tf_op jit(solution)/shard_map/ppermute | solution.py:802
  66.7 2.2 %collective-permute-done.10.gb.refs_4_ = f32[85,8,128]{2,1,0:T(8,128)S(1)} collective-permute-done((f32[85,8,128]{2,1,0:T(8,128)S(1)}, f32[85,8,128]{2,1,0:T(8,128)S(1)}, u32[]{:S(2)}, u32[]{:S(2)}) %collective-permute-start.10) | collective-permute-done | bytes 348192 | tf_op jit(solution)/shard_map/ppermute | solution.py:802
  68.9 5.7 %smooth_0_0.1 = (f32[48,4,256]{2,1,0:T(4,128)S(1)}, f32[48,4,256]{2,1,0:T(4,128)S(1)}, f32[48,4,256]{2,1,0:T(4,128)S(1)}, f32[48,4,256]{2,1,0:T(4,128)S(1)}) custom-call(s32[2]{0:T(128)S(1)} %pad_add_fusion.ids.refs_0_, f32[24,2,3,16,128]{4,3,2,1,0:T(8,128)S(1)} %get-tuple-element.74.g, f32[85,8,128]{2,1,0:T(8,128)S(1)} %collective-permute-done.9.ga.refs_3_, ...), custom_call_target="tpu_custom_call" | custom-call | tf_op jit(solution)/shard_map/smooth_0_0/pallas_call | solution.py:57
  74.7 5.3 %collective-permute-start.20 = (f32[48,4,256]{2,1,0:T(4,128)S(1)}, f32[48,4,256]{2,1,0:T(4,128)S(1)}, u32[]{:S(2)}, u32[]{:S(2)}) collective-permute-start(f32[48,4,256]{2,1,0:T(4,128)S(1)} %get-tuple-element.86), channel_id=1, source_target_pairs={{0,2},{1,3},{2,0},{3,1},{4,6},{5,7},{6,4},{7,5},{8,10},{9,11},{10,... | collective-permute-start | bytes 589832 | tf_op jit(solution)/shard_map/ppermute | solution.py:805
  80.0 5.2 %smooth_1_0.1 = (f32[44,4,256]{2,1,0:T(4,128)S(1)}, f32[44,4,256]{2,1,0:T(4,128)S(1)}, f32[44,4,256]{2,1,0:T(4,128)S(1)}, f32[44,4,256]{2,1,0:T(4,128)S(1)}) custom-call(s32[2]{0:T(128)S(1)} %pad_add_fusion.ids.refs_0_, f32[42,2,3,16,128]{4,3,2,1,0:T(8,128)S(1)} %get-tuple-element.71.after.g, f32[90,8,128]{2,1,0:T(8,128)S(1)} %collective-permute-done.11.ga, ...), custom_call_target="tpu_custom_call" | custom-call | tf_op jit(solution)/shard_map/smooth_1_0/pallas_call | solution.py:57
  85.7 1.4 %collective-permute-start.17 = (f32[44,4,256]{2,1,0:T(4,128)S(1)}, f32[44,4,256]{2,1,0:T(4,128)S(1)}, u32[]{:S(2)}, u32[]{:S(2)}) collective-permute-start(f32[44,4,256]{2,1,0:T(4,128)S(1)} %get-tuple-element.83), channel_id=1, source_target_pairs={{0,2},{1,3},{2,0},{3,1},{4,6},{5,7},{6,4},{7,5},{8,10},{9,11},{10,... | collective-permute-start | bytes 540680 | tf_op jit(solution)/shard_map/ppermute | solution.py:805
  87.5 4.8 %smooth_1_22.1 = (f32[40,4,256]{2,1,0:T(4,128)S(1)}, f32[40,4,256]{2,1,0:T(4,128)S(1)}, f32[40,4,256]{2,1,0:T(4,128)S(1)}, f32[40,4,256]{2,1,0:T(4,128)S(1)}) custom-call(s32[2]{0:T(128)S(1)} %pad_add_fusion.ids.refs_0_, f32[42,2,3,16,128]{4,3,2,1,0:T(8,128)S(1)} %get-tuple-element.71.after.g, f32[90,8,128]{2,1,0:T(8,128)S(1)} %collective-permute-done.11.ga, ...), custom_call_target="tpu_custom_call" | custom-call | tf_op jit(solution)/shard_map/smooth_1_22/pallas_call | solution.py:57
  92.7 1.4 %collective-permute-start.14 = (f32[40,4,256]{2,1,0:T(4,128)S(1)}, f32[40,4,256]{2,1,0:T(4,128)S(1)}, u32[]{:S(2)}, u32[]{:S(2)}) collective-permute-start(f32[40,4,256]{2,1,0:T(4,128)S(1)} %get-tuple-element.80), channel_id=1, source_target_pairs={{0,2},{1,3},{2,0},{3,1},{4,6},{5,7},{6,4},{7,5},{8,10},{9,11},{10,... | collective-permute-start | bytes 491528 | tf_op jit(solution)/shard_map/ppermute | solution.py:805
  94.6 4.3 %last_uv.1 = f32[64,4,16,256]{3,2,1,0:T(8,128)} custom-call(s32[2]{0:T(128)S(1)} %pad_add_fusion.ids.refs_0_, f32[2,3,1024,128]{3,2,1,0:T(8,128)S(1)} %get-tuple-element.60.refs_1_, f32[5,3,1024,128]{3,2,1,0:T(8,128)S(1)} %get-tuple-element.59.cfi.refs_2_, f32[85,8,128]{2,1,0:T(8,128)S(1)} %collective-permute-done.9.ga.refs_3_, ...), custom_call_target="tpu_custom_call", output_to_operand_aliasing={{}: (6, {})} | custom-call | tf_op jit(solution)/shard_map/last_uv/pallas_call | solution.py:57
  98.8 1.5 %gather_0.1.refs_0_ = f32[132,4,1024]{2,1,0:T(4,128)} custom-call(s32[2]{0:T(128)S(1)} %pad_add_fusion.ids.refs_0_, f32[48,4,256]{2,1,0:T(4,128)S(1)} %get-tuple-element.75.after.z0, f32[48,4,256]{2,1,0:T(4,128)S(1)} %collective-permute-done.19.z1, f32[48,4,256]{2,1,0:T(4,128)S(1)} %collective-permute-done.20.z2, f32[48,4,256]{2,1,0:T(4,128)S(1)} %collective-permute-done.21.z3), custom_call_target="tpu_custom_call" | custom-call | tf_op jit(solution)/shard_map/gather_0/pallas_call | solution.py:57
  100.3 1.4 %gather_48.1.refs_0_ = f32[132,4,1024]{2,1,0:T(4,128)} custom-call(s32[2]{0:T(128)S(1)} %pad_add_fusion.ids.refs_0_, f32[44,4,256]{2,1,0:T(4,128)S(1)} %get-tuple-element.76.after.z0, f32[44,4,256]{2,1,0:T(4,128)S(1)} %collective-permute-done.16.z1, f32[44,4,256]{2,1,0:T(4,128)S(1)} %collective-permute-done.17.z2, ...), custom_call_target="tpu_custom_call", output_to_operand_aliasing={{}: (5, {})} | custom-call | tf_op jit(solution)/shard_map/gather_48/pallas_call | solution.py:57
  101.8 2.3 %collective-permute-done.15.z3 = f32[40,4,256]{2,1,0:T(4,128)S(1)} collective-permute-done((f32[40,4,256]{2,1,0:T(4,128)S(1)}, f32[40,4,256]{2,1,0:T(4,128)S(1)}, u32[]{:S(2)}, u32[]{:S(2)}) %collective-permute-start.15) | collective-permute-done | bytes 163872 | tf_op jit(solution)/shard_map/ppermute | solution.py:805
  (39 shorter events, 8.0 us)
Async XLA Ops:
  0.6 12.1 %collective-permute-start.1 = (f32[2,4,1024]{2,1,0:T(4,128)}, f32[2,4,1024]{2,1,0:T(4,128)S(1)}, u32[]{:S(2)}, u32[]{:S(2)}) collective-permute-start(f32[2,4,1024]{2,1,0:T(4,128)} %w0.1), channel_id=1, source_target_pairs={{0,2},{1,3},{2,0},{3,1},{4,6},{5,7},{6,4},{7,5},{8,10},{9,11},{10,... | collective-permute-start | bytes 98312 | tf_op jit(solution)/shard_map/ppermute | solution.py:805
  3.2 9.6 %collective-permute-start = (f32[2,4,1024]{2,1,0:T(4,128)}, f32[2,4,1024]{2,1,0:T(4,128)S(1)}, u32[]{:S(2)}, u32[]{:S(2)}) collective-permute-start(f32[2,4,1024]{2,1,0:T(4,128)} %w0.1), channel_id=1, source_target_pairs={{0,1},{1,0},{2,3},{3,2},{4,5},{5,4},{6,7},{7,6},{8,9},{9,8},{10,11... | collective-permute-start | bytes 98312 | tf_op jit(solution)/shard_map/ppermute | solution.py:805
  4.1 8.7 %collective-permute-start.2 = (f32[2,4,1024]{2,1,0:T(4,128)}, f32[2,4,1024]{2,1,0:T(4,128)S(1)}, u32[]{:S(2)}, u32[]{:S(2)}) collective-permute-start(f32[2,4,1024]{2,1,0:T(4,128)} %w0.1), channel_id=1, source_target_pairs={{0,3},{1,2},{2,1},{3,0},{4,7},{5,6},{6,5},{7,4},{8,11},{9,10},{10,... | collective-permute-start | bytes 98312 | tf_op jit(solution)/shard_map/ppermute | solution.py:805
  4.2 8.6 %copy-start = (f32[2,4,1024]{2,1,0:T(4,128)S(1)}, f32[2,4,1024]{2,1,0:T(4,128)}, u32[]{:S(2)}) copy-start(f32[2,4,1024]{2,1,0:T(4,128)} %w0.1) | copy-start | bytes 98308
  13.4 4.5 %collective-permute-start.3 = (f32[512,128]{1,0:T(8,128)S(1)}, f32[512,128]{1,0:T(8,128)S(1)}, u32[]{:S(2)}, u32[]{:S(2)}) collective-permute-start(f32[512,128]{1,0:T(8,128)S(1)} %get-tuple-element.48), channel_id=1, source_target_pairs={{0,1},{1,0},{2,3},{3,2},{4,5},{5,4},{6,7},{7,6},{8,9},{9,8},{10,11... | collective-permute-start | bytes 786440 | tf_op jit(solution)/shard_map/ppermute | solution.py:830
  13.7 7.7 %collective-permute-start.4 = (f32[512,128]{1,0:T(8,128)S(1)}, f32[512,128]{1,0:T(8,128)S(1)}, u32[]{:S(2)}, u32[]{:S(2)}) collective-permute-start(f32[512,128]{1,0:T(8,128)S(1)} %get-tuple-element.49), channel_id=1, source_target_pairs={{0,0},{1,2},{2,1},{3,3},{4,4},{5,6},{6,5},{7,7},{8,8},{9,10},{10,9... | collective-permute-start | bytes 786440 | tf_op jit(solution)/shard_map/ppermute | solution.py:831
  21.9 14.6 %collective-permute-start.5 = (f32[704,128]{1,0:T(8,128)S(1)}, f32[704,128]{1,0:T(8,128)S(1)}, u32[]{:S(2)}, u32[]{:S(2)}) collective-permute-start(f32[704,128]{1,0:T(8,128)S(1)} %get-tuple-element.56), channel_id=1, source_target_pairs={{0,124},{4,8},{8,4},{12,16},{16,12},{20,24},{24,20},{28,32},{32,28... | collective-permute-start | bytes 1081352 | tf_op jit(solution)/shard_map/ppermute | solution.py:802
  30.6 6.3 %collective-permute-start.6 = (f32[704,128]{1,0:T(8,128)S(1)}, f32[704,128]{1,0:T(8,128)S(1)}, u32[]{:S(2)}, u32[]{:S(2)}) collective-permute-start(f32[704,128]{1,0:T(8,128)S(1)} %get-tuple-element.57), channel_id=1, source_target_pairs={{0,4},{4,0},{8,12},{12,8},{16,20},{20,16},{24,28},{28,24},{32,36},... | collective-permute-start | bytes 1081352 | tf_op jit(solution)/shard_map/ppermute | solution.py:802
  41.8 10.4 %collective-permute-start.7 = (f32[320,128]{1,0:T(8,128)S(1)}, f32[320,128]{1,0:T(8,128)S(1)}, u32[]{:S(2)}, u32[]{:S(2)}) collective-permute-start(f32[320,128]{1,0:T(8,128)S(1)} %get-tuple-element.62), channel_id=1, source_target_pairs={{0,124},{4,8},{8,4},{12,16},{16,12},{20,24},{24,20},{28,32},{32,28... | collective-permute-start | bytes 491528 | tf_op jit(solution)/shard_map/ppermute | solution.py:802
  47.6 4.6 %collective-permute-start.8 = (f32[320,128]{1,0:T(8,128)S(1)}, f32[320,128]{1,0:T(8,128)S(1)}, u32[]{:S(2)}, u32[]{:S(2)}) collective-permute-start(f32[320,128]{1,0:T(8,128)S(1)} %get-tuple-element.63), channel_id=1, source_target_pairs={{0,4},{4,0},{8,12},{12,8},{16,20},{20,16},{24,28},{28,24},{32,36},... | collective-permute-start | bytes 491528 | tf_op jit(solution)/shard_map/ppermute | solution.py:802
  54.7 11.9 %collective-permute-start.9 = (f32[85,8,128]{2,1,0:T(8,128)S(1)}, f32[85,8,128]{2,1,0:T(8,128)S(1)}, u32[]{:S(2)}, u32[]{:S(2)}) collective-permute-start(f32[85,8,128]{2,1,0:T(8,128)S(1)} %get-tuple-element.66), channel_id=1, source_target_pairs={{0,124},{4,8},{8,4},{12,16},{16,12},{20,24},{24,20},{28,32},{32,28... | collective-permute-start | bytes 1044488 | tf_op jit(solution)/shard_map/ppermute | solution.py:802
  60.1 8.8 %collective-permute-start.10 = (f32[85,8,128]{2,1,0:T(8,128)S(1)}, f32[85,8,128]{2,1,0:T(8,128)S(1)}, u32[]{:S(2)}, u32[]{:S(2)}) collective-permute-start(f32[85,8,128]{2,1,0:T(8,128)S(1)} %get-tuple-element.67), channel_id=1, source_target_pairs={{0,4},{4,0},{8,12},{12,8},{16,20},{20,16},{24,28},{28,24},{32,36},... | collective-permute-start | bytes 1044488 | tf_op jit(solution)/shard_map/ppermute | solution.py:802
  63.4 16.6 %collective-permute-start.11 = (f32[90,8,128]{2,1,0:T(8,128)S(1)}, f32[90,8,128]{2,1,0:T(8,128)S(1)}, u32[]{:S(2)}, u32[]{:S(2)}) collective-permute-start(f32[90,8,128]{2,1,0:T(8,128)S(1)} %get-tuple-element.72), channel_id=1, source_target_pairs={{0,124},{4,8},{8,4},{12,16},{16,12},{20,24},{24,20},{28,32},{32,28... | collective-permute-start | bytes 1105928 | tf_op jit(solution)/shard_map/ppermute | solution.py:802
  65.4 14.7 %collective-permute-start.12 = (f32[90,8,128]{2,1,0:T(8,128)S(1)}, f32[90,8,128]{2,1,0:T(8,128)S(1)}, u32[]{:S(2)}, u32[]{:S(2)}) collective-permute-start(f32[90,8,128]{2,1,0:T(8,128)S(1)} %get-tuple-element.73), channel_id=1, source_target_pairs={{0,4},{4,0},{8,12},{12,8},{16,20},{20,16},{24,28},{28,24},{32,36},... | collective-permute-start | bytes 1105928 | tf_op jit(solution)/shard_map/ppermute | solution.py:802
  74.6 12.6 %collective-permute-start.19 = (f32[48,4,256]{2,1,0:T(4,128)S(1)}, f32[48,4,256]{2,1,0:T(4,128)S(1)}, u32[]{:S(2)}, u32[]{:S(2)}) collective-permute-start(f32[48,4,256]{2,1,0:T(4,128)S(1)} %get-tuple-element.85), channel_id=1, source_target_pairs={{0,1},{1,0},{2,3},{3,2},{4,5},{5,4},{6,7},{7,6},{8,9},{9,8},{10,11... | collective-permute-start | bytes 589832 | tf_op jit(solution)/shard_map/ppermute | solution.py:805
  74.7 17.7 %collective-permute-start.20 = (f32[48,4,256]{2,1,0:T(4,128)S(1)}, f32[48,4,256]{2,1,0:T(4,128)S(1)}, u32[]{:S(2)}, u32[]{:S(2)}) collective-permute-start(f32[48,4,256]{2,1,0:T(4,128)S(1)} %get-tuple-element.86), channel_id=1, source_target_pairs={{0,2},{1,3},{2,0},{3,1},{4,6},{5,7},{6,4},{7,5},{8,10},{9,11},{10,... | collective-permute-start | bytes 589832 | tf_op jit(solution)/shard_map/ppermute | solution.py:805
  80.0 12.8 %collective-permute-start.21 = (f32[48,4,256]{2,1,0:T(4,128)S(1)}, f32[48,4,256]{2,1,0:T(4,128)S(1)}, u32[]{:S(2)}, u32[]{:S(2)}) collective-permute-start(f32[48,4,256]{2,1,0:T(4,128)S(1)} %get-tuple-element.87), channel_id=1, source_target_pairs={{0,3},{1,2},{2,1},{3,0},{4,7},{5,6},{6,5},{7,4},{8,11},{9,10},{10,... | collective-permute-start | bytes 589832 | tf_op jit(solution)/shard_map/ppermute | solution.py:805
  85.3 8.9 %collective-permute-start.16 = (f32[44,4,256]{2,1,0:T(4,128)S(1)}, f32[44,4,256]{2,1,0:T(4,128)S(1)}, u32[]{:S(2)}, u32[]{:S(2)}) collective-permute-start(f32[44,4,256]{2,1,0:T(4,128)S(1)} %get-tuple-element.82), channel_id=1, source_target_pairs={{0,1},{1,0},{2,3},{3,2},{4,5},{5,4},{6,7},{7,6},{8,9},{9,8},{10,11... | collective-permute-start | bytes 540680 | tf_op jit(solution)/shard_map/ppermute | solution.py:805
  85.7 14.6 %collective-permute-start.17 = (f32[44,4,256]{2,1,0:T(4,128)S(1)}, f32[44,4,256]{2,1,0:T(4,128)S(1)}, u32[]{:S(2)}, u32[]{:S(2)}) collective-permute-start(f32[44,4,256]{2,1,0:T(4,128)S(1)} %get-tuple-element.83), channel_id=1, source_target_pairs={{0,2},{1,3},{2,0},{3,1},{4,6},{5,7},{6,4},{7,5},{8,10},{9,11},{10,... | collective-permute-start | bytes 540680 | tf_op jit(solution)/shard_map/ppermute | solution.py:805
  87.2 13.1 %collective-permute-start.18 = (f32[44,4,256]{2,1,0:T(4,128)S(1)}, f32[44,4,256]{2,1,0:T(4,128)S(1)}, u32[]{:S(2)}, u32[]{:S(2)}) collective-permute-start(f32[44,4,256]{2,1,0:T(4,128)S(1)} %get-tuple-element.84), channel_id=1, source_target_pairs={{0,3},{1,2},{2,1},{3,0},{4,7},{5,6},{6,5},{7,4},{8,11},{9,10},{10,... | collective-permute-start | bytes 540680 | tf_op jit(solution)/shard_map/ppermute | solution.py:805
  92.4 9.4 %collective-permute-start.13 = (f32[40,4,256]{2,1,0:T(4,128)S(1)}, f32[40,4,256]{2,1,0:T(4,128)S(1)}, u32[]{:S(2)}, u32[]{:S(2)}) collective-permute-start(f32[40,4,256]{2,1,0:T(4,128)S(1)} %get-tuple-element.79), channel_id=1, source_target_pairs={{0,1},{1,0},{2,3},{3,2},{4,5},{5,4},{6,7},{7,6},{8,9},{9,8},{10,11... | collective-permute-start | bytes 491528 | tf_op jit(solution)/shard_map/ppermute | solution.py:805
  92.7 9.1 %collective-permute-start.14 = (f32[40,4,256]{2,1,0:T(4,128)S(1)}, f32[40,4,256]{2,1,0:T(4,128)S(1)}, u32[]{:S(2)}, u32[]{:S(2)}) collective-permute-start(f32[40,4,256]{2,1,0:T(4,128)S(1)} %get-tuple-element.80), channel_id=1, source_target_pairs={{0,2},{1,3},{2,0},{3,1},{4,6},{5,7},{6,4},{7,5},{8,10},{9,11},{10,... | collective-permute-start | bytes 491528 | tf_op jit(solution)/shard_map/ppermute | solution.py:805
  94.2 9.9 %collective-permute-start.15 = (f32[40,4,256]{2,1,0:T(4,128)S(1)}, f32[40,4,256]{2,1,0:T(4,128)S(1)}, u32[]{:S(2)}, u32[]{:S(2)}) collective-permute-start(f32[40,4,256]{2,1,0:T(4,128)S(1)} %get-tuple-element.81), channel_id=1, source_target_pairs={{0,3},{1,2},{2,1},{3,0},{4,7},{5,6},{6,5},{7,4},{8,11},{9,10},{10,... | collective-permute-start | bytes 491528 | tf_op jit(solution)/shard_map/ppermute | solution.py:805

commit v4 on v3

--- a/solution.py
+++ b/solution.py
@@ -793,13 +793,20 @@
     ids = jnp.stack([lax.axis_index("face"), lax.axis_index("tile")]).astype(jnp.int32)
     tiles = lax.axis_size("tile")
     pair_a = [(i, i ^ 1) for i in range(tiles)]
-    pair_b = [(i, (i + (1 if i % 2 else -1)) % tiles) for i in range(tiles)]
+    pair_b = []
+    for t in range(tiles):
+        for f in range(4):
+            if t in (0, tiles - 1):
+                partner = 4 * t + (f ^ 1)
+            else:
+                partner = 4 * (t + 1 if t % 2 else t - 1) + f
+            pair_b.append((4 * t + f, partner))
     side_a = [(0, 1), (1, 0), (2, 3), (3, 2)]
     side_b = [(0, 0), (1, 2), (2, 1), (3, 3)]
     hbm, any_space = pltpu.HBM, pl.ANY
 
     def across(a, b):
-        return lax.ppermute(a, "tile", pair_b), lax.ppermute(b, "tile", pair_a)
+        return lax.ppermute(a, ("tile", "face"), pair_b), lax.ppermute(b, "tile", pair_a)
 
     def to_face(x, k):
         return lax.ppermute(x, "face", [(i, i ^ k) for i in range(4)])

time: 106 us -> 102 us (0.962)
  the two profiles are of different devices: /device:TPU:1 before, /device:TPU:97 now
where the time goes in v4:
time: 102 us
  Pallas kernels  56 us (55%)
  starting transfers between devices  40.2 us (39%)
  waiting for transfers between devices  4.98 us (5%)
    pallas_call x16, Pallas kernels, run(): pl.pallas_call(kernel, out_shape=[jax.ShapeDtypeStruct(s, F32) for s, _ i...  56 us
    ppermute x12, starting transfers between devices, to_face(): return lax.ppermute(x, 'face', [(i, i ^ k) for i in range(4)])  21.6 us
    ppermute x4, starting transfers between devices, across(): lax.ppermute(a, ('tile', 'face'), pair_b)  17.3 us
    ppermute x4, waiting for transfers between devices, across(): lax.ppermute(a, ('tile', 'face'), pair_b)  2.8 us
    ppermute x12, waiting for transfers between devices, to_face(): return lax.ppermute(x, 'face', [(i, i ^ k) for i in range(4)])  2.16 us
  transfers between devices with their start and end apart: 22, of which 4 were waited for; matrix products, arithmetic and copies ran while one was open for 0% of the time, Pallas kernels for 45%

profile of v4, /device:TPU:97, one launch (start us, length us, event | category | flops | bytes accessed | tf_op | source)
XLA Modules:
  0.0 102.2 jit_solution(9639324423149683961)
XLA Ops:
  1.8 1.2 %collective-permute-start.2 = (f32[2,4,1024]{2,1,0:T(4,128)}, f32[2,4,1024]{2,1,0:T(4,128)S(1)}, u32[]{:S(2)}, u32[]{:S(2)}) collective-permute-start(f32[2,4,1024]{2,1,0:T(4,128)} %w0.1), channel_id=1, source_target_pairs={{0,3},{1,2},{2,1},{3,0},{4,7},{5,6},{6,5},{7,4},{8,11},{9,10},{10,... | collective-permute-start | bytes 98312 | tf_op jit(solution)/shard_map/ppermute | solution.py:812
  3.1 8.6 %first_solve.1 = (f32[8,2,1024,128]{3,2,1,0:T(8,128)S(1)}, f32[3,2,1024,128]{3,2,1,0:T(8,128)S(1)}, f32[512,128]{1,0:T(8,128)S(1)}, f32[512,128]{1,0:T(8,128)S(1)}) custom-call(s32[2]{0:T(128)S(1)} %pad_add_fusion.ids.refs_0_, f32[64,4,16,256]{3,2,1,0:T(8,128)} %seed.1, f32[2,64,16,256]{3,2,1,0:T(8,128)} %flow.1, f32[64,16,256]{2,1,0:T(8,128)} %vd.1, ...), custom_call_target="tpu_custom_call" | custom-call | tf_op jit(solution)/shard_map/first_solve/pallas_call | solution.py:57
  14.9 5.0 %collective-permute-start.5 = (f32[704,128]{1,0:T(8,128)S(1)}, f32[704,128]{1,0:T(8,128)S(1)}, u32[]{:S(2)}, u32[]{:S(2)}) collective-permute-start(f32[704,128]{1,0:T(8,128)S(1)} %get-tuple-element.56), channel_id=1, source_target_pairs={{0,1},{1,0},{2,3},{3,2},{4,8},{5,9},{6,10},{7,11},{8,4},{9,5},{10,... | collective-permute-start | bytes 1081352 | tf_op jit(solution)/shard_map/ppermute | solution.py:809
  19.9 6.0 %coefficients.1 = (f32[8,1024,128]{2,1,0:T(8,128)S(1)}, f32[5,3,1024,128]{3,2,1,0:T(8,128)S(1)}, f32[3,1,1024,128]{3,2,1,0:T(8,128)S(1)}) custom-call(s32[2]{0:T(128)S(1)} %pad_add_fusion.ids.refs_0_, f32[8,2,1024,128]{3,2,1,0:T(8,128)S(1)} %get-tuple-element.45.fld, f32[512,128]{1,0:T(8,128)S(1)} %collective-permute-done.3.xa, ...), custom_call_target="tpu_custom_call" | custom-call | tf_op jit(solution)/shard_map/coefficients/pallas_call | solution.py:57
  27.0 5.0 %step_ts.1 = (f32[5,3,1024,128]{3,2,1,0:T(8,128)S(1)}, f32[2,3,1024,128]{3,2,1,0:T(8,128)S(1)}, f32[320,128]{1,0:T(8,128)S(1)}, f32[320,128]{1,0:T(8,128)S(1)}, f32[2,3,16,128]{3,2,1,0:T(8,128)S(1)}) custom-call(s32[2]{0:T(128)S(1)} %pad_add_fusion.ids.refs_0_, f32[8,2,1024,128]{3,2,1,0:T(8,128)S(1)} %get-tuple-element.45.fld, ...), custom_call_target="tpu_custom_call", output_to_operand_aliasing={{0}: (3, {})} | custom-call | tf_op jit(solution)/shard_map/step_ts/pallas_call | solution.py:57
  32.0 5.0 %collective-permute-start.7 = (f32[320,128]{1,0:T(8,128)S(1)}, f32[320,128]{1,0:T(8,128)S(1)}, u32[]{:S(2)}, u32[]{:S(2)}) collective-permute-start(f32[320,128]{1,0:T(8,128)S(1)} %get-tuple-element.62), channel_id=1, source_target_pairs={{0,1},{1,0},{2,3},{3,2},{4,8},{5,9},{6,10},{7,11},{8,4},{9,5},{10,... | collective-permute-start | bytes 491528 | tf_op jit(solution)/shard_map/ppermute | solution.py:809
  37.0 4.6 %step_uv.1 = (f32[2,3,1024,128]{3,2,1,0:T(8,128)S(1)}, f32[272,128]{1,0:T(8,128)S(1)}, f32[272,128]{1,0:T(8,128)S(1)}, f32[2,3,16,128]{3,2,1,0:T(8,128)S(1)}) custom-call(s32[2]{0:T(128)S(1)} %pad_add_fusion.ids.refs_0_, f32[8,2,1024,128]{3,2,1,0:T(8,128)S(1)} %get-tuple-element.45.fld, f32[8,1024,128]{2,1,0:T(8,128)S(1)} %get-tuple-element.50.fe, ...), custom_call_target="tpu_custom_call" | custom-call | tf_op jit(solution)/shard_map/step_uv/pallas_call | solution.py:57
  41.9 2.5 %last_ts_0.1 = (f32[64,4,16,256]{3,2,1,0:T(8,128)}, f32[24,2,3,16,128]{4,3,2,1,0:T(8,128)S(1)}, f32[85,8,128]{2,1,0:T(8,128)S(1)}, f32[85,8,128]{2,1,0:T(8,128)S(1)}) custom-call(s32[2]{0:T(128)S(1)} %pad_add_fusion.ids.refs_0_, f32[2,3,1024,128]{3,2,1,0:T(8,128)S(1)} %get-tuple-element.61.refs_1_, f32[5,3,1024,128]{3,2,1,0:T(8,128)S(1)} %get-tuple-element.59.cfi.refs_2_, ...), custom_call_target="tpu_custom_call" | custom-call | tf_op jit(solution)/shard_map/last_ts_0/pallas_call | solution.py:57
  44.5 5.0 %collective-permute-start.9 = (f32[85,8,128]{2,1,0:T(8,128)S(1)}, f32[85,8,128]{2,1,0:T(8,128)S(1)}, u32[]{:S(2)}, u32[]{:S(2)}) collective-permute-start(f32[85,8,128]{2,1,0:T(8,128)S(1)} %get-tuple-element.66), channel_id=1, source_target_pairs={{0,1},{1,0},{2,3},{3,2},{4,8},{5,9},{6,10},{7,11},{8,4},{9,5},{10,... | collective-permute-start | bytes 1044488 | tf_op jit(solution)/shard_map/ppermute | solution.py:809
  49.5 3.3 %last_ts_24.1 = (f32[64,4,16,256]{3,2,1,0:T(8,128)}, f32[42,2,3,16,128]{4,3,2,1,0:T(8,128)S(1)}, f32[90,8,128]{2,1,0:T(8,128)S(1)}, f32[90,8,128]{2,1,0:T(8,128)S(1)}) custom-call(s32[2]{0:T(128)S(1)} %pad_add_fusion.ids.refs_0_, f32[2,3,1024,128]{3,2,1,0:T(8,128)S(1)} %get-tuple-element.61.refs_1_, ...), custom_call_target="tpu_custom_call", output_to_operand_aliasing={{0}: (7, {})} | custom-call | tf_op jit(solution)/shard_map/last_ts_24/pallas_call | solution.py:57
  52.7 2.4 %collective-permute-start.11 = (f32[90,8,128]{2,1,0:T(8,128)S(1)}, f32[90,8,128]{2,1,0:T(8,128)S(1)}, u32[]{:S(2)}, u32[]{:S(2)}) collective-permute-start(f32[90,8,128]{2,1,0:T(8,128)S(1)} %get-tuple-element.72), channel_id=1, source_target_pairs={{0,1},{1,0},{2,3},{3,2},{4,8},{5,9},{6,10},{7,11},{8,4},{9,5},{10,... | collective-permute-start | bytes 1105928 | tf_op jit(solution)/shard_map/ppermute | solution.py:809
  55.1 1.3 %collective-permute-done.9.ga.refs_3_ = f32[85,8,128]{2,1,0:T(8,128)S(1)} collective-permute-done((f32[85,8,128]{2,1,0:T(8,128)S(1)}, f32[85,8,128]{2,1,0:T(8,128)S(1)}, u32[]{:S(2)}, u32[]{:S(2)}) %collective-permute-start.9) | collective-permute-done | bytes 348192 | tf_op jit(solution)/shard_map/ppermute | solution.py:809
  56.4 5.7 %smooth_0_0.1 = (f32[48,4,256]{2,1,0:T(4,128)S(1)}, f32[48,4,256]{2,1,0:T(4,128)S(1)}, f32[48,4,256]{2,1,0:T(4,128)S(1)}, f32[48,4,256]{2,1,0:T(4,128)S(1)}) custom-call(s32[2]{0:T(128)S(1)} %pad_add_fusion.ids.refs_0_, f32[24,2,3,16,128]{4,3,2,1,0:T(8,128)S(1)} %get-tuple-element.74.g, f32[85,8,128]{2,1,0:T(8,128)S(1)} %collective-permute-done.9.ga.refs_3_, ...), custom_call_target="tpu_custom_call" | custom-call | tf_op jit(solution)/shard_map/smooth_0_0/pallas_call | solution.py:57
  62.1 13.1 %collective-permute-start.19 = (f32[48,4,256]{2,1,0:T(4,128)S(1)}, f32[48,4,256]{2,1,0:T(4,128)S(1)}, u32[]{:S(2)}, u32[]{:S(2)}) collective-permute-start(f32[48,4,256]{2,1,0:T(4,128)S(1)} %get-tuple-element.85), channel_id=1, source_target_pairs={{0,1},{1,0},{2,3},{3,2},{4,5},{5,4},{6,7},{7,6},{8,9},{9,8},{10,11... | collective-permute-start | bytes 589832 | tf_op jit(solution)/shard_map/ppermute | solution.py:812
  75.2 1.7 %collective-permute-start.21 = (f32[48,4,256]{2,1,0:T(4,128)S(1)}, f32[48,4,256]{2,1,0:T(4,128)S(1)}, u32[]{:S(2)}, u32[]{:S(2)}) collective-permute-start(f32[48,4,256]{2,1,0:T(4,128)S(1)} %get-tuple-element.87), channel_id=1, source_target_pairs={{0,3},{1,2},{2,1},{3,0},{4,7},{5,6},{6,5},{7,4},{8,11},{9,10},{10,... | collective-permute-start | bytes 589832 | tf_op jit(solution)/shard_map/ppermute | solution.py:812
  76.9 5.2 %smooth_1_0.1 = (f32[44,4,256]{2,1,0:T(4,128)S(1)}, f32[44,4,256]{2,1,0:T(4,128)S(1)}, f32[44,4,256]{2,1,0:T(4,128)S(1)}, f32[44,4,256]{2,1,0:T(4,128)S(1)}) custom-call(s32[2]{0:T(128)S(1)} %pad_add_fusion.ids.refs_0_, f32[42,2,3,16,128]{4,3,2,1,0:T(8,128)S(1)} %get-tuple-element.71.after.g, f32[90,8,128]{2,1,0:T(8,128)S(1)} %collective-permute-done.11.ga, ...), custom_call_target="tpu_custom_call" | custom-call | tf_op jit(solution)/shard_map/smooth_1_0/pallas_call | solution.py:57
  82.4 2.0 %collective-permute-start.18 = (f32[44,4,256]{2,1,0:T(4,128)S(1)}, f32[44,4,256]{2,1,0:T(4,128)S(1)}, u32[]{:S(2)}, u32[]{:S(2)}) collective-permute-start(f32[44,4,256]{2,1,0:T(4,128)S(1)} %get-tuple-element.84), channel_id=1, source_target_pairs={{0,3},{1,2},{2,1},{3,0},{4,7},{5,6},{6,5},{7,4},{8,11},{9,10},{10,... | collective-permute-start | bytes 540680 | tf_op jit(solution)/shard_map/ppermute | solution.py:812
  84.4 4.8 %smooth_1_22.1 = (f32[40,4,256]{2,1,0:T(4,128)S(1)}, f32[40,4,256]{2,1,0:T(4,128)S(1)}, f32[40,4,256]{2,1,0:T(4,128)S(1)}, f32[40,4,256]{2,1,0:T(4,128)S(1)}) custom-call(s32[2]{0:T(128)S(1)} %pad_add_fusion.ids.refs_0_, f32[42,2,3,16,128]{4,3,2,1,0:T(8,128)S(1)} %get-tuple-element.71.after.g, f32[90,8,128]{2,1,0:T(8,128)S(1)} %collective-permute-done.11.ga, ...), custom_call_target="tpu_custom_call" | custom-call | tf_op jit(solution)/shard_map/smooth_1_22/pallas_call | solution.py:57
  89.4 2.0 %collective-permute-start.15 = (f32[40,4,256]{2,1,0:T(4,128)S(1)}, f32[40,4,256]{2,1,0:T(4,128)S(1)}, u32[]{:S(2)}, u32[]{:S(2)}) collective-permute-start(f32[40,4,256]{2,1,0:T(4,128)S(1)} %get-tuple-element.81), channel_id=1, source_target_pairs={{0,3},{1,2},{2,1},{3,0},{4,7},{5,6},{6,5},{7,4},{8,11},{9,10},{10,... | collective-permute-start | bytes 491528 | tf_op jit(solution)/shard_map/ppermute | solution.py:812
  91.5 4.3 %last_uv.1 = f32[64,4,16,256]{3,2,1,0:T(8,128)} custom-call(s32[2]{0:T(128)S(1)} %pad_add_fusion.ids.refs_0_, f32[2,3,1024,128]{3,2,1,0:T(8,128)S(1)} %get-tuple-element.60.refs_1_, f32[5,3,1024,128]{3,2,1,0:T(8,128)S(1)} %get-tuple-element.59.cfi.refs_2_, f32[85,8,128]{2,1,0:T(8,128)S(1)} %collective-permute-done.9.ga.refs_3_, ...), custom_call_target="tpu_custom_call", output_to_operand_aliasing={{}: (6, {})} | custom-call | tf_op jit(solution)/shard_map/last_uv/pallas_call | solution.py:57
  95.7 1.5 %gather_0.1.refs_0_ = f32[132,4,1024]{2,1,0:T(4,128)} custom-call(s32[2]{0:T(128)S(1)} %pad_add_fusion.ids.refs_0_, f32[48,4,256]{2,1,0:T(4,128)S(1)} %get-tuple-element.75.after.z0, f32[48,4,256]{2,1,0:T(4,128)S(1)} %collective-permute-done.19.z1, f32[48,4,256]{2,1,0:T(4,128)S(1)} %collective-permute-done.20.z2, f32[48,4,256]{2,1,0:T(4,128)S(1)} %collective-permute-done.21.z3), custom_call_target="tpu_custom_call" | custom-call | tf_op jit(solution)/shard_map/gather_0/pallas_call | solution.py:57
  97.2 1.4 %gather_48.1.refs_0_ = f32[132,4,1024]{2,1,0:T(4,128)} custom-call(s32[2]{0:T(128)S(1)} %pad_add_fusion.ids.refs_0_, f32[44,4,256]{2,1,0:T(4,128)S(1)} %get-tuple-element.76.after.z0, f32[44,4,256]{2,1,0:T(4,128)S(1)} %collective-permute-done.16.z1, f32[44,4,256]{2,1,0:T(4,128)S(1)} %collective-permute-done.17.z2, ...), custom_call_target="tpu_custom_call", output_to_operand_aliasing={{}: (5, {})} | custom-call | tf_op jit(solution)/shard_map/gather_48/pallas_call | solution.py:57
  98.7 2.1 %collective-permute-done.15.z3 = f32[40,4,256]{2,1,0:T(4,128)S(1)} collective-permute-done((f32[40,4,256]{2,1,0:T(4,128)S(1)}, f32[40,4,256]{2,1,0:T(4,128)S(1)}, u32[]{:S(2)}, u32[]{:S(2)}) %collective-permute-start.15) | collective-permute-done | bytes 163872 | tf_op jit(solution)/shard_map/ppermute | solution.py:812
  100.8 1.4 %gather_92.1 = f32[132,4,1024]{2,1,0:T(4,128)} custom-call(s32[2]{0:T(128)S(1)} %pad_add_fusion.ids.refs_0_, f32[40,4,256]{2,1,0:T(4,128)S(1)} %get-tuple-element.77.refs_5_.z0, f32[40,4,256]{2,1,0:T(4,128)S(1)} %collective-permute-done.13.z1, f32[40,4,256]{2,1,0:T(4,128)S(1)} %collective-permute-done.14.z2, ...), custom_call_target="tpu_custom_call", output_to_operand_aliasing={{}: (5, {})} | custom-call | tf_op jit(solution)/shard_map/gather_92/pallas_call | solution.py:57
  (39 shorter events, 6.4 us)
Async XLA Ops:
  0.6 11.0 %collective-permute-start.1 = (f32[2,4,1024]{2,1,0:T(4,128)}, f32[2,4,1024]{2,1,0:T(4,128)S(1)}, u32[]{:S(2)}, u32[]{:S(2)}) collective-permute-start(f32[2,4,1024]{2,1,0:T(4,128)} %w0.1), channel_id=1, source_target_pairs={{0,2},{1,3},{2,0},{3,1},{4,6},{5,7},{6,4},{7,5},{8,10},{9,11},{10,... | collective-permute-start | bytes 98312 | tf_op jit(solution)/shard_map/ppermute | solution.py:812
  0.8 10.8 %collective-permute-start = (f32[2,4,1024]{2,1,0:T(4,128)}, f32[2,4,1024]{2,1,0:T(4,128)S(1)}, u32[]{:S(2)}, u32[]{:S(2)}) collective-permute-start(f32[2,4,1024]{2,1,0:T(4,128)} %w0.1), channel_id=1, source_target_pairs={{0,1},{1,0},{2,3},{3,2},{4,5},{5,4},{6,7},{7,6},{8,9},{9,8},{10,11... | collective-permute-start | bytes 98312 | tf_op jit(solution)/shard_map/ppermute | solution.py:812
  1.8 9.9 %collective-permute-start.2 = (f32[2,4,1024]{2,1,0:T(4,128)}, f32[2,4,1024]{2,1,0:T(4,128)S(1)}, u32[]{:S(2)}, u32[]{:S(2)}) collective-permute-start(f32[2,4,1024]{2,1,0:T(4,128)} %w0.1), channel_id=1, source_target_pairs={{0,3},{1,2},{2,1},{3,0},{4,7},{5,6},{6,5},{7,4},{8,11},{9,10},{10,... | collective-permute-start | bytes 98312 | tf_op jit(solution)/shard_map/ppermute | solution.py:812
  3.1 8.6 %copy-start = (f32[2,4,1024]{2,1,0:T(4,128)S(1)}, f32[2,4,1024]{2,1,0:T(4,128)}, u32[]{:S(2)}) copy-start(f32[2,4,1024]{2,1,0:T(4,128)} %w0.1) | copy-start | bytes 98308
  12.3 2.0 %collective-permute-start.3 = (f32[512,128]{1,0:T(8,128)S(1)}, f32[512,128]{1,0:T(8,128)S(1)}, u32[]{:S(2)}, u32[]{:S(2)}) collective-permute-start(f32[512,128]{1,0:T(8,128)S(1)} %get-tuple-element.48), channel_id=1, source_target_pairs={{0,1},{1,0},{2,3},{3,2},{4,5},{5,4},{6,7},{7,6},{8,9},{9,8},{10,11... | collective-permute-start | bytes 786440 | tf_op jit(solution)/shard_map/ppermute | solution.py:837
  12.9 1.5 %collective-permute-start.4 = (f32[512,128]{1,0:T(8,128)S(1)}, f32[512,128]{1,0:T(8,128)S(1)}, u32[]{:S(2)}, u32[]{:S(2)}) collective-permute-start(f32[512,128]{1,0:T(8,128)S(1)} %get-tuple-element.49), channel_id=1, source_target_pairs={{0,0},{1,2},{2,1},{3,3},{4,4},{5,6},{6,5},{7,7},{8,8},{9,10},{10,9... | collective-permute-start | bytes 786440 | tf_op jit(solution)/shard_map/ppermute | solution.py:838
  14.9 12.1 %collective-permute-start.5 = (f32[704,128]{1,0:T(8,128)S(1)}, f32[704,128]{1,0:T(8,128)S(1)}, u32[]{:S(2)}, u32[]{:S(2)}) collective-permute-start(f32[704,128]{1,0:T(8,128)S(1)} %get-tuple-element.56), channel_id=1, source_target_pairs={{0,1},{1,0},{2,3},{3,2},{4,8},{5,9},{6,10},{7,11},{8,4},{9,5},{10,... | collective-permute-start | bytes 1081352 | tf_op jit(solution)/shard_map/ppermute | solution.py:809
  19.9 7.1 %collective-permute-start.6 = (f32[704,128]{1,0:T(8,128)S(1)}, f32[704,128]{1,0:T(8,128)S(1)}, u32[]{:S(2)}, u32[]{:S(2)}) collective-permute-start(f32[704,128]{1,0:T(8,128)S(1)} %get-tuple-element.57), channel_id=1, source_target_pairs={{0,4},{4,0},{8,12},{12,8},{16,20},{20,16},{24,28},{28,24},{32,36},... | collective-permute-start | bytes 1081352 | tf_op jit(solution)/shard_map/ppermute | solution.py:809
  32.0 10.0 %collective-permute-start.7 = (f32[320,128]{1,0:T(8,128)S(1)}, f32[320,128]{1,0:T(8,128)S(1)}, u32[]{:S(2)}, u32[]{:S(2)}) collective-permute-start(f32[320,128]{1,0:T(8,128)S(1)} %get-tuple-element.62), channel_id=1, source_target_pairs={{0,1},{1,0},{2,3},{3,2},{4,8},{5,9},{6,10},{7,11},{8,4},{9,5},{10,... | collective-permute-start | bytes 491528 | tf_op jit(solution)/shard_map/ppermute | solution.py:809
  37.0 5.0 %collective-permute-start.8 = (f32[320,128]{1,0:T(8,128)S(1)}, f32[320,128]{1,0:T(8,128)S(1)}, u32[]{:S(2)}, u32[]{:S(2)}) collective-permute-start(f32[320,128]{1,0:T(8,128)S(1)} %get-tuple-element.63), channel_id=1, source_target_pairs={{0,4},{4,0},{8,12},{12,8},{16,20},{20,16},{24,28},{28,24},{32,36},... | collective-permute-start | bytes 491528 | tf_op jit(solution)/shard_map/ppermute | solution.py:809
  44.5 11.9 %collective-permute-start.9 = (f32[85,8,128]{2,1,0:T(8,128)S(1)}, f32[85,8,128]{2,1,0:T(8,128)S(1)}, u32[]{:S(2)}, u32[]{:S(2)}) collective-permute-start(f32[85,8,128]{2,1,0:T(8,128)S(1)} %get-tuple-element.66), channel_id=1, source_target_pairs={{0,1},{1,0},{2,3},{3,2},{4,8},{5,9},{6,10},{7,11},{8,4},{9,5},{10,... | collective-permute-start | bytes 1044488 | tf_op jit(solution)/shard_map/ppermute | solution.py:809
  49.5 7.0 %collective-permute-start.10 = (f32[85,8,128]{2,1,0:T(8,128)S(1)}, f32[85,8,128]{2,1,0:T(8,128)S(1)}, u32[]{:S(2)}, u32[]{:S(2)}) collective-permute-start(f32[85,8,128]{2,1,0:T(8,128)S(1)} %get-tuple-element.67), channel_id=1, source_target_pairs={{0,4},{4,0},{8,12},{12,8},{16,20},{20,16},{24,28},{28,24},{32,36},... | collective-permute-start | bytes 1044488 | tf_op jit(solution)/shard_map/ppermute | solution.py:809
  52.7 24.2 %collective-permute-start.11 = (f32[90,8,128]{2,1,0:T(8,128)S(1)}, f32[90,8,128]{2,1,0:T(8,128)S(1)}, u32[]{:S(2)}, u32[]{:S(2)}) collective-permute-start(f32[90,8,128]{2,1,0:T(8,128)S(1)} %get-tuple-element.72), channel_id=1, source_target_pairs={{0,1},{1,0},{2,3},{3,2},{4,8},{5,9},{6,10},{7,11},{8,4},{9,5},{10,... | collective-permute-start | bytes 1105928 | tf_op jit(solution)/shard_map/ppermute | solution.py:809
  55.1 21.8 %collective-permute-start.12 = (f32[90,8,128]{2,1,0:T(8,128)S(1)}, f32[90,8,128]{2,1,0:T(8,128)S(1)}, u32[]{:S(2)}, u32[]{:S(2)}) collective-permute-start(f32[90,8,128]{2,1,0:T(8,128)S(1)} %get-tuple-element.73), channel_id=1, source_target_pairs={{0,4},{4,0},{8,12},{12,8},{16,20},{20,16},{24,28},{28,24},{32,36},... | collective-permute-start | bytes 1105928 | tf_op jit(solution)/shard_map/ppermute | solution.py:809
  62.1 20.3 %collective-permute-start.19 = (f32[48,4,256]{2,1,0:T(4,128)S(1)}, f32[48,4,256]{2,1,0:T(4,128)S(1)}, u32[]{:S(2)}, u32[]{:S(2)}) collective-permute-start(f32[48,4,256]{2,1,0:T(4,128)S(1)} %get-tuple-element.85), channel_id=1, source_target_pairs={{0,1},{1,0},{2,3},{3,2},{4,5},{5,4},{6,7},{7,6},{8,9},{9,8},{10,11... | collective-permute-start | bytes 589832 | tf_op jit(solution)/shard_map/ppermute | solution.py:812
  75.2 14.0 %collective-permute-start.20 = (f32[48,4,256]{2,1,0:T(4,128)S(1)}, f32[48,4,256]{2,1,0:T(4,128)S(1)}, u32[]{:S(2)}, u32[]{:S(2)}) collective-permute-start(f32[48,4,256]{2,1,0:T(4,128)S(1)} %get-tuple-element.86), channel_id=1, source_target_pairs={{0,2},{1,3},{2,0},{3,1},{4,6},{5,7},{6,4},{7,5},{8,10},{9,11},{10,... | collective-permute-start | bytes 589832 | tf_op jit(solution)/shard_map/ppermute | solution.py:812
  75.2 14.1 %collective-permute-start.21 = (f32[48,4,256]{2,1,0:T(4,128)S(1)}, f32[48,4,256]{2,1,0:T(4,128)S(1)}, u32[]{:S(2)}, u32[]{:S(2)}) collective-permute-start(f32[48,4,256]{2,1,0:T(4,128)S(1)} %get-tuple-element.87), channel_id=1, source_target_pairs={{0,3},{1,2},{2,1},{3,0},{4,7},{5,6},{6,5},{7,4},{8,11},{9,10},{10,... | collective-permute-start | bytes 589832 | tf_op jit(solution)/shard_map/ppermute | solution.py:812
  82.2 7.3 %collective-permute-start.16 = (f32[44,4,256]{2,1,0:T(4,128)S(1)}, f32[44,4,256]{2,1,0:T(4,128)S(1)}, u32[]{:S(2)}, u32[]{:S(2)}) collective-permute-start(f32[44,4,256]{2,1,0:T(4,128)S(1)} %get-tuple-element.82), channel_id=1, source_target_pairs={{0,1},{1,0},{2,3},{3,2},{4,5},{5,4},{6,7},{7,6},{8,9},{9,8},{10,11... | collective-permute-start | bytes 540680 | tf_op jit(solution)/shard_map/ppermute | solution.py:812
  82.4 14.8 %collective-permute-start.17 = (f32[44,4,256]{2,1,0:T(4,128)S(1)}, f32[44,4,256]{2,1,0:T(4,128)S(1)}, u32[]{:S(2)}, u32[]{:S(2)}) collective-permute-start(f32[44,4,256]{2,1,0:T(4,128)S(1)} %get-tuple-element.83), channel_id=1, source_target_pairs={{0,2},{1,3},{2,0},{3,1},{4,6},{5,7},{6,4},{7,5},{8,10},{9,11},{10,... | collective-permute-start | bytes 540680 | tf_op jit(solution)/shard_map/ppermute | solution.py:812
  82.4 14.8 %collective-permute-start.18 = (f32[44,4,256]{2,1,0:T(4,128)S(1)}, f32[44,4,256]{2,1,0:T(4,128)S(1)}, u32[]{:S(2)}, u32[]{:S(2)}) collective-permute-start(f32[44,4,256]{2,1,0:T(4,128)S(1)} %get-tuple-element.84), channel_id=1, source_target_pairs={{0,3},{1,2},{2,1},{3,0},{4,7},{5,6},{6,5},{7,4},{8,11},{9,10},{10,... | collective-permute-start | bytes 540680 | tf_op jit(solution)/shard_map/ppermute | solution.py:812
  89.2 9.4 %collective-permute-start.13 = (f32[40,4,256]{2,1,0:T(4,128)S(1)}, f32[40,4,256]{2,1,0:T(4,128)S(1)}, u32[]{:S(2)}, u32[]{:S(2)}) collective-permute-start(f32[40,4,256]{2,1,0:T(4,128)S(1)} %get-tuple-element.79), channel_id=1, source_target_pairs={{0,1},{1,0},{2,3},{3,2},{4,5},{5,4},{6,7},{7,6},{8,9},{9,8},{10,11... | collective-permute-start | bytes 491528 | tf_op jit(solution)/shard_map/ppermute | solution.py:812
  89.3 9.3 %collective-permute-start.14 = (f32[40,4,256]{2,1,0:T(4,128)S(1)}, f32[40,4,256]{2,1,0:T(4,128)S(1)}, u32[]{:S(2)}, u32[]{:S(2)}) collective-permute-start(f32[40,4,256]{2,1,0:T(4,128)S(1)} %get-tuple-element.80), channel_id=1, source_target_pairs={{0,2},{1,3},{2,0},{3,1},{4,6},{5,7},{6,4},{7,5},{8,10},{9,11},{10,... | collective-permute-start | bytes 491528 | tf_op jit(solution)/shard_map/ppermute | solution.py:812
  89.4 11.4 %collective-permute-start.15 = (f32[40,4,256]{2,1,0:T(4,128)S(1)}, f32[40,4,256]{2,1,0:T(4,128)S(1)}, u32[]{:S(2)}, u32[]{:S(2)}) collective-permute-start(f32[40,4,256]{2,1,0:T(4,128)S(1)} %get-tuple-element.81), channel_id=1, source_target_pairs={{0,3},{1,2},{2,1},{3,0},{4,7},{5,6},{6,5},{7,4},{8,11},{9,10},{10,... | collective-permute-start | bytes 491528 | tf_op jit(solution)/shard_map/ppermute | solution.py:812

commit v5 on v4

--- a/solution.py
+++ b/solution.py
@@ -17,10 +17,10 @@
 MIB = 2**20
 UNROLL_S = 8
 UNROLL_L = 8
-UNROLL_M = 2
+UNROLL_M = 3
 
 CHUNKS = ((0, 24), (24, 64))
-PIECES = ((0, 0, 24), (1, 0, 22), (1, 22, 42))
+PIECES = ((0, 0, 24), (1, 0, 24), (1, 24, 42))
 CARRIER = 0
 
 
@@ -44,7 +44,7 @@
     return [jnp.where(first, turned[(i + 2) % 3], turned[i]) for i in range(3)]
 
 
-def call(kernel, outs, scratch=(), limit=8, alias=None, name=None, ins=None):
+def call(kernel, outs, scratch=(), limit=8, alias=None, name=None, ins=None, cost=None):
     def run(*args):
         args = list(args)
         specs = [pl.BlockSpec(memory_space=pltpu.SMEM)]
@@ -63,6 +63,7 @@
             input_output_aliases=alias or {},
             compiler_params=pltpu.CompilerParams(vmem_limit_bytes=limit * MIB),
             name=name,
+            cost_estimate=cost and pl.CostEstimate(flops=cost[0], bytes_accessed=cost[1], transcendentals=0),
         )(*args)
 
     return run
@@ -950,6 +951,7 @@
             ],
             ins=[None] + [VM] * 6 + [any_space],
             limit=4,
+            cost=(2 * n * 4 * 24 * 384 * 9, 2 * n * 4 * (16 * 384 + 16 * 256)),
             name="smooth_%d_%d" % (c, u0),
         )(ids, g, ga, gb, wloc, ta, tb, after)
         after = zs[0]
@@ -963,6 +965,7 @@
         limit=6,
         alias={6: 0},
         ins=[None] + [VM] * 4 + [any_space] * 2,
+        cost=(LEV * 2 * ROWS * 256 * 9, LEV * ROWS * 4 * (2 * 384 + 2 * 256 + 5 * 384)),
         name="last_uv",
     )(ids, sol_u, cf, ga, gb, after, adj)
     for start, size, parts in sent:

time: 102 us -> 102 us (level)
  transfers between devices with their start and end apart: 22 -> 22, of which waited for: 4 -> 4; matrix products, arithmetic and copies ran while one was open for 0% -> 0% of each run, Pallas kernels for 45% -> 44%
where the time goes in v5:
time: 102 us
  Pallas kernels  55 us (54%)
  starting transfers between devices  40.2 us (39%)
  waiting for transfers between devices  5.58 us (5%)
    pallas_call x16, Pallas kernels, run(): pl.pallas_call(kernel, out_shape=[jax.ShapeDtypeStruct(s, F32) for s, _ i...  55 us
    ppermute x12, starting transfers between devices, to_face(): return lax.ppermute(x, 'face', [(i, i ^ k) for i in range(4)])  21.6 us
    ppermute x4, starting transfers between devices, across(): lax.ppermute(a, ('tile', 'face'), pair_b)  17.3 us
    ppermute x4, waiting for transfers between devices, across(): lax.ppermute(a, ('tile', 'face'), pair_b)  2.8 us
    ppermute x12, waiting for transfers between devices, to_face(): return lax.ppermute(x, 'face', [(i, i ^ k) for i in range(4)])  2.77 us
  transfers between devices with their start and end apart: 22, of which 4 were waited for; matrix products, arithmetic and copies ran while one was open for 0% of the time, Pallas kernels for 44%

profile of v5, /device:TPU:97, one launch (start us, length us, event | category | flops | bytes accessed | tf_op | source)
XLA Modules:
  0.0 101.8 jit_solution(17421329072550004182)
XLA Ops:
  1.8 1.2 %collective-permute-start.2 = (f32[2,4,1024]{2,1,0:T(4,128)}, f32[2,4,1024]{2,1,0:T(4,128)S(1)}, u32[]{:S(2)}, u32[]{:S(2)}) collective-permute-start(f32[2,4,1024]{2,1,0:T(4,128)} %w0.1), channel_id=1, source_target_pairs={{0,3},{1,2},{2,1},{3,0},{4,7},{5,6},{6,5},{7,4},{8,11},{9,10},{10,... | collective-permute-start | bytes 98312 | tf_op jit(solution)/shard_map/ppermute | solution.py:813
  3.1 8.6 %first_solve.1 = (f32[8,2,1024,128]{3,2,1,0:T(8,128)S(1)}, f32[3,2,1024,128]{3,2,1,0:T(8,128)S(1)}, f32[512,128]{1,0:T(8,128)S(1)}, f32[512,128]{1,0:T(8,128)S(1)}) custom-call(s32[2]{0:T(128)S(1)} %pad_add_fusion.ids.refs_0_, f32[64,4,16,256]{3,2,1,0:T(8,128)} %seed.1, f32[2,64,16,256]{3,2,1,0:T(8,128)} %flow.1, f32[64,16,256]{2,1,0:T(8,128)} %vd.1, ...), custom_call_target="tpu_custom_call" | custom-call | tf_op jit(solution)/shard_map/first_solve/pallas_call | solution.py:57
  14.9 5.0 %collective-permute-start.5 = (f32[704,128]{1,0:T(8,128)S(1)}, f32[704,128]{1,0:T(8,128)S(1)}, u32[]{:S(2)}, u32[]{:S(2)}) collective-permute-start(f32[704,128]{1,0:T(8,128)S(1)} %get-tuple-element.56), channel_id=1, source_target_pairs={{0,1},{1,0},{2,3},{3,2},{4,8},{5,9},{6,10},{7,11},{8,4},{9,5},{10,... | collective-permute-start | bytes 1081352 | tf_op jit(solution)/shard_map/ppermute | solution.py:810
  19.9 6.0 %coefficients.1 = (f32[8,1024,128]{2,1,0:T(8,128)S(1)}, f32[5,3,1024,128]{3,2,1,0:T(8,128)S(1)}, f32[3,1,1024,128]{3,2,1,0:T(8,128)S(1)}) custom-call(s32[2]{0:T(128)S(1)} %pad_add_fusion.ids.refs_0_, f32[8,2,1024,128]{3,2,1,0:T(8,128)S(1)} %get-tuple-element.45.fld, f32[512,128]{1,0:T(8,128)S(1)} %collective-permute-done.3.xa, ...), custom_call_target="tpu_custom_call" | custom-call | tf_op jit(solution)/shard_map/coefficients/pallas_call | solution.py:57
  27.0 5.0 %step_ts.1 = (f32[5,3,1024,128]{3,2,1,0:T(8,128)S(1)}, f32[2,3,1024,128]{3,2,1,0:T(8,128)S(1)}, f32[320,128]{1,0:T(8,128)S(1)}, f32[320,128]{1,0:T(8,128)S(1)}, f32[2,3,16,128]{3,2,1,0:T(8,128)S(1)}) custom-call(s32[2]{0:T(128)S(1)} %pad_add_fusion.ids.refs_0_, f32[8,2,1024,128]{3,2,1,0:T(8,128)S(1)} %get-tuple-element.45.fld, ...), custom_call_target="tpu_custom_call", output_to_operand_aliasing={{0}: (3, {})} | custom-call | tf_op jit(solution)/shard_map/step_ts/pallas_call | solution.py:57
  32.0 5.0 %collective-permute-start.7 = (f32[320,128]{1,0:T(8,128)S(1)}, f32[320,128]{1,0:T(8,128)S(1)}, u32[]{:S(2)}, u32[]{:S(2)}) collective-permute-start(f32[320,128]{1,0:T(8,128)S(1)} %get-tuple-element.62), channel_id=1, source_target_pairs={{0,1},{1,0},{2,3},{3,2},{4,8},{5,9},{6,10},{7,11},{8,4},{9,5},{10,... | collective-permute-start | bytes 491528 | tf_op jit(solution)/shard_map/ppermute | solution.py:810
  37.0 4.6 %step_uv.1 = (f32[2,3,1024,128]{3,2,1,0:T(8,128)S(1)}, f32[272,128]{1,0:T(8,128)S(1)}, f32[272,128]{1,0:T(8,128)S(1)}, f32[2,3,16,128]{3,2,1,0:T(8,128)S(1)}) custom-call(s32[2]{0:T(128)S(1)} %pad_add_fusion.ids.refs_0_, f32[8,2,1024,128]{3,2,1,0:T(8,128)S(1)} %get-tuple-element.45.fld, f32[8,1024,128]{2,1,0:T(8,128)S(1)} %get-tuple-element.50.fe, ...), custom_call_target="tpu_custom_call" | custom-call | tf_op jit(solution)/shard_map/step_uv/pallas_call | solution.py:57
  41.9 2.5 %last_ts_0.1 = (f32[64,4,16,256]{3,2,1,0:T(8,128)}, f32[24,2,3,16,128]{4,3,2,1,0:T(8,128)S(1)}, f32[85,8,128]{2,1,0:T(8,128)S(1)}, f32[85,8,128]{2,1,0:T(8,128)S(1)}) custom-call(s32[2]{0:T(128)S(1)} %pad_add_fusion.ids.refs_0_, f32[2,3,1024,128]{3,2,1,0:T(8,128)S(1)} %get-tuple-element.61.refs_1_, f32[5,3,1024,128]{3,2,1,0:T(8,128)S(1)} %get-tuple-element.59.cfi.refs_2_, ...), custom_call_target="tpu_custom_call" | custom-call | tf_op jit(solution)/shard_map/last_ts_0/pallas_call | solution.py:57
  44.5 5.0 %collective-permute-start.9 = (f32[85,8,128]{2,1,0:T(8,128)S(1)}, f32[85,8,128]{2,1,0:T(8,128)S(1)}, u32[]{:S(2)}, u32[]{:S(2)}) collective-permute-start(f32[85,8,128]{2,1,0:T(8,128)S(1)} %get-tuple-element.66), channel_id=1, source_target_pairs={{0,1},{1,0},{2,3},{3,2},{4,8},{5,9},{6,10},{7,11},{8,4},{9,5},{10,... | collective-permute-start | bytes 1044488 | tf_op jit(solution)/shard_map/ppermute | solution.py:810
  49.5 3.3 %last_ts_24.1 = (f32[64,4,16,256]{3,2,1,0:T(8,128)}, f32[42,2,3,16,128]{4,3,2,1,0:T(8,128)S(1)}, f32[90,8,128]{2,1,0:T(8,128)S(1)}, f32[90,8,128]{2,1,0:T(8,128)S(1)}) custom-call(s32[2]{0:T(128)S(1)} %pad_add_fusion.ids.refs_0_, f32[2,3,1024,128]{3,2,1,0:T(8,128)S(1)} %get-tuple-element.61.refs_1_, ...), custom_call_target="tpu_custom_call", output_to_operand_aliasing={{0}: (7, {})} | custom-call | tf_op jit(solution)/shard_map/last_ts_24/pallas_call | solution.py:57
  52.7 2.4 %collective-permute-start.11 = (f32[90,8,128]{2,1,0:T(8,128)S(1)}, f32[90,8,128]{2,1,0:T(8,128)S(1)}, u32[]{:S(2)}, u32[]{:S(2)}) collective-permute-start(f32[90,8,128]{2,1,0:T(8,128)S(1)} %get-tuple-element.72), channel_id=1, source_target_pairs={{0,1},{1,0},{2,3},{3,2},{4,8},{5,9},{6,10},{7,11},{8,4},{9,5},{10,... | collective-permute-start | bytes 1105928 | tf_op jit(solution)/shard_map/ppermute | solution.py:810
  55.1 1.3 %collective-permute-done.9.ga.refs_3_ = f32[85,8,128]{2,1,0:T(8,128)S(1)} collective-permute-done((f32[85,8,128]{2,1,0:T(8,128)S(1)}, f32[85,8,128]{2,1,0:T(8,128)S(1)}, u32[]{:S(2)}, u32[]{:S(2)}) %collective-permute-start.9) | collective-permute-done | bytes 348192 | tf_op jit(solution)/shard_map/ppermute | solution.py:810
  56.4 5.3 %smooth_0_0.1 = (f32[48,4,256]{2,1,0:T(4,128)S(1)}, f32[48,4,256]{2,1,0:T(4,128)S(1)}, f32[48,4,256]{2,1,0:T(4,128)S(1)}, f32[48,4,256]{2,1,0:T(4,128)S(1)}) custom-call(s32[2]{0:T(128)S(1)} %pad_add_fusion.ids.refs_0_, f32[24,2,3,16,128]{4,3,2,1,0:T(8,128)S(1)} %get-tuple-element.74.g, f32[85,8,128]{2,1,0:T(8,128)S(1)} %collective-permute-done.9.ga.refs_3_, ...), custom_call_target="tpu_custom_call" | custom-call | flops 15925248 | bytes 1966080 | tf_op jit(solution)/shard_map/smooth_0_0/pallas_call | solution.py:57
  61.7 13.1 %collective-permute-start.19 = (f32[48,4,256]{2,1,0:T(4,128)S(1)}, f32[48,4,256]{2,1,0:T(4,128)S(1)}, u32[]{:S(2)}, u32[]{:S(2)}) collective-permute-start(f32[48,4,256]{2,1,0:T(4,128)S(1)} %get-tuple-element.85), channel_id=1, source_target_pairs={{0,1},{1,0},{2,3},{3,2},{4,5},{5,4},{6,7},{7,6},{8,9},{9,8},{10,11... | collective-permute-start | bytes 589832 | tf_op jit(solution)/shard_map/ppermute | solution.py:813
  74.8 1.7 %collective-permute-start.21 = (f32[48,4,256]{2,1,0:T(4,128)S(1)}, f32[48,4,256]{2,1,0:T(4,128)S(1)}, u32[]{:S(2)}, u32[]{:S(2)}) collective-permute-start(f32[48,4,256]{2,1,0:T(4,128)S(1)} %get-tuple-element.87), channel_id=1, source_target_pairs={{0,3},{1,2},{2,1},{3,0},{4,7},{5,6},{6,5},{7,4},{8,11},{9,10},{10,... | collective-permute-start | bytes 589832 | tf_op jit(solution)/shard_map/ppermute | solution.py:813
  76.5 5.3 %smooth_1_0.1 = (f32[48,4,256]{2,1,0:T(4,128)S(1)}, f32[48,4,256]{2,1,0:T(4,128)S(1)}, f32[48,4,256]{2,1,0:T(4,128)S(1)}, f32[48,4,256]{2,1,0:T(4,128)S(1)}) custom-call(s32[2]{0:T(128)S(1)} %pad_add_fusion.ids.refs_0_, f32[42,2,3,16,128]{4,3,2,1,0:T(8,128)S(1)} %get-tuple-element.71.after.g, f32[90,8,128]{2,1,0:T(8,128)S(1)} %collective-permute-done.11.ga, ...), custom_call_target="tpu_custom_call" | custom-call | flops 15925248 | bytes 1966080 | tf_op jit(solution)/shard_map/smooth_1_0/pallas_call | solution.py:57
  82.1 2.0 %collective-permute-start.18 = (f32[48,4,256]{2,1,0:T(4,128)S(1)}, f32[48,4,256]{2,1,0:T(4,128)S(1)}, u32[]{:S(2)}, u32[]{:S(2)}) collective-permute-start(f32[48,4,256]{2,1,0:T(4,128)S(1)} %get-tuple-element.84), channel_id=1, source_target_pairs={{0,3},{1,2},{2,1},{3,0},{4,7},{5,6},{6,5},{7,4},{8,11},{9,10},{10,... | collective-permute-start | bytes 589832 | tf_op jit(solution)/shard_map/ppermute | solution.py:813
  84.1 4.1 %smooth_1_24.1 = (f32[36,4,256]{2,1,0:T(4,128)S(1)}, f32[36,4,256]{2,1,0:T(4,128)S(1)}, f32[36,4,256]{2,1,0:T(4,128)S(1)}, f32[36,4,256]{2,1,0:T(4,128)S(1)}) custom-call(s32[2]{0:T(128)S(1)} %pad_add_fusion.ids.refs_0_, f32[42,2,3,16,128]{4,3,2,1,0:T(8,128)S(1)} %get-tuple-element.71.after.g, f32[90,8,128]{2,1,0:T(8,128)S(1)} %collective-permute-done.11.ga, ...), custom_call_target="tpu_custom_call" | custom-call | flops 11943936 | bytes 1474560 | tf_op jit(solution)/shard_map/smooth_1_24/pallas_call | solution.py:57
  88.4 2.0 %collective-permute-start.15 = (f32[36,4,256]{2,1,0:T(4,128)S(1)}, f32[36,4,256]{2,1,0:T(4,128)S(1)}, u32[]{:S(2)}, u32[]{:S(2)}) collective-permute-start(f32[36,4,256]{2,1,0:T(4,128)S(1)} %get-tuple-element.81), channel_id=1, source_target_pairs={{0,3},{1,2},{2,1},{3,0},{4,7},{5,6},{6,5},{7,4},{8,11},{9,10},{10,... | collective-permute-start | bytes 442376 | tf_op jit(solution)/shard_map/ppermute | solution.py:813
  90.5 4.3 %last_uv.1 = f32[64,4,16,256]{3,2,1,0:T(8,128)} custom-call(s32[2]{0:T(128)S(1)} %pad_add_fusion.ids.refs_0_, f32[2,3,1024,128]{3,2,1,0:T(8,128)S(1)} %get-tuple-element.60.refs_1_, f32[5,3,1024,128]{3,2,1,0:T(8,128)S(1)} %get-tuple-element.59.cfi.refs_2_, f32[85,8,128]{2,1,0:T(8,128)S(1)} %collective-permute-done.9.ga.refs_3_, ...), custom_call_target="tpu_custom_call", output_to_operand_aliasing={{}: (6, {})} | custom-call | flops 4718592 | bytes 13107200 | tf_op jit(solution)/shard_map/last_uv/pallas_call | solution.py:57
  94.7 1.5 %gather_0.1.refs_0_ = f32[132,4,1024]{2,1,0:T(4,128)} custom-call(s32[2]{0:T(128)S(1)} %pad_add_fusion.ids.refs_0_, f32[48,4,256]{2,1,0:T(4,128)S(1)} %get-tuple-element.75.after.z0, f32[48,4,256]{2,1,0:T(4,128)S(1)} %collective-permute-done.19.z1, f32[48,4,256]{2,1,0:T(4,128)S(1)} %collective-permute-done.20.z2, f32[48,4,256]{2,1,0:T(4,128)S(1)} %collective-permute-done.21.z3), custom_call_target="tpu_custom_call" | custom-call | tf_op jit(solution)/shard_map/gather_0/pallas_call | solution.py:57
  96.2 1.5 %gather_48.1.refs_0_ = f32[132,4,1024]{2,1,0:T(4,128)} custom-call(s32[2]{0:T(128)S(1)} %pad_add_fusion.ids.refs_0_, f32[48,4,256]{2,1,0:T(4,128)S(1)} %get-tuple-element.76.after.z0, f32[48,4,256]{2,1,0:T(4,128)S(1)} %collective-permute-done.16.z1, f32[48,4,256]{2,1,0:T(4,128)S(1)} %collective-permute-done.17.z2, ...), custom_call_target="tpu_custom_call", output_to_operand_aliasing={{}: (5, {})} | custom-call | tf_op jit(solution)/shard_map/gather_48/pallas_call | solution.py:57
  97.7 2.7 %collective-permute-done.15.z3 = f32[36,4,256]{2,1,0:T(4,128)S(1)} collective-permute-done((f32[36,4,256]{2,1,0:T(4,128)S(1)}, f32[36,4,256]{2,1,0:T(4,128)S(1)}, u32[]{:S(2)}, u32[]{:S(2)}) %collective-permute-start.15) | collective-permute-done | bytes 147488 | tf_op jit(solution)/shard_map/ppermute | solution.py:813
  100.4 1.4 %gather_96.1 = f32[132,4,1024]{2,1,0:T(4,128)} custom-call(s32[2]{0:T(128)S(1)} %pad_add_fusion.ids.refs_0_, f32[36,4,256]{2,1,0:T(4,128)S(1)} %get-tuple-element.77.refs_5_.z0, f32[36,4,256]{2,1,0:T(4,128)S(1)} %collective-permute-done.13.z1, f32[36,4,256]{2,1,0:T(4,128)S(1)} %collective-permute-done.14.z2, ...), custom_call_target="tpu_custom_call", output_to_operand_aliasing={{}: (5, {})} | custom-call | tf_op jit(solution)/shard_map/gather_96/pallas_call | solution.py:57
  (39 shorter events, 6.4 us)
Async XLA Ops:
  0.6 11.0 %collective-permute-start.1 = (f32[2,4,1024]{2,1,0:T(4,128)}, f32[2,4,1024]{2,1,0:T(4,128)S(1)}, u32[]{:S(2)}, u32[]{:S(2)}) collective-permute-start(f32[2,4,1024]{2,1,0:T(4,128)} %w0.1), channel_id=1, source_target_pairs={{0,2},{1,3},{2,0},{3,1},{4,6},{5,7},{6,4},{7,5},{8,10},{9,11},{10,... | collective-permute-start | bytes 98312 | tf_op jit(solution)/shard_map/ppermute | solution.py:813
  0.8 10.8 %collective-permute-start = (f32[2,4,1024]{2,1,0:T(4,128)}, f32[2,4,1024]{2,1,0:T(4,128)S(1)}, u32[]{:S(2)}, u32[]{:S(2)}) collective-permute-start(f32[2,4,1024]{2,1,0:T(4,128)} %w0.1), channel_id=1, source_target_pairs={{0,1},{1,0},{2,3},{3,2},{4,5},{5,4},{6,7},{7,6},{8,9},{9,8},{10,11... | collective-permute-start | bytes 98312 | tf_op jit(solution)/shard_map/ppermute | solution.py:813
  1.8 9.9 %collective-permute-start.2 = (f32[2,4,1024]{2,1,0:T(4,128)}, f32[2,4,1024]{2,1,0:T(4,128)S(1)}, u32[]{:S(2)}, u32[]{:S(2)}) collective-permute-start(f32[2,4,1024]{2,1,0:T(4,128)} %w0.1), channel_id=1, source_target_pairs={{0,3},{1,2},{2,1},{3,0},{4,7},{5,6},{6,5},{7,4},{8,11},{9,10},{10,... | collective-permute-start | bytes 98312 | tf_op jit(solution)/shard_map/ppermute | solution.py:813
  3.1 8.6 %copy-start = (f32[2,4,1024]{2,1,0:T(4,128)S(1)}, f32[2,4,1024]{2,1,0:T(4,128)}, u32[]{:S(2)}) copy-start(f32[2,4,1024]{2,1,0:T(4,128)} %w0.1) | copy-start | bytes 98308
  12.3 2.0 %collective-permute-start.3 = (f32[512,128]{1,0:T(8,128)S(1)}, f32[512,128]{1,0:T(8,128)S(1)}, u32[]{:S(2)}, u32[]{:S(2)}) collective-permute-start(f32[512,128]{1,0:T(8,128)S(1)} %get-tuple-element.48), channel_id=1, source_target_pairs={{0,1},{1,0},{2,3},{3,2},{4,5},{5,4},{6,7},{7,6},{8,9},{9,8},{10,11... | collective-permute-start | bytes 786440 | tf_op jit(solution)/shard_map/ppermute | solution.py:838
  12.9 1.5 %collective-permute-start.4 = (f32[512,128]{1,0:T(8,128)S(1)}, f32[512,128]{1,0:T(8,128)S(1)}, u32[]{:S(2)}, u32[]{:S(2)}) collective-permute-start(f32[512,128]{1,0:T(8,128)S(1)} %get-tuple-element.49), channel_id=1, source_target_pairs={{0,0},{1,2},{2,1},{3,3},{4,4},{5,6},{6,5},{7,7},{8,8},{9,10},{10,9... | collective-permute-start | bytes 786440 | tf_op jit(solution)/shard_map/ppermute | solution.py:839
  14.9 12.1 %collective-permute-start.5 = (f32[704,128]{1,0:T(8,128)S(1)}, f32[704,128]{1,0:T(8,128)S(1)}, u32[]{:S(2)}, u32[]{:S(2)}) collective-permute-start(f32[704,128]{1,0:T(8,128)S(1)} %get-tuple-element.56), channel_id=1, source_target_pairs={{0,1},{1,0},{2,3},{3,2},{4,8},{5,9},{6,10},{7,11},{8,4},{9,5},{10,... | collective-permute-start | bytes 1081352 | tf_op jit(solution)/shard_map/ppermute | solution.py:810
  19.9 7.1 %collective-permute-start.6 = (f32[704,128]{1,0:T(8,128)S(1)}, f32[704,128]{1,0:T(8,128)S(1)}, u32[]{:S(2)}, u32[]{:S(2)}) collective-permute-start(f32[704,128]{1,0:T(8,128)S(1)} %get-tuple-element.57), channel_id=1, source_target_pairs={{0,4},{4,0},{8,12},{12,8},{16,20},{20,16},{24,28},{28,24},{32,36},... | collective-permute-start | bytes 1081352 | tf_op jit(solution)/shard_map/ppermute | solution.py:810
  32.0 10.0 %collective-permute-start.7 = (f32[320,128]{1,0:T(8,128)S(1)}, f32[320,128]{1,0:T(8,128)S(1)}, u32[]{:S(2)}, u32[]{:S(2)}) collective-permute-start(f32[320,128]{1,0:T(8,128)S(1)} %get-tuple-element.62), channel_id=1, source_target_pairs={{0,1},{1,0},{2,3},{3,2},{4,8},{5,9},{6,10},{7,11},{8,4},{9,5},{10,... | collective-permute-start | bytes 491528 | tf_op jit(solution)/shard_map/ppermute | solution.py:810
  37.0 5.0 %collective-permute-start.8 = (f32[320,128]{1,0:T(8,128)S(1)}, f32[320,128]{1,0:T(8,128)S(1)}, u32[]{:S(2)}, u32[]{:S(2)}) collective-permute-start(f32[320,128]{1,0:T(8,128)S(1)} %get-tuple-element.63), channel_id=1, source_target_pairs={{0,4},{4,0},{8,12},{12,8},{16,20},{20,16},{24,28},{28,24},{32,36},... | collective-permute-start | bytes 491528 | tf_op jit(solution)/shard_map/ppermute | solution.py:810
  44.5 11.9 %collective-permute-start.9 = (f32[85,8,128]{2,1,0:T(8,128)S(1)}, f32[85,8,128]{2,1,0:T(8,128)S(1)}, u32[]{:S(2)}, u32[]{:S(2)}) collective-permute-start(f32[85,8,128]{2,1,0:T(8,128)S(1)} %get-tuple-element.66), channel_id=1, source_target_pairs={{0,1},{1,0},{2,3},{3,2},{4,8},{5,9},{6,10},{7,11},{8,4},{9,5},{10,... | collective-permute-start | bytes 1044488 | tf_op jit(solution)/shard_map/ppermute | solution.py:810
  49.5 7.0 %collective-permute-start.10 = (f32[85,8,128]{2,1,0:T(8,128)S(1)}, f32[85,8,128]{2,1,0:T(8,128)S(1)}, u32[]{:S(2)}, u32[]{:S(2)}) collective-permute-start(f32[85,8,128]{2,1,0:T(8,128)S(1)} %get-tuple-element.67), channel_id=1, source_target_pairs={{0,4},{4,0},{8,12},{12,8},{16,20},{20,16},{24,28},{28,24},{32,36},... | collective-permute-start | bytes 1044488 | tf_op jit(solution)/shard_map/ppermute | solution.py:810
  52.7 23.8 %collective-permute-start.11 = (f32[90,8,128]{2,1,0:T(8,128)S(1)}, f32[90,8,128]{2,1,0:T(8,128)S(1)}, u32[]{:S(2)}, u32[]{:S(2)}) collective-permute-start(f32[90,8,128]{2,1,0:T(8,128)S(1)} %get-tuple-element.72), channel_id=1, source_target_pairs={{0,1},{1,0},{2,3},{3,2},{4,8},{5,9},{6,10},{7,11},{8,4},{9,5},{10,... | collective-permute-start | bytes 1105928 | tf_op jit(solution)/shard_map/ppermute | solution.py:810
  55.1 21.5 %collective-permute-start.12 = (f32[90,8,128]{2,1,0:T(8,128)S(1)}, f32[90,8,128]{2,1,0:T(8,128)S(1)}, u32[]{:S(2)}, u32[]{:S(2)}) collective-permute-start(f32[90,8,128]{2,1,0:T(8,128)S(1)} %get-tuple-element.73), channel_id=1, source_target_pairs={{0,4},{4,0},{8,12},{12,8},{16,20},{20,16},{24,28},{28,24},{32,36},... | collective-permute-start | bytes 1105928 | tf_op jit(solution)/shard_map/ppermute | solution.py:810
  61.7 20.4 %collective-permute-start.19 = (f32[48,4,256]{2,1,0:T(4,128)S(1)}, f32[48,4,256]{2,1,0:T(4,128)S(1)}, u32[]{:S(2)}, u32[]{:S(2)}) collective-permute-start(f32[48,4,256]{2,1,0:T(4,128)S(1)} %get-tuple-element.85), channel_id=1, source_target_pairs={{0,1},{1,0},{2,3},{3,2},{4,5},{5,4},{6,7},{7,6},{8,9},{9,8},{10,11... | collective-permute-start | bytes 589832 | tf_op jit(solution)/shard_map/ppermute | solution.py:813
  74.8 13.4 %collective-permute-start.20 = (f32[48,4,256]{2,1,0:T(4,128)S(1)}, f32[48,4,256]{2,1,0:T(4,128)S(1)}, u32[]{:S(2)}, u32[]{:S(2)}) collective-permute-start(f32[48,4,256]{2,1,0:T(4,128)S(1)} %get-tuple-element.86), channel_id=1, source_target_pairs={{0,2},{1,3},{2,0},{3,1},{4,6},{5,7},{6,4},{7,5},{8,10},{9,11},{10,... | collective-permute-start | bytes 589832 | tf_op jit(solution)/shard_map/ppermute | solution.py:813
  74.8 13.5 %collective-permute-start.21 = (f32[48,4,256]{2,1,0:T(4,128)S(1)}, f32[48,4,256]{2,1,0:T(4,128)S(1)}, u32[]{:S(2)}, u32[]{:S(2)}) collective-permute-start(f32[48,4,256]{2,1,0:T(4,128)S(1)} %get-tuple-element.87), channel_id=1, source_target_pairs={{0,3},{1,2},{2,1},{3,0},{4,7},{5,6},{6,5},{7,4},{8,11},{9,10},{10,... | collective-permute-start | bytes 589832 | tf_op jit(solution)/shard_map/ppermute | solution.py:813
  81.8 6.6 %collective-permute-start.16 = (f32[48,4,256]{2,1,0:T(4,128)S(1)}, f32[48,4,256]{2,1,0:T(4,128)S(1)}, u32[]{:S(2)}, u32[]{:S(2)}) collective-permute-start(f32[48,4,256]{2,1,0:T(4,128)S(1)} %get-tuple-element.82), channel_id=1, source_target_pairs={{0,1},{1,0},{2,3},{3,2},{4,5},{5,4},{6,7},{7,6},{8,9},{9,8},{10,11... | collective-permute-start | bytes 589832 | tf_op jit(solution)/shard_map/ppermute | solution.py:813
  82.1 14.1 %collective-permute-start.17 = (f32[48,4,256]{2,1,0:T(4,128)S(1)}, f32[48,4,256]{2,1,0:T(4,128)S(1)}, u32[]{:S(2)}, u32[]{:S(2)}) collective-permute-start(f32[48,4,256]{2,1,0:T(4,128)S(1)} %get-tuple-element.83), channel_id=1, source_target_pairs={{0,2},{1,3},{2,0},{3,1},{4,6},{5,7},{6,4},{7,5},{8,10},{9,11},{10,... | collective-permute-start | bytes 589832 | tf_op jit(solution)/shard_map/ppermute | solution.py:813
  82.1 14.1 %collective-permute-start.18 = (f32[48,4,256]{2,1,0:T(4,128)S(1)}, f32[48,4,256]{2,1,0:T(4,128)S(1)}, u32[]{:S(2)}, u32[]{:S(2)}) collective-permute-start(f32[48,4,256]{2,1,0:T(4,128)S(1)} %get-tuple-element.84), channel_id=1, source_target_pairs={{0,3},{1,2},{2,1},{3,0},{4,7},{5,6},{6,5},{7,4},{8,11},{9,10},{10,... | collective-permute-start | bytes 589832 | tf_op jit(solution)/shard_map/ppermute | solution.py:813
  88.2 9.4 %collective-permute-start.13 = (f32[36,4,256]{2,1,0:T(4,128)S(1)}, f32[36,4,256]{2,1,0:T(4,128)S(1)}, u32[]{:S(2)}, u32[]{:S(2)}) collective-permute-start(f32[36,4,256]{2,1,0:T(4,128)S(1)} %get-tuple-element.79), channel_id=1, source_target_pairs={{0,1},{1,0},{2,3},{3,2},{4,5},{5,4},{6,7},{7,6},{8,9},{9,8},{10,11... | collective-permute-start | bytes 442376 | tf_op jit(solution)/shard_map/ppermute | solution.py:813
  88.3 9.3 %collective-permute-start.14 = (f32[36,4,256]{2,1,0:T(4,128)S(1)}, f32[36,4,256]{2,1,0:T(4,128)S(1)}, u32[]{:S(2)}, u32[]{:S(2)}) collective-permute-start(f32[36,4,256]{2,1,0:T(4,128)S(1)} %get-tuple-element.80), channel_id=1, source_target_pairs={{0,2},{1,3},{2,0},{3,1},{4,6},{5,7},{6,4},{7,5},{8,10},{9,11},{10,... | collective-permute-start | bytes 442376 | tf_op jit(solution)/shard_map/ppermute | solution.py:813
  88.4 12.0 %collective-permute-start.15 = (f32[36,4,256]{2,1,0:T(4,128)S(1)}, f32[36,4,256]{2,1,0:T(4,128)S(1)}, u32[]{:S(2)}, u32[]{:S(2)}) collective-permute-start(f32[36,4,256]{2,1,0:T(4,128)S(1)} %get-tuple-element.81), channel_id=1, source_target_pairs={{0,3},{1,2},{2,1},{3,0},{4,7},{5,6},{6,5},{7,4},{8,11},{9,10},{10,... | collective-permute-start | bytes 442376 | tf_op jit(solution)/shard_map/ppermute | solution.py:813
